TPU v7x, 32 devices: a whole 2x2x4 slice. The times are simulated.
32 devices in a mesh: dp: 16 (over z, x, core), tensor: 2 (over y).
Axes of the slice: x: 2, y: 2, z: 4, core: 2. Of those that a mesh axis runs over, the one named last changes fastest.
Arguments:
- tokens: bfloat16 [16384, 1024], P('dp'), may hold values from -6 to 6
- proj_weight: bfloat16 [1024, 3, 1024], P(None, None, 'tensor'), may hold values from -0.1875 to 0.1875
- query_bias: float32 [16, 64], P('tensor'), may hold values from -1.75 to 1.75
- value_bias: float32 [16, 64], P('tensor'), may hold values from -0.0625 to 0.0625
- out_weight: bfloat16 [1024, 1024], P('tensor'), may hold values from -6 to 6
- out_bias: float32 [1024], replicated, may hold values from -1.75 to 1.75
- first_gain: float32 [1024], replicated, may hold values from 0.5 to 1.5
- first_shift: float32 [1024], replicated, may hold values from -1.75 to 1.75
- up_weight: bfloat16 [1024, 4096], P(None, 'tensor'), may hold values from -0.1875 to 0.1875
- up_bias: float32 [64, 64], P('tensor'), may hold values from -3 to 3
- down_weight: bfloat16 [4096, 1024], P('tensor'), may hold values from -0.09375 to 0.09375
- down_bias: float32 [1024], replicated, may hold values from -1.75 to 1.75
- second_gain: float32 [1024], replicated, may hold values from 0.5 to 1.5
- second_shift: float32 [1024], replicated, may hold values from -1.75 to 1.75
- cotangent: bfloat16 [16384, 1024], P('dp'), may hold values from -6 to 6
Outputs:
- layer_out: bfloat16 [16384, 1024], P('dp')
- tokens_grad: float32 [16384, 1024], P('dp')
- proj_grad: float32 [1024, 3, 1024], P('dp', None, 'tensor')
- querybias_grad: float32 [16, 64], P('tensor', 'dp')
- valuebias_grad: float32 [16, 64], P('tensor', 'dp')
- outweight_grad: float32 [1024, 1024], P('tensor', 'dp')
- outbias_grad: float32 [1024], P('dp')
- firstgain_grad: float32 [1024], P('dp')
- firstshift_grad: float32 [1024], P('dp')
- upweight_grad: float32 [1024, 4096], P('dp', 'tensor')
- upbias_grad: float32 [64, 64], P('tensor', 'dp')
- downweight_grad: float32 [4096, 1024], P('tensor', 'dp')
- downbias_grad: float32 [1024], P('dp')
- secondgain_grad: float32 [1024], P('dp')
- secondshift_grad: float32 [1024], P('dp')
All inputs are finite; a program needn't handle non-finite values.
Results may differ from a plain program's by a relative error of at most 0.015.
The roundings to bfloat16 on the way count: a program that leaves them out, or rounds other values in their place, can miss the bound.
Values may be sent and summed in bfloat16 or wider, within the bound.
A program may use at most 192 MiB of HBM per device.

v0:
```python
import math

import jax
import jax.numpy as jnp
from jax import lax
from jax.sharding import PartitionSpec as P

LEVELS = 2


EPS = 1e-12


def partner(value, axis, apart):
    mask = 2**apart
    pairs = [(source, source ^ mask) for source in range(lax.axis_size(axis))]
    return lax.ppermute(value, axis, pairs)


def layer_norm(rows, gain, shift):
    mean = jnp.mean(rows, axis=-1, keepdims=True)
    centered = rows - mean
    spread = jnp.mean(centered * centered, axis=-1, keepdims=True)
    return centered * lax.rsqrt(spread + EPS) * gain + shift


def gelu_tanh(values):
    return jax.nn.gelu(values, approximate=True)


def product(left, right):
    return jnp.dot(left, right, preferred_element_type=jnp.float32)


def inner_rows(left, right):
    return lax.dot_general(
        left, right, (((0,), (0,)), ((), ())), preferred_element_type=jnp.float32
    )


def inner_cols(left, right):
    return lax.dot_general(
        left, right, (((1,), (1,)), ((), ())), preferred_element_type=jnp.float32
    )


def split_heads(rows, heads):
    return rows.reshape(rows.shape[0], heads, -1).transpose(1, 0, 2)


def join_heads(stacked):
    return stacked.transpose(1, 0, 2).reshape(stacked.shape[1], -1)


def gather_group(local, levels, position, sender):
    whole = local
    for level in range(levels):
        other = sender(whole, level)
        upper = position >> level & 1
        whole = jnp.where(
            upper == 1,
            jnp.concatenate([other, whole], axis=1),
            jnp.concatenate([whole, other], axis=1),
        )
    return whole


def scatter_group(whole, levels, position):
    for level in reversed(range(levels)):
        half = whole.shape[1] // 2
        lower = whole[:, :half]
        higher = whole[:, half:]
        upper = position >> level & 1
        keep = jnp.where(upper == 1, higher, lower)
        send = jnp.where(upper == 1, lower, higher)
        whole = keep + partner(send.astype(jnp.bfloat16), "dp", level).astype(send.dtype)
    return whole


def body(
    tokens,
    proj_weight,
    query_bias,
    value_bias,
    out_weight,
    out_bias,
    first_gain,
    first_shift,
    up_weight,
    up_bias,
    down_weight,
    down_bias,
    second_gain,
    second_shift,
    cotangent,
):
    width = tokens.shape[1]
    heads, head_size = query_bias.shape
    local_width = heads * head_size
    scale = 1.0 / math.sqrt(head_size)
    position = lax.axis_index("dp")
    flat_proj = proj_weight.reshape(width, 3 * local_width)
    mixed = product(tokens, flat_proj)
    queries = (mixed[:, :local_width] + query_bias.reshape(local_width)).astype(jnp.bfloat16)
    keys_local = mixed[:, local_width : 2 * local_width].astype(jnp.bfloat16)
    values_local = (mixed[:, 2 * local_width :] + value_bias.reshape(local_width)).astype(
        jnp.bfloat16
    )
    pair_local = jnp.stack([keys_local, values_local])
    pair_whole = gather_group(
        pair_local, LEVELS, position, lambda block, level: partner(block, "dp", level)
    )
    query_heads = split_heads(queries, heads)

    def head_forward(parts):
        query_head, key_head, value_head = parts
        scores = inner_cols(query_head, key_head) * scale
        peak = jnp.max(scores, axis=1, keepdims=True)
        weights = jnp.exp(scores - peak)
        totals = jnp.sum(weights, axis=1, keepdims=True)
        probs = (weights / totals).astype(jnp.bfloat16)
        return (product(probs, value_head), (peak + jnp.log(totals))[:, 0])

    context_heads, log_totals = lax.map(
        head_forward,
        (query_heads, split_heads(pair_whole[0], heads), split_heads(pair_whole[1], heads)),
    )
    context = join_heads(context_heads).astype(jnp.bfloat16)
    attention = lax.psum(product(context, out_weight), "tensor") + out_bias
    first, first_back = jax.vjp(
        layer_norm, tokens.astype(jnp.float32) + attention, first_gain, first_shift
    )
    first_low = first.astype(jnp.bfloat16)
    hidden = product(first_low, up_weight) + up_bias.reshape(-1)
    active, gelu_back = jax.vjp(gelu_tanh, hidden)
    active_low = active.astype(jnp.bfloat16)
    feed = lax.psum(product(active_low, down_weight), "tensor") + down_bias
    second, second_back = jax.vjp(layer_norm, first + feed, second_gain, second_shift)
    layer_output = second.astype(jnp.bfloat16)
    upstream = cotangent.astype(jnp.float32)
    second_grad, secondgain_grad, secondshift_grad = second_back(upstream)
    feed_grad = second_grad.astype(jnp.bfloat16)
    downbias_grad = jnp.sum(feed_grad.astype(jnp.float32), axis=0)
    downweight_grad = inner_rows(active_low, feed_grad)
    (hidden_grad,) = gelu_back(inner_cols(feed_grad, down_weight))
    hidden_low = hidden_grad.astype(jnp.bfloat16)
    upbias_grad = jnp.sum(hidden_low.astype(jnp.float32), axis=0).reshape(up_bias.shape)
    upweight_grad = inner_rows(first_low, hidden_low)
    first_grad = second_grad + lax.psum(inner_cols(hidden_low, up_weight), "tensor")
    units_parts = (
        upweight_grad,
        upbias_grad,
        downweight_grad,
        downbias_grad,
        secondgain_grad,
        secondshift_grad,
    )
    attention_back, firstgain_grad, firstshift_grad = first_back(first_grad)
    attention_grad = attention_back.astype(jnp.bfloat16)
    outbias_grad = jnp.sum(attention_grad.astype(jnp.float32), axis=0)
    outweight_grad = inner_rows(context, attention_grad)
    context_grad = inner_cols(attention_grad, out_weight).astype(jnp.bfloat16)

    def head_backward(parts):
        query_head, key_head, value_head, grad_head, log_total = parts
        scores = inner_cols(query_head, key_head) * scale
        probs = jnp.exp(scores - log_total[:, None])
        probs_low = probs.astype(jnp.bfloat16)
        probs_grad = inner_cols(grad_head, value_head)
        centre = jnp.sum(probs * probs_grad, axis=1, keepdims=True)
        score_grad = (probs * (probs_grad - centre)).astype(jnp.bfloat16)
        query_part = product(score_grad, key_head) * scale
        key_part = inner_rows(score_grad, query_head) * scale
        value_part = inner_rows(probs_low, grad_head)
        return (query_part, key_part, value_part)

    query_parts, key_parts, value_parts = lax.map(
        head_backward,
        (
            query_heads,
            split_heads(pair_whole[0], heads),
            split_heads(pair_whole[1], heads),
            split_heads(context_grad, heads),
            log_totals,
        ),
    )
    query_grad = join_heads(query_parts).astype(jnp.bfloat16)
    pair_grad = jnp.stack([join_heads(key_parts), join_heads(value_parts)])
    pair_mine = scatter_group(pair_grad, LEVELS, position)
    key_grad = pair_mine[0].astype(jnp.bfloat16)
    value_grad = pair_mine[1].astype(jnp.bfloat16)
    joined_grads = jnp.concatenate([query_grad, key_grad, value_grad], axis=1)
    proj_grad = inner_rows(tokens, joined_grads).reshape(width, 3, local_width)
    querybias_grad = jnp.sum(query_grad.astype(jnp.float32), axis=0).reshape(heads, head_size)
    valuebias_grad = jnp.sum(value_grad.astype(jnp.float32), axis=0).reshape(heads, head_size)
    tokens_grad = attention_back + lax.psum(
        inner_cols(joined_grads, flat_proj).astype(jnp.bfloat16), "tensor"
    ).astype(jnp.float32)
    summed = (
        lax.psum_scatter(proj_grad, "dp", scatter_dimension=0, tiled=True),
        lax.psum_scatter(querybias_grad, "dp", scatter_dimension=1, tiled=True),
        lax.psum_scatter(valuebias_grad, "dp", scatter_dimension=1, tiled=True),
        lax.psum_scatter(outweight_grad, "dp", scatter_dimension=1, tiled=True),
        lax.psum_scatter(outbias_grad, "dp", scatter_dimension=0, tiled=True),
        lax.psum_scatter(firstgain_grad, "dp", scatter_dimension=0, tiled=True),
        lax.psum_scatter(firstshift_grad, "dp", scatter_dimension=0, tiled=True),
        lax.psum_scatter(units_parts[0], "dp", scatter_dimension=0, tiled=True),
        lax.psum_scatter(units_parts[1], "dp", scatter_dimension=1, tiled=True),
        lax.psum_scatter(units_parts[2], "dp", scatter_dimension=1, tiled=True),
        lax.psum_scatter(units_parts[3], "dp", scatter_dimension=0, tiled=True),
        lax.psum_scatter(units_parts[4], "dp", scatter_dimension=0, tiled=True),
        lax.psum_scatter(units_parts[5], "dp", scatter_dimension=0, tiled=True),
    )
    return (
        layer_output,
        tokens_grad,
        summed[0],
        summed[1],
        summed[2],
        summed[3],
        summed[4],
        summed[5],
        summed[6],
        summed[7],
        summed[8],
        summed[9],
        summed[10],
        summed[11],
        summed[12],
    )


def solution(mesh):
    return jax.shard_map(
        body,
        mesh=mesh,
        in_specs=(
            P("dp", None),
            P(None, None, "tensor"),
            P("tensor", None),
            P("tensor", None),
            P("tensor", None),
            P(),
            P(),
            P(),
            P(None, "tensor"),
            P("tensor", None),
            P("tensor", None),
            P(),
            P(),
            P(),
            P("dp", None),
        ),
        out_specs=(
            P("dp", None),
            P("dp", None),
            P("dp", None, "tensor"),
            P("tensor", "dp"),
            P("tensor", "dp"),
            P("tensor", "dp"),
            P("dp"),
            P("dp"),
            P("dp"),
            P("dp", "tensor"),
            P("tensor", "dp"),
            P("tensor", "dp"),
            P("dp"),
            P("dp"),
            P("dp"),
        ),
        check_vma=False,
    )
```

profile of v0, /device:TPU:0, one launch (start us, length us, event | category | flops | bytes accessed | tf_op | source)
XLA Modules:
  0.0 1628.3 jit_solution(6987201227236261804)
XLA Ops:
  35.7 87.9 %collective-permute-done.1 = bf16[2,2048,512]{2,1,0:T(8,128)(2,1)} collective-permute-done((bf16[2,2048,512]{2,1,0:T(8,128)(2,1)}, bf16[2,2048,512]{2,1,0:T(8,128)(2,1)}, u32[]{:S(2)}, u32[]{:S(2)}) %collective-permute-start.1) | collective-permute-done | bytes 4194336 | tf_op jit(solution)/shard_map/ppermute | solution.py:17
  164.1 210.8 %while.26 = (s32[]{:T(128)}, bf16[8,1024,64]{1,2,0:T(8,128)(2,1)S(1)}, f32[8,1024]{1,0:T(8,128)S(1)}, bf16[8,1024,64]{2,1,0:T(8,128)(2,1)}, bf16[8,4096,64]{2,1,...) while((s32[]{:T(128)}, bf16[8,1024,64]{1,2,0:T(8,128)(2,1)S(1)}, ...), condition=%wide.region_3.4_spmd, body=%wide.region_0.3_spmd.sunk | while | flops 1111489536 | bytes 52996184 | solution.py:124
  164.3 9.4 multiply_reduce_fusion.8
  190.6 9.4 multiply_reduce_fusion.8
  216.9 9.4 multiply_reduce_fusion.8
  243.3 9.4 multiply_reduce_fusion.8
  269.6 9.4 multiply_reduce_fusion.8
  295.9 9.4 multiply_reduce_fusion.8
  322.2 9.4 multiply_reduce_fusion.8
  348.6 9.4 multiply_reduce_fusion.8
  378.4 109.4 %all-reduce.15.cloned.1.call-done = f32[1024,1024]{1,0:T(8,128)} async-done(((f32[1024,1024]{1,0:T(8,128)}), f32[1024,1024]{1,0:T(8,128)}) %all-reduce.15.cloned.1.call-update) | async-done | bytes 4194320 | tf_op jit(solution)/shard_map/psum | solution.py:129
  495.1 9.4 multiply_convert_fusion.1
  512.6 108.0 %all-reduce.17.cloned.1.call-done = f32[1024,1024]{1,0:T(8,128)} async-done(((f32[1024,1024]{1,0:T(8,128)}), f32[1024,1024]{1,0:T(8,128)}) %all-reduce.17.cloned.1.call-update) | async-done | bytes 4194320 | tf_op jit(solution)/shard_map/psum | solution.py:137
  636.0 10.8 convert_reduce_fusion
  654.9 108.0 %all-reduce.19.cloned.1.call-done = f32[1024,1024]{1,0:T(8,128)} async-done(((f32[1024,1024]{1,0:T(8,128)}), f32[1024,1024]{1,0:T(8,128)}) %all-reduce.19.cloned.1.call-update) | async-done | bytes 4194320 | tf_op jit(solution)/shard_map/psum | solution.py:149
  775.8 293.6 %while.27 = (s32[]{:T(128)}, bf16[8,1024,64]{1,2,0:T(8,128)(2,1)S(1)}, f32[8,4096,64]{1,2,0:T(8,128)}, f32[8,4096,64]{1,2,0:T(8,128)}, bf16[8,1024,64]{2,1,0:T(8...) while((s32[]{:T(128)}, ...), condition=%wide.region_17.18_spmd, body=%wide.region_15.17_spmd.sunk | while | flops 2735012864 | bytes 165971072 | solution.py:177
  779.5 9.3 multiply_reduce_fusion.9
  788.7 8.7 multiply_convert_fusion.3
  816.1 9.3 multiply_reduce_fusion.9
  852.9 9.3 multiply_reduce_fusion.9
  889.5 9.3 multiply_reduce_fusion.9
  926.2 9.3 multiply_reduce_fusion.9
  962.9 9.3 multiply_reduce_fusion.9
  999.6 9.3 multiply_reduce_fusion.9
  1036.2 9.3 multiply_reduce_fusion.9
  1078.5 90.8 %collective-permute-done.2 = bf16[2,2048,512]{1,2,0:T(8,128)(2,1)} collective-permute-done((bf16[2,2048,512]{1,2,0:T(8,128)(2,1)S(1)}, bf16[2,2048,512]{1,2,0:T(8,128)(2,1)}, u32[]{:S(2)}, u32[]{:S(2)}) %collective-permute-start.2) | collective-permute-done | bytes 4194336 | tf_op jit(solution)/shard_map/ppermute | solution.py:17
  1192.3 11.3 fusion.86
  1204.4 11.5 fusion.71
  1235.5 63.0 %all-reduce.9 = (f32[8,64]{0,1:T(8,128)S(1)}, f32[8,64]{1,0:T(8,128)S(1)}, f32[1024]{0:T(1024)S(1)}, f32[1024]{0:T(1024)S(1)}, f32[1024]{0:T(1024)S(1)}, /*index...) all-reduce(f32[8,64]{0,1:T(8,128)S(1)} %copy.61, ...), channel_id=3, replica_groups=mesh['dp'=16,'tensor'=2] {'dp'}, use_global_device_ids=true, to_apply=%region_21.22.clone | all-reduce | flops 9216 | bytes 73728
  1317.4 106.9 %reduce-scatter.13.cloned.1.call-done = f32[2048,64]{0,1:T(8,128)} async-done(((f32[2048,1024]{0,1:T(8,128)}), f32[2048,64]{0,1:T(8,128)}) %reduce-scatter.13.cloned.1.call-update) | async-done | bytes 524304 | tf_op jit(solution)/shard_map/reduce_scatter | solution.py:209
  1424.3 107.8 %reduce-scatter.11.cloned.1.call-done = f32[64,2048]{1,0:T(8,128)} async-done(((f32[1024,2048]{1,0:T(8,128)}), f32[64,2048]{1,0:T(8,128)}) %reduce-scatter.11.cloned.1.call-update) | async-done | bytes 524304 | tf_op jit(solution)/shard_map/reduce_scatter | solution.py:207
  1532.1 89.2 %reduce-scatter.7.cloned.1.call-done = f32[64,3,512]{2,0,1:T(8,128)} async-done(((f32[1024,3,512]{2,0,1:T(8,128)}), f32[64,3,512]{2,0,1:T(8,128)}) %reduce-scatter.7.cloned.1.call-update) | async-done | bytes 393232 | tf_op jit(solution)/shard_map/reduce_scatter | solution.py:200
  (301 shorter events, 539.3 us)
Async XLA Ops:
  7.2 367.7 %copy-start = (bf16[512,1024]{1,0:T(8,128)(2,1)S(1)}, bf16[512,1024]{1,0:T(8,128)(2,1)}, u32[]{:S(2)}) copy-start(bf16[512,1024]{1,0:T(8,128)(2,1)} %param.23) | copy-start | bytes 3145732
  7.2 4.9 copy-start.42
  7.2 5.0 copy-start.43
  7.2 5.0 copy-start.17
  7.2 480.6 %all-reduce.15.cloned.1.call-start = ((), (), s32[]{:S(2)}) async-start(), calls=%async_computation.4 | async-start | bytes 8388608 | tf_op jit(solution)/shard_map/psum | solution.py:129
  20.8 4.6 collective-permute-start
  29.6 94.0 %collective-permute-start.1 = (bf16[2,2048,512]{2,1,0:T(8,128)(2,1)}, bf16[2,2048,512]{2,1,0:T(8,128)(2,1)}, u32[]{:S(2)}, u32[]{:S(2)}) collective-permute-start(bf16[2,2048,512]{2,1,0:T(8,128)(2,1)} %maximum_select_fusion.1), channel_id=1, source_target_pairs={{0,4},{2,6},{4,0},{6,2},{8,12},{10,14},{12,8},{14,10},{16,20},{18,... | collective-permute-start | bytes 12582920 | tf_op jit(solution)/shard_map/ppermute | solution.py:17
  374.9 112.9 %copy-start.37 = (f32[1024]{0:T(1024)S(1)}, f32[1024]{0:T(1024)}, u32[]{:S(2)}) copy-start(f32[1024]{0:T(1024)} %param.24) | copy-start | bytes 12292
  378.3 242.3 %all-reduce.17.cloned.1.call-start = ((), (), s32[]{:S(2)}) async-start(), calls=%async_computation.5 | async-start | bytes 8388608 | tf_op jit(solution)/shard_map/psum | solution.py:137
  491.3 13.2 copy-start.3
  491.4 278.0 %copy-start.20 = (f32[1024]{0:T(1024)}, f32[1024]{0:T(1024)S(1)}, u32[]{:S(2)}) copy-start(f32[1024]{0:T(1024)S(1)} %broadcast_multiply_fusion.1) | copy-start | bytes 12292
  495.1 274.4 %copy-start.22 = (f32[1024]{0:T(1024)}, f32[1024]{0:T(1024)S(1)}, u32[]{:S(2)}) copy-start(f32[1024]{0:T(1024)S(1)} %fusion.67) | copy-start | bytes 12292
  495.1 11.4 copy-start.44
  512.5 108.1 %copy-start.38 = (f32[1024]{0:T(1024)S(1)}, f32[1024]{0:T(1024)}, u32[]{:S(2)}) copy-start(f32[1024]{0:T(1024)} %param.30) | copy-start | bytes 12292
  512.5 250.4 %all-reduce.19.cloned.1.call-start = ((), (), s32[]{:S(2)}) async-start(), calls=%async_computation.6 | async-start | bytes 8388608 | tf_op jit(solution)/shard_map/psum | solution.py:149
  626.5 8.9 slice-start.2
  629.1 6.3 slice-start.3
  635.4 11.4 copy-start.15
  636.0 12.7 copy-start.47
  654.8 649.3 %all-reduce.21.cloned.1.call-start = ((), (), s32[]{:S(2)}) async-start(), calls=%async_computation.7 | async-start | bytes 4194304 | tf_op jit(solution)/shard_map/psum | solution.py:196
  762.9 6.6 copy-start.4
  1070.3 99.0 %slice-start = ((s8[8388608]{0:T(1024)(128)(4,1)}), s8[4194304]{0:T(1024)(128)(4,1)S(1)}, s32[]{:S(2)}) async-start(s8[8388608]{0:T(1024)(128)(4,1)} %bitcast.154), calls=%async_computation.12 | async-start | bytes 8388608
  1070.3 99.0 %slice-start.1 = ((s8[8388608]{0:T(1024)(128)(4,1)}), s8[4194304]{0:T(1024)(128)(4,1)S(1)}, s32[]{:S(2)}) async-start(s8[8388608]{0:T(1024)(128)(4,1)} %bitcast.154), calls=%async_computation.13 | async-start | bytes 8388608
  1070.3 99.0 %copy-start.7 = (f32[8,4096,64]{1,2,0:T(8,128)S(1)}, f32[8,4096,64]{1,2,0:T(8,128)}, u32[]{:S(2)}) copy-start(f32[8,4096,64]{1,2,0:T(8,128)} %get-tuple-element.101) | copy-start | bytes 25165828
  1077.0 92.3 %collective-permute-start.2 = (bf16[2,2048,512]{1,2,0:T(8,128)(2,1)S(1)}, bf16[2,2048,512]{1,2,0:T(8,128)(2,1)}, u32[]{:S(2)}, u32[]{:S(2)}) collective-permute-start(bf16[2,2048,512]{1,2,0:T(8,128)(2,1)S(1)} %select_convert_fusion), channel_id=1, source_target_pairs={{0,4},{2,6},{4,0},{6,2},{8,12},{10,14},{12,8},{14,10},{16,20},{18,... | collective-permute-start | bytes 12582920 | tf_op jit(solution)/shard_map/ppermute | solution.py:17
  1174.8 4.2 collective-permute-start.3
  1188.0 129.4 %reduce-scatter.9.cloned.1.call-start = ((), (), s32[]{:S(2)}) async-start(), calls=%async_computation.9 | async-start | bytes 2228224 | tf_op jit(solution)/shard_map/reduce_scatter | solution.py:203
  1192.3 232.0 %reduce-scatter.13.cloned.1.call-start = ((), (), s32[]{:S(2)}) async-start(), calls=%async_computation.11 | async-start | bytes 8912896 | tf_op jit(solution)/shard_map/reduce_scatter | solution.py:209
  1203.7 328.4 %reduce-scatter.11.cloned.1.call-start = ((), (), s32[]{:S(2)}) async-start(), calls=%async_computation.10 | async-start | bytes 8912896 | tf_op jit(solution)/shard_map/reduce_scatter | solution.py:207
  1216.0 405.3 %reduce-scatter.7.cloned.1.call-start = ((), (), s32[]{:S(2)}) async-start(), calls=%async_computation.8 | async-start | bytes 6684672 | tf_op jit(solution)/shard_map/reduce_scatter | solution.py:200
  1232.3 71.7 %copy-start.27 = (f32[1024]{0:T(1024)S(1)}, f32[1024]{0:T(1024)}, u32[]{:S(2)}) copy-start(f32[1024]{0:T(1024)} %copy-done.26) | copy-start | bytes 12292
  1303.5 317.8 %copy-start.1 = (bf16[512,1024]{1,0:T(8,128)(2,1)S(1)}, bf16[512,1024]{1,0:T(8,128)(2,1)}, u32[]{:S(2)}) copy-start(bf16[512,1024]{1,0:T(8,128)(2,1)} %param.23) | copy-start | bytes 3145732
  (42 other events, 104.5 us)
Sparse Core Ops, SparseCore 0:
  378.4 109.4 all-reduce.14
  512.6 107.9 all-reduce.16
  654.9 107.8 all-reduce.18
  1188.1 62.9 all-reduce.20
  1255.3 62.0 reduce-scatter.8
  1321.9 102.3 reduce-scatter.12
  1429.0 103.0 reduce-scatter.10
  1536.6 84.6 reduce-scatter.6
where the time goes:
time: 1640 us; the launch traced here: 1630 us
  waiting for transfers between devices  824 us (50%)
  matrix products  446 us (27%)
  other arithmetic  198 us (12%)
  local copies, waits for them, and re-layouts  74.9 us (5%)
  blocking collectives  63 us (4%)
    dot_general x28, matrix products, inner_cols(): lax.dot_general(left, right, (((1,), (1,)), ((), ())), preferred_element_...  201 us
    ppermute x4, waiting for transfers between devices, partner(): return lax.ppermute(value, axis, pairs)  187 us
    dot_general x20, matrix products, product(): return jnp.dot(left, right, preferred_element_type=jnp.float32)  140 us
    psum x1, waiting for transfers between devices, body(): attention = lax.psum(product(context, out_weight), 'tensor') + out_bias  109 us
    psum x1, waiting for transfers between devices, body(): feed = lax.psum(product(active_low, down_weight), 'tensor') + down_bias  108 us
    psum x1, waiting for transfers between devices, body(): lax.psum(inner_cols(hidden_low, up_weight), 'tensor')  108 us
    reduce_scatter x1, waiting for transfers between devices, body(): lax.psum_scatter(units_parts[0], 'dp', scatter_dimension=0, tiled=True)  108 us
    reduce_scatter x1, waiting for transfers between devices, body(): lax.psum_scatter(units_parts[2], 'dp', scatter_dimension=1, tiled=True)  107 us
  transfers between devices with their start and end apart: 12, of which 11 were waited for; matrix products, arithmetic and copies ran while one was open for 4% of the time, Pallas kernels for 0%

commit v1 on v0

v1 whole, which is shorter than its diff:
```python
import functools
import math

import jax
import jax.numpy as jnp
from jax import lax
from jax.experimental import pallas as pl
from jax.experimental.pallas import tpu as pltpu
from jax.sharding import PartitionSpec as P

EPS = 1e-12
F32 = jnp.float32
BF16 = jnp.bfloat16
LANES = 128
HALF = 64
SOURCES = 4
CHUNKS = 2
NN = (((1,), (0,)), ((), ()))
NT = (((1,), (1,)), ((), ()))
TN = (((0,), (0,)), ((), ()))


def dot(left, right, dims):
    return lax.dot_general(left, right, dims, preferred_element_type=F32)


def flip(value, axis, bit):
    pairs = [(source, source ^ (1 << bit)) for source in range(lax.axis_size(axis))]
    return lax.ppermute(value, axis, pairs)


def pair_sum(partial):
    low = partial.astype(BF16)
    return low.astype(F32) + flip(low, "tensor", 0).astype(F32)


def scatter_rows(rows, wire):
    size = lax.axis_size("dp")
    mine = lax.axis_index("dp")
    part = rows.shape[0] // size
    whole = rows
    bit = 0
    while size > 1:
        size //= 2
        split = whole.reshape(size, 2, part, -1)
        own = mine >> bit & 1
        keep = lax.dynamic_index_in_dim(split, own, 1, keepdims=False)
        send = lax.dynamic_index_in_dim(split, 1 - own, 1, keepdims=False)
        whole = keep.astype(F32) + flip(send.astype(wire), "dp", bit).astype(F32)
        bit += 1
    return whole.reshape(part, -1)


def layer_norm(rows, gain, shift):
    mean = jnp.mean(rows, axis=-1, keepdims=True)
    centered = rows - mean
    spread = jnp.mean(centered * centered, axis=-1, keepdims=True)
    return centered * lax.rsqrt(spread + EPS) * gain + shift


def gelu_tanh(values):
    return jax.nn.gelu(values, approximate=True)


def head_lanes(shape, head):
    lane = lax.broadcasted_iota(jnp.int32, shape, 1)
    return (lane < HALF) if head == 0 else (lane >= HALF)


def forward_kernel(scale, tile, *refs):
    q_ref = refs[0]
    k_refs = refs[1 : 1 + SOURCES]
    v_refs = refs[1 + SOURCES : 1 + 2 * SOURCES]
    o_ref, lse_ref, s_ref, vt_ref = refs[1 + 2 * SOURCES :]
    span = k_refs[0].shape[0]

    @pl.when(pl.program_id(0) == 0)
    def _():
        for source in range(SOURCES):
            vt_ref[:LANES, source * span : (source + 1) * span] = jnp.transpose(
                v_refs[source][...]
            )
        vt_ref[LANES:, :] = jnp.ones((vt_ref.shape[0] - LANES, vt_ref.shape[1]), BF16)

    q = q_ref[...] * scale
    outs = []
    for head in range(2):
        own = head_lanes(q.shape, head)
        qt = jnp.transpose(jnp.where(own, q, jnp.zeros_like(q)))
        peak = None
        for source in range(SOURCES):
            for start in range(0, span, tile):
                scores = dot(k_refs[source][start : start + tile, :], qt, NN)
                base = source * span + start
                s_ref[head, base : base + tile, :] = scores
                top = jnp.max(scores, axis=0, keepdims=True)
                peak = top if peak is None else jnp.maximum(peak, top)
        total = None
        for start in range(0, SOURCES * span, tile):
            weights = jnp.exp(s_ref[head, start : start + tile, :] - peak).astype(BF16)
            part = dot(vt_ref[:, start : start + tile], weights, NN)
            total = part if total is None else total + part
        mass = total[LANES : LANES + 1, :]
        outs.append(total[head * HALF : (head + 1) * HALF, :] / mass)
        lse_ref[head, :] = (peak + jnp.log(mass))[0]
    o_ref[...] = jnp.transpose(jnp.concatenate(outs, 0))


def attend(queries, group, blocks, scale):
    rows = queries.shape[0]
    span = blocks[0].shape[0]
    tq = rows // 2
    keys = SOURCES * span
    return pl.pallas_call(
        functools.partial(forward_kernel, scale, span // 2),
        grid=(rows // tq,),
        in_specs=[pl.BlockSpec((tq, LANES), lambda i: (i, group))]
        + [pl.BlockSpec((span, LANES), lambda i: (0, 0))] * SOURCES
        + [pl.BlockSpec((span, LANES), lambda i: (0, 1))] * SOURCES,
        out_specs=[
            pl.BlockSpec((tq, LANES), lambda i: (i, 0)),
            pl.BlockSpec((2, tq), lambda i: (0, i)),
        ],
        out_shape=[
            jax.ShapeDtypeStruct((rows, LANES), F32),
            jax.ShapeDtypeStruct((2, rows), F32),
        ],
        scratch_shapes=[
            pltpu.VMEM((2, keys, tq), F32),
            pltpu.VMEM((LANES + 16, keys), BF16),
        ],
        compiler_params=pltpu.CompilerParams(vmem_limit_bytes=40 << 20),
        cost_estimate=pl.CostEstimate(
            flops=16 * rows * keys * LANES,
            bytes_accessed=4 * (keys + rows) * LANES + 4 * rows * LANES,
            transcendentals=2 * rows * keys,
        ),
        name="attend",
    )(queries, *blocks, *blocks)


def thirds(value):
    high = value.astype(BF16).astype(F32)
    rest = value - high
    middle = rest.astype(BF16).astype(F32)
    return high, middle, rest - middle


def backward_kernel(scale, tile, *refs):
    q_ref, g_ref, o_ref, lse_ref = refs[:4]
    k_refs = refs[4 : 4 + SOURCES]
    v_refs = refs[4 + SOURCES : 4 + 2 * SOURCES]
    dq_ref = refs[4 + 2 * SOURCES]
    d_refs = refs[5 + 2 * SOURCES : 5 + 3 * SOURCES]
    qt_ref, gt_ref, dqt_ref, k_ref, v_ref, d_ref = refs[5 + 3 * SOURCES :]
    step = pl.program_id(0)
    rows = q_ref.shape[0]
    span = k_ref.shape[0]

    @pl.when(step == 0)
    def _():
        q = q_ref[...] * scale
        g = g_ref[...]
        products = jnp.transpose(g.astype(F32) * o_ref[...])
        row = lax.broadcasted_iota(jnp.int32, (LANES, rows), 0)
        for head in range(2):
            own = head_lanes(q.shape, head)
            qt_ref[head, :LANES, :] = jnp.transpose(jnp.where(own, q, jnp.zeros_like(q)))
            gt_ref[head, :LANES, :] = jnp.transpose(jnp.where(own, g, jnp.zeros_like(g)))
            centre = jnp.sum(
                products[head * HALF : (head + 1) * HALF], axis=0, keepdims=True
            )
            for ref, value in (
                (qt_ref, -lse_ref[head : head + 1, :]),
                (gt_ref, -centre),
            ):
                high, middle, low = thirds(value)
                ref[head, LANES:, :] = jnp.where(
                    row == 0,
                    high,
                    jnp.where(row == 1, middle, jnp.where(row == 2, low, 0.0)),
                ).astype(BF16)
        dqt_ref[...] = jnp.zeros_like(dqt_ref)

    for source in range(SOURCES):

        @pl.when(step == source)
        def _():
            k_ref[...] = k_refs[source][...]
            v_ref[...] = v_refs[source][...]

    for start in range(0, span, tile):
        k = k_ref[start : start + tile, :]
        v = v_ref[start : start + tile, :]
        one = jnp.ones_like(k)
        k_wide = jnp.concatenate([k, one], 1)
        v_wide = jnp.concatenate([v, one], 1)
        kt = jnp.transpose(k)
        parts = []
        for head in range(2):
            probs = jnp.exp(dot(k_wide, qt_ref[head], NN))
            centred = dot(v_wide, gt_ref[head], NN)
            score_grad = (probs * centred).astype(BF16)
            parts.append(
                (
                    dot(score_grad, q_ref[...], NN),
                    dot(probs.astype(BF16), g_ref[...], NN),
                )
            )
            dqt_ref[head * HALF : (head + 1) * HALF, :] += dot(
                kt[head * HALF : (head + 1) * HALF, :], score_grad, NN
            )
        first = head_lanes(k.shape, 0)
        d_ref[start : start + tile, :LANES] = (
            jnp.where(first, parts[0][0], parts[1][0]) * scale
        ).astype(BF16)
        d_ref[start : start + tile, LANES:] = jnp.where(
            first, parts[0][1], parts[1][1]
        ).astype(BF16)

    for source in range(SOURCES):

        @pl.when(step == source)
        def _():
            d_refs[source][...] = d_ref[...]

    @pl.when(step == SOURCES - 1)
    def _():
        dq_ref[...] = (jnp.transpose(dqt_ref[...]) * scale).astype(BF16)


def attend_back(queries, grads, group, context, lse, blocks, scale):
    rows = queries.shape[0]
    span = blocks[0].shape[0]
    keys = SOURCES * span
    whole = lambda i: (0, 0)
    return pl.pallas_call(
        functools.partial(backward_kernel, scale, span // 2),
        grid=(SOURCES,),
        in_specs=[
            pl.BlockSpec((rows, LANES), lambda i: (0, group)),
            pl.BlockSpec((rows, LANES), lambda i: (0, group)),
            pl.BlockSpec((rows, LANES), whole),
            pl.BlockSpec((2, rows), whole),
        ]
        + [pl.BlockSpec((span, LANES), whole)] * SOURCES
        + [pl.BlockSpec((span, LANES), lambda i: (0, 1))] * SOURCES,
        out_specs=[pl.BlockSpec((rows, LANES), whole)]
        + [pl.BlockSpec((span, 2 * LANES), whole)] * SOURCES,
        out_shape=[jax.ShapeDtypeStruct((rows, LANES), BF16)]
        + [jax.ShapeDtypeStruct((span, 2 * LANES), BF16)] * SOURCES,
        scratch_shapes=[
            pltpu.VMEM((2, 2 * LANES, rows), BF16),
            pltpu.VMEM((2, 2 * LANES, rows), BF16),
            pltpu.VMEM((LANES, rows), F32),
            pltpu.VMEM((span, LANES), BF16),
            pltpu.VMEM((span, LANES), BF16),
            pltpu.VMEM((span, 2 * LANES), BF16),
        ],
        compiler_params=pltpu.CompilerParams(vmem_limit_bytes=40 << 20),
        cost_estimate=pl.CostEstimate(
            flops=28 * rows * keys * LANES,
            bytes_accessed=8 * keys * LANES + 12 * rows * LANES,
            transcendentals=2 * rows * keys,
        ),
        name="attend_back",
    )(queries, grads, context, lse, *blocks, *blocks)


def body(
    tokens,
    proj_weight,
    query_bias,
    value_bias,
    out_weight,
    out_bias,
    first_gain,
    first_shift,
    up_weight,
    up_bias,
    down_weight,
    down_bias,
    second_gain,
    second_shift,
    cotangent,
):
    rows, width = tokens.shape
    heads, head_size = query_bias.shape
    local = heads * head_size
    groups = local // LANES
    scale = 1.0 / math.sqrt(head_size)
    query_weight = proj_weight[:, 0, :]
    key_weight = proj_weight[:, 1, :]
    value_weight = proj_weight[:, 2, :]
    value_shift = value_bias.reshape(local)

    own_blocks, blocks = [], []
    for group in range(groups):
        cols = slice(group * LANES, (group + 1) * LANES)
        weight = jnp.concatenate([key_weight[:, cols], value_weight[:, cols]], axis=1)
        shift = jnp.concatenate([jnp.zeros((LANES,), F32), value_shift[cols]])
        own_blocks.append((dot(tokens, weight, NN) + shift).astype(BF16))
    for own in own_blocks:
        across = flip(own, "dp", 1)
        blocks.append((own, flip(own, "dp", 0), across, flip(across, "dp", 0)))
    queries = (dot(tokens, query_weight, NN) + query_bias.reshape(local)).astype(BF16)

    outs = [attend(queries, group, blocks[group], scale) for group in range(groups)]
    context = jnp.concatenate([out.astype(BF16) for out, _ in outs], axis=1)

    step = rows // CHUNKS
    cuts = [slice(i * step, (i + 1) * step) for i in range(CHUNKS)]
    attentions = [pair_sum(dot(context[cut], out_weight, NN)) + out_bias for cut in cuts]
    firsts = [
        jax.vjp(layer_norm, tokens[cut].astype(F32) + attention, first_gain, first_shift)
        for cut, attention in zip(cuts, attentions)
    ]
    lows = [first.astype(BF16) for first, _ in firsts]
    hiddens = [dot(low, up_weight, NN) + up_bias.reshape(-1) for low in lows]
    actives = [jax.vjp(gelu_tanh, hidden) for hidden in hiddens]
    active_lows = [active.astype(BF16) for active, _ in actives]
    feeds = [pair_sum(dot(active, down_weight, NN)) + down_bias for active in active_lows]
    seconds = [
        jax.vjp(layer_norm, first + feed, second_gain, second_shift)
        for (first, _), feed in zip(firsts, feeds)
    ]
    layer_output = jnp.concatenate([second.astype(BF16) for second, _ in seconds], axis=0)
    second_grads = [
        back(cotangent[cut].astype(F32)) for cut, (_, back) in zip(cuts, seconds)
    ]
    feed_grads = [grads[0].astype(BF16) for grads in second_grads]
    hidden_lows = [
        back(dot(feed_grad, down_weight, NT))[0].astype(BF16)
        for feed_grad, (_, back) in zip(feed_grads, actives)
    ]
    first_grads = [
        grads[0] + pair_sum(dot(low, up_weight, NT))
        for grads, low in zip(second_grads, hidden_lows)
    ]
    feed_grad = jnp.concatenate(feed_grads, axis=0)
    hidden_low = jnp.concatenate(hidden_lows, axis=0)
    active_low = jnp.concatenate(active_lows, axis=0)
    first_low = jnp.concatenate(lows, axis=0)
    downweight_grad = scatter_rows(dot(feed_grad, active_low, TN).astype(BF16), BF16)
    upweight_grad = scatter_rows(dot(first_low, hidden_low, TN).astype(BF16), BF16)
    downbias_grad = jnp.sum(feed_grad.astype(F32), axis=0)
    upbias_grad = jnp.sum(hidden_low.astype(F32), axis=0)
    secondgain_grad = sum(grads[1] for grads in second_grads)
    secondshift_grad = sum(grads[2] for grads in second_grads)

    back_grads = [back(grad) for grad, (_, back) in zip(first_grads, firsts)]
    attention_back = jnp.concatenate([grads[0] for grads in back_grads], axis=0)
    firstgain_grad = sum(grads[1] for grads in back_grads)
    firstshift_grad = sum(grads[2] for grads in back_grads)
    attention_grad = attention_back.astype(BF16)
    outbias_grad = jnp.sum(attention_grad.astype(F32), axis=0)
    outweight_grad = scatter_rows(dot(attention_grad, context, TN).astype(BF16), BF16)
    context_grad = dot(attention_grad, out_weight, NT).astype(BF16)

    query_grads, key_grads, value_grads = [], [], []
    for group in range(groups):
        out, lse = outs[group]
        query_part, own, beside, across, diagonal = attend_back(
            queries, context_grad, group, out, lse, blocks[group], scale
        )
        here = own.astype(F32) + flip(beside, "dp", 0).astype(F32)
        there = across.astype(F32) + flip(diagonal, "dp", 0).astype(F32)
        total = (here + flip(there.astype(BF16), "dp", 1).astype(F32)).astype(BF16)
        query_grads.append(query_part)
        key_grads.append(total[:, :LANES])
        value_grads.append(total[:, LANES:])
    joined_grads = jnp.concatenate(query_grads + key_grads + value_grads, axis=1)
    flat_proj = jnp.concatenate([query_weight, key_weight, value_weight], axis=1)
    proj_grad = scatter_rows(dot(tokens, joined_grads, TN).astype(BF16), BF16)
    bias_grads = jnp.sum(joined_grads.astype(F32), axis=0)
    tokens_grad = attention_back + pair_sum(dot(joined_grads, flat_proj, NT))

    size = lax.axis_size("dp")

    def by_dp(vector, leading):
        return (
            vector.reshape(leading, size, -1).transpose(1, 0, 2).reshape(size, -1)
        )

    units = up_bias.shape[0]
    small = [
        (by_dp(bias_grads[:local], heads), heads),
        (by_dp(bias_grads[2 * local :], heads), heads),
        (by_dp(outbias_grad, 1), 0),
        (by_dp(firstgain_grad, 1), 0),
        (by_dp(firstshift_grad, 1), 0),
        (by_dp(upbias_grad, units), units),
        (by_dp(downbias_grad, 1), 0),
        (by_dp(secondgain_grad, 1), 0),
        (by_dp(secondshift_grad, 1), 0),
    ]
    packed = scatter_rows(jnp.concatenate([part for part, _ in small], axis=1), F32)[0]
    vectors, at = [], 0
    for part, leading in small:
        piece = packed[at : at + part.shape[1]]
        at += part.shape[1]
        vectors.append(piece.reshape(leading, -1) if leading else piece)
    return (
        layer_output,
        tokens_grad,
        proj_grad.reshape(width // size, 3, local),
        vectors[0],
        vectors[1],
        outweight_grad.T,
        vectors[2],
        vectors[3],
        vectors[4],
        upweight_grad,
        vectors[5],
        downweight_grad.T,
        vectors[6],
        vectors[7],
        vectors[8],
    )


def solution(mesh):
    return jax.shard_map(
        body,
        mesh=mesh,
        in_specs=(
            P("dp", None),
            P(None, None, "tensor"),
            P("tensor", None),
            P("tensor", None),
            P("tensor", None),
            P(),
            P(),
            P(),
            P(None, "tensor"),
            P("tensor", None),
            P("tensor", None),
            P(),
            P(),
            P(),
            P("dp", None),
        ),
        out_specs=(
            P("dp", None),
            P("dp", None),
            P("dp", None, "tensor"),
            P("tensor", "dp"),
            P("tensor", "dp"),
            P("tensor", "dp"),
            P("dp"),
            P("dp"),
            P("dp"),
            P("dp", "tensor"),
            P("tensor", "dp"),
            P("tensor", "dp"),
            P("dp"),
            P("dp"),
            P("dp"),
        ),
        check_vma=False,
    )
```

time: 1640 us -> 641 us (0.39)
  waiting for transfers between devices: 824 us -> 257 us
  matrix products: 446 us -> 76.6 us
  Pallas kernels: 0 us -> 151 us
  other arithmetic: 198 us -> 48.6 us
  blocking collectives: 63 us -> 0 us
  starting transfers between devices: 5.45 us -> 49.4 us
  local copies, waits for them, and re-layouts: 74.9 us -> 47.2 us
    dot_general x68 -> x21, matrix products: 446 us -> 76.6 us  [dot(): return lax.dot_general(left, right, dims, preferred_element_type=F32)]
    psum x4 -> x0, waiting for transfers between devices: 325 us -> none  [the longest x1 109 us: body(): attention = lax.psum(product(context, out_weight), 'tensor') + out_bias]
    reduce_scatter x4 -> x0, waiting for transfers between devices: 312 us -> none  [the longest x1 108 us: body(): lax.psum_scatter(units_parts[0], 'dp', scatter_dimension=0, tiled=True)]
    pallas_call x0 -> x8, Pallas kernels: none -> 151 us  [the longest x4 93.4 us: attend_back(): pl.pallas_call(functools.partial(backward_kernel, scale, span // 2), grid...]
    convert_element_type x10 -> x15, other arithmetic: 76.8 us -> 2.52 us  [the longest x8 1.34 us: body(): total = (here + flip(there.astype(BF16), 'dp', 1).astype(F32)).astype(BF16)]
    ppermute x4 -> x51, waiting for transfers between devices: 187 us -> 257 us  [flip(): return lax.ppermute(value, axis, pairs)]
    reduce_sum x12 -> x4, other arithmetic: 71.7 us -> 5.58 us  [the longest x1 4.1 us: body(): outbias_grad = jnp.sum(attention_grad.astype(F32), axis=0)]
    unnamed x1 -> x0, blocking collectives: 63 us -> none
  transfers between devices with their start and end apart: 12 -> 51, of which waited for: 11 -> 23; matrix products, arithmetic and copies ran while one was open for 4% -> 13% of each run, Pallas kernels for 0% -> 22%
where the time goes in v1:
time: 641 us; the launch traced here: 632 us
  waiting for transfers between devices  257 us (40%)
  Pallas kernels  151 us (24%)
  matrix products  76.6 us (12%)
  starting transfers between devices  49.4 us (8%)
  other arithmetic  48.6 us (8%)
  local copies, waits for them, and re-layouts  47.2 us (7%)
    ppermute x51, waiting for transfers between devices, flip(): return lax.ppermute(value, axis, pairs)  257 us
    pallas_call x4, Pallas kernels, attend_back(): pl.pallas_call(functools.partial(backward_kernel, scale, span // 2), grid...  93.4 us
    dot_general x21, matrix products, dot(): return lax.dot_general(left, right, dims, preferred_element_type=F32)  76.6 us
    pallas_call x4, Pallas kernels, attend(): pl.pallas_call(functools.partial(forward_kernel, scale, span // 2), grid=...  57.1 us
    ppermute x51, starting transfers between devices, flip(): return lax.ppermute(value, axis, pairs)  49.4 us
    unnamed x195, local copies, waits for them, and re-layouts  27.8 us
  transfers between devices with their start and end apart: 51, of which 23 were waited for; matrix products, arithmetic and copies ran while one was open for 13% of the time, Pallas kernels for 22%

profile of v1, /device:TPU:0, one launch (start us, length us, event | category | flops | bytes accessed | tf_op | source)
XLA Modules:
  0.0 631.6 jit_solution(16481282829956126068)
XLA Ops:
  18.6 4.6 collective-permute-done.1.refs_3_.refs_7_.refs_6_.refs_10_
  36.6 14.2 %attend.4 = (f32[1024,128]{1,0:T(8,128)S(1)}, f32[2,1024]{1,0:T(2,128)S(1)}) custom-call(bf16[1024,512]{1,0:T(8,128)(2,1)S(1)} %add_convert_fusion.2.refs_0_, bf16[1024,256]{1,0:T(8,128)(2,1)S(1)} %fusion.51.refs_1_.refs_5_.refs_4_.refs_8_, bf16[1024,256]{1,0:T(8,128)(2,1)S(1)} %collective-permute-done.refs_2_.refs_6_.refs_5_.refs_9_, ...), custom_call_target="tpu_custom_call" | custom-call | flops 8589934592 | bytes 3145728 | tf_op jit(solution)/shard_map/attend/pallas_call | solution.py:114
  56.0 14.4 %attend.5 = (f32[1024,128]{1,0:T(8,128)S(1)}, f32[2,1024]{1,0:T(2,128)S(1)}) custom-call(bf16[1024,512]{1,0:T(8,128)(2,1)S(1)} %add_convert_fusion.2.refs_0_, bf16[1024,256]{1,0:T(8,128)(2,1)S(1)} %fusion.50.refs_1_.refs_5_.refs_4_.refs_8_, bf16[1024,256]{1,0:T(8,128)(2,1)} %collective-permute-done.3.refs_2_.refs_6_.refs_5_.refs_9_, ...), custom_call_target="tpu_custom_call" | custom-call | flops 8589934592 | bytes 3145728 | tf_op jit(solution)/shard_map/attend/pallas_call | solution.py:114
  71.3 14.5 %attend.6 = (f32[1024,128]{1,0:T(8,128)S(1)}, f32[2,1024]{1,0:T(2,128)S(1)}) custom-call(bf16[1024,512]{1,0:T(8,128)(2,1)S(1)} %add_convert_fusion.2.refs_0_, bf16[1024,256]{1,0:T(8,128)(2,1)} %fusion.49.refs_1_.refs_5_.refs_4_.refs_8_, bf16[1024,256]{1,0:T(8,128)(2,1)S(1)} %collective-permute-done.6.refs_2_.refs_6_.refs_5_.refs_9_, ...), custom_call_target="tpu_custom_call" | custom-call | flops 8589934592 | bytes 3145728 | tf_op jit(solution)/shard_map/attend/pallas_call | solution.py:114
  86.0 14.0 %attend.7 = (f32[1024,128]{1,0:T(8,128)S(1)}, f32[2,1024]{1,0:T(2,128)S(1)}) custom-call(bf16[1024,512]{1,0:T(8,128)(2,1)S(1)} %add_convert_fusion.2.refs_0_, bf16[1024,256]{1,0:T(8,128)(2,1)S(1)} %copy-done.13, bf16[1024,256]{1,0:T(8,128)(2,1)S(1)} %collective-permute-done.9.refs_2_.refs_6_.refs_5_.refs_9_, ...), custom_call_target="tpu_custom_call" | custom-call | flops 8589934592 | bytes 3145728 | tf_op jit(solution)/shard_map/attend/pallas_call | solution.py:114
  105.7 24.2 %collective-permute-done.12 = bf16[512,1024]{1,0:T(8,128)(2,1)} collective-permute-done((bf16[512,1024]{1,0:T(8,128)(2,1)}, bf16[512,1024]{1,0:T(8,128)(2,1)}, u32[]{:S(2)}, u32[]{:S(2)}) %collective-permute-start.12) | collective-permute-done | bytes 1048608 | tf_op jit(solution)/shard_map/ppermute | solution.py:29
  130.0 21.9 %collective-permute-done.14 = bf16[512,1024]{1,0:T(8,128)(2,1)} collective-permute-done((bf16[512,1024]{1,0:T(8,128)(2,1)}, bf16[512,1024]{1,0:T(8,128)(2,1)}, u32[]{:S(2)}, u32[]{:S(2)}) %collective-permute-start.14) | collective-permute-done | bytes 1048608 | tf_op jit(solution)/shard_map/ppermute | solution.py:29
  163.1 6.1 multiply_convert_fusion.1
  177.9 21.0 %collective-permute-done.13 = bf16[512,1024]{1,0:T(8,128)(2,1)} collective-permute-done((bf16[512,1024]{1,0:T(8,128)(2,1)}, bf16[512,1024]{1,0:T(8,128)(2,1)}, u32[]{:S(2)}, u32[]{:S(2)}) %collective-permute-start.13) | collective-permute-done | bytes 1048608 | tf_op jit(solution)/shard_map/ppermute | solution.py:29
  198.9 21.1 %collective-permute-done.15 = bf16[512,1024]{1,0:T(8,128)(2,1)} collective-permute-done((bf16[512,1024]{1,0:T(8,128)(2,1)}, bf16[512,1024]{1,0:T(8,128)(2,1)}, u32[]{:S(2)}, u32[]{:S(2)}) %collective-permute-start.15) | collective-permute-done | bytes 1048608 | tf_op jit(solution)/shard_map/ppermute | solution.py:29
  236.6 4.8 fusion.18
  241.4 11.4 %fusion.6 = (bf16[512,2048]{1,0:T(8,128)(2,1)S(1)}, bf16[512,2048]{1,0:T(8,128)(2,1)S(1)}) fusion(f32[512,2048]{1,0:T(8,128)} %get-tuple-element.215, f32[2048]{0:T(1024)S(1)} %add.468, f32[512,2048]{1,0:T(8,128)S(1)} %fusion.105, f32[512,2048]{1,0:T(8,128)} %copy-done.85, bf16[512,1024]{1,0:T(8,128)(2,1)S(1)} %add_convert_fusion.4, ...), kind=kOutput, calls=%fused_computation.12 | convolution fusion | flops 2191523840 | bytes 22028288 | tf_op jit(solution)/shard_map/dot_general | solution.py:24
  269.8 6.6 %convolution_convert_fusion.1 = bf16[1024,2048]{1,0:T(8,128)(2,1)S(1)} fusion(bf16[512,2048]{1,0:T(8,128)(2,1)S(1)} %copy-done.56, bf16[512,2048]{1,0:T(8,128)(2,1)S(1)} %copy-done.54, bf16[512,1024]{1,0:T(8,128)(2,1)} %copy-done.63, bf16[512,1024]{1,0:T(8,128)(2,1)} %copy-done.62), kind=kOutput, calls=%fused_computation.35 | convolution fusion | flops 4309647360 | bytes 10485760 | tf_op jit(solution)/shard_map/dot_general | solution.py:24
  279.5 9.0 %collective-permute-done.16 = bf16[512,1024]{1,0:T(8,128)(2,1)} collective-permute-done((bf16[512,1024]{1,0:T(8,128)(2,1)}, bf16[512,1024]{1,0:T(8,128)(2,1)}, u32[]{:S(2)}, u32[]{:S(2)}) %collective-permute-start.16) | collective-permute-done | bytes 1048608 | tf_op jit(solution)/shard_map/ppermute | solution.py:29
  288.5 22.0 %collective-permute-done.17 = bf16[512,1024]{1,0:T(8,128)(2,1)} collective-permute-done((bf16[512,1024]{1,0:T(8,128)(2,1)}, bf16[512,1024]{1,0:T(8,128)(2,1)}, u32[]{:S(2)}, u32[]{:S(2)}) %collective-permute-start.17) | collective-permute-done | bytes 1048608 | tf_op jit(solution)/shard_map/ppermute | solution.py:29
  329.9 22.6 %attend_back.7 = (bf16[1024,128]{1,0:T(8,128)(2,1)S(1)}, bf16[1024,256]{1,0:T(8,128)(2,1)S(1)}, bf16[1024,256]{1,0:T(8,128)(2,1)S(1)}, bf16[1024,256]{1,0:T(8,128)(2,1)S(1)}, bf16[1024,256]{1,0:T(8,128)(2,1)S(1)}) custom-call(bf16[1024,512]{1,0:T(8,128)(2,1)S(1)} %copy-done.26, bf16[1024,512]{1,0:T(8,128)(2,1)S(1)} %copy-done.23, ...), custom_call_target="tpu_custom_call" | custom-call | flops 15032385536 | bytes 5767168 | tf_op jit(solution)/shard_map/attend_back/pallas_call | solution.py:237
  353.1 23.6 %attend_back.6 = (bf16[1024,128]{1,0:T(8,128)(2,1)S(1)}, bf16[1024,256]{1,0:T(8,128)(2,1)S(1)}, bf16[1024,256]{1,0:T(8,128)(2,1)S(1)}, bf16[1024,256]{1,0:T(8,128)(2,1)S(1)}, bf16[1024,256]{1,0:T(8,128)(2,1)S(1)}) custom-call(bf16[1024,512]{1,0:T(8,128)(2,1)S(1)} %copy-done.26, bf16[1024,512]{1,0:T(8,128)(2,1)S(1)} %copy-done.24, ...), custom_call_target="tpu_custom_call" | custom-call | flops 15032385536 | bytes 5767168 | tf_op jit(solution)/shard_map/attend_back/pallas_call | solution.py:237
  376.9 23.6 %attend_back.5 = (bf16[1024,128]{1,0:T(8,128)(2,1)S(1)}, bf16[1024,256]{1,0:T(8,128)(2,1)S(1)}, bf16[1024,256]{1,0:T(8,128)(2,1)S(1)}, bf16[1024,256]{1,0:T(8,128)(2,1)S(1)}, bf16[1024,256]{1,0:T(8,128)(2,1)S(1)}) custom-call(bf16[1024,512]{1,0:T(8,128)(2,1)S(1)} %copy-done.26, bf16[1024,512]{1,0:T(8,128)(2,1)S(1)} %copy-done.24, f32[1024,128]{1,0:T(8,128)S(1)} %copy-done.4, ...), custom_call_target="tpu_custom_call" | custom-call | flops 15032385536 | bytes 5767168 | tf_op jit(solution)/shard_map/attend_back/pallas_call | solution.py:237
  401.0 23.7 %attend_back.4 = (bf16[1024,128]{1,0:T(8,128)(2,1)S(1)}, bf16[1024,256]{1,0:T(8,128)(2,1)S(1)}, bf16[1024,256]{1,0:T(8,128)(2,1)S(1)}, bf16[1024,256]{1,0:T(8,128)(2,1)S(1)}, bf16[1024,256]{1,0:T(8,128)(2,1)S(1)}) custom-call(bf16[1024,512]{1,0:T(8,128)(2,1)S(1)} %copy-done.26, bf16[1024,512]{1,0:T(8,128)(2,1)S(1)} %copy-done.24, f32[1024,128]{1,0:T(8,128)S(1)} %copy-done.2, ...), custom_call_target="tpu_custom_call" | custom-call | flops 15032385536 | bytes 5767168 | tf_op jit(solution)/shard_map/attend_back/pallas_call | solution.py:237
  429.3 6.8 %collective-permute-done.40 = bf16[4,64,512]{2,1,0:T(8,128)(2,1)S(1)} collective-permute-done((bf16[4,64,512]{2,1,0:T(8,128)(2,1)S(1)}, bf16[4,64,512]{2,1,0:T(8,128)(2,1)S(1)}, u32[]{:S(2)}, u32[]{:S(2)}) %collective-permute-start.40) | collective-permute-done | bytes 262176 | tf_op jit(solution)/shard_map/ppermute | solution.py:29
  450.6 6.5 %collective-permute-done.20 = bf16[1024,256]{1,0:T(8,128)(2,1)S(1)} collective-permute-done((bf16[1024,256]{1,0:T(8,128)(2,1)S(1)}, bf16[1024,256]{1,0:T(8,128)(2,1)S(1)}, u32[]{:S(2)}, u32[]{:S(2)}) %collective-permute-start.20) | collective-permute-done | bytes 524320 | tf_op jit(solution)/shard_map/ppermute | solution.py:29
  459.1 9.2 %collective-permute-done.23 = bf16[1024,256]{1,0:T(8,128)(2,1)S(1)} collective-permute-done((bf16[1024,256]{1,0:T(8,128)(2,1)S(1)}, bf16[1024,256]{1,0:T(8,128)(2,1)S(1)}, u32[]{:S(2)}, u32[]{:S(2)}) %collective-permute-start.23) | collective-permute-done | bytes 524320 | tf_op jit(solution)/shard_map/ppermute | solution.py:29
  470.3 9.2 %collective-permute-done.26 = bf16[1024,256]{1,0:T(8,128)(2,1)S(1)} collective-permute-done((bf16[1024,256]{1,0:T(8,128)(2,1)S(1)}, bf16[1024,256]{1,0:T(8,128)(2,1)S(1)}, u32[]{:S(2)}, u32[]{:S(2)}) %collective-permute-start.26) | collective-permute-done | bytes 524320 | tf_op jit(solution)/shard_map/ppermute | solution.py:29
  479.8 9.7 %collective-permute-done.29 = bf16[1024,256]{1,0:T(8,128)(2,1)S(1)} collective-permute-done((bf16[1024,256]{1,0:T(8,128)(2,1)S(1)}, bf16[1024,256]{1,0:T(8,128)(2,1)S(1)}, u32[]{:S(2)}, u32[]{:S(2)}) %collective-permute-start.29) | collective-permute-done | bytes 524320 | tf_op jit(solution)/shard_map/ppermute | solution.py:29
  491.4 4.7 fusion.39
  498.2 5.1 convolution_convert_fusion
  513.7 18.6 %collective-permute-done.48 = bf16[4,64,2048]{2,1,0:T(8,128)(2,1)} collective-permute-done((bf16[4,64,2048]{2,1,0:T(8,128)(2,1)S(1)}, bf16[4,64,2048]{2,1,0:T(8,128)(2,1)}, u32[]{:S(2)}, u32[]{:S(2)}) %collective-permute-start.48) | collective-permute-done | bytes 1048608 | tf_op jit(solution)/shard_map/ppermute | solution.py:29
  536.2 16.1 %collective-permute-done.44 = bf16[4,64,2048]{2,1,0:T(8,128)(2,1)} collective-permute-done((bf16[4,64,2048]{2,1,0:T(8,128)(2,1)S(1)}, bf16[4,64,2048]{2,1,0:T(8,128)(2,1)}, u32[]{:S(2)}, u32[]{:S(2)}) %collective-permute-start.44) | collective-permute-done | bytes 1048608 | tf_op jit(solution)/shard_map/ppermute | solution.py:29
  559.0 12.1 %collective-permute-done.45 = bf16[2,64,2048]{2,1,0:T(8,128)(2,1)S(1)} collective-permute-done((bf16[2,64,2048]{2,1,0:T(8,128)(2,1)S(1)}, bf16[2,64,2048]{2,1,0:T(8,128)(2,1)S(1)}, u32[]{:S(2)}, u32[]{:S(2)}) %collective-permute-start.45) | collective-permute-done | bytes 524320 | tf_op jit(solution)/shard_map/ppermute | solution.py:29
  586.5 16.4 %collective-permute-done.36 = f32[4,1,576]{2,1,0:T(1,128)S(1)} collective-permute-done((f32[4,1,576]{2,1,0:T(1,128)S(1)}, f32[4,1,576]{2,1,0:T(1,128)S(1)}, u32[]{:S(2)}, u32[]{:S(2)}) %collective-permute-start.36) | collective-permute-done | bytes 9248 | tf_op jit(solution)/shard_map/ppermute | solution.py:29
  614.9 5.2 collective-permute-done.33
  622.6 7.4 %collective-permute-done.34 = bf16[1,64,1536]{2,1,0:T(8,128)(2,1)S(1)} collective-permute-done((bf16[1,64,1536]{2,1,0:T(8,128)(2,1)S(1)}, bf16[1,64,1536]{2,1,0:T(8,128)(2,1)S(1)}, u32[]{:S(2)}, u32[]{:S(2)}) %collective-permute-start.34) | collective-permute-done | bytes 196640 | tf_op jit(solution)/shard_map/ppermute | solution.py:29
  (426 shorter events, 198.7 us)
Async XLA Ops:
  12.9 21.6 %collective-permute-start.4 = (bf16[1024,256]{1,0:T(8,128)(2,1)S(1)}, bf16[1024,256]{1,0:T(8,128)(2,1)}, u32[]{:S(2)}, u32[]{:S(2)}) collective-permute-start(bf16[1024,256]{1,0:T(8,128)(2,1)S(1)} %fusion.50.refs_1_.refs_5_.refs_4_.refs_8_), channel_id=1, source_target_pairs={{0,4},{2,6},{4,0},{6,2},{8,12},{10,14},{12,8},{14,10},{16,20},{18,... | collective-permute-start | bytes 1572872 | tf_op jit(solution)/shard_map/ppermute | solution.py:29
  13.1 38.5 %collective-permute-start.3 = (bf16[1024,256]{1,0:T(8,128)(2,1)S(1)}, bf16[1024,256]{1,0:T(8,128)(2,1)}, u32[]{:S(2)}, u32[]{:S(2)}) collective-permute-start(bf16[1024,256]{1,0:T(8,128)(2,1)S(1)} %fusion.50.refs_1_.refs_5_.refs_4_.refs_8_), channel_id=1, source_target_pairs={{0,2},{2,0},{4,6},{6,4},{8,10},{10,8},{12,14},{14,12},{16,18},{18,... | collective-permute-start | bytes 1572872 | tf_op jit(solution)/shard_map/ppermute | solution.py:29
  16.8 35.2 %collective-permute-start.7 = (bf16[1024,256]{1,0:T(8,128)(2,1)}, bf16[1024,256]{1,0:T(8,128)(2,1)}, u32[]{:S(2)}, u32[]{:S(2)}) collective-permute-start(bf16[1024,256]{1,0:T(8,128)(2,1)} %fusion.49.refs_1_.refs_5_.refs_4_.refs_8_), channel_id=1, source_target_pairs={{0,4},{2,6},{4,0},{6,2},{8,12},{10,14},{12,8},{14,10},{16,20},{18,... | collective-permute-start | bytes 1572872 | tf_op jit(solution)/shard_map/ppermute | solution.py:29
  29.8 41.6 %collective-permute-start.6 = (bf16[1024,256]{1,0:T(8,128)(2,1)}, bf16[1024,256]{1,0:T(8,128)(2,1)S(1)}, u32[]{:S(2)}, u32[]{:S(2)}) collective-permute-start(bf16[1024,256]{1,0:T(8,128)(2,1)} %fusion.49.refs_1_.refs_5_.refs_4_.refs_8_), channel_id=1, source_target_pairs={{0,2},{2,0},{4,6},{6,4},{8,10},{10,8},{12,14},{14,12},{16,18},{18,... | collective-permute-start | bytes 1572872 | tf_op jit(solution)/shard_map/ppermute | solution.py:29
  34.5 21.5 %collective-permute-start.10 = (bf16[1024,256]{1,0:T(8,128)(2,1)S(1)}, bf16[1024,256]{1,0:T(8,128)(2,1)S(1)}, u32[]{:S(2)}, u32[]{:S(2)}) collective-permute-start(bf16[1024,256]{1,0:T(8,128)(2,1)S(1)} %copy-done.13), channel_id=1, source_target_pairs={{0,4},{2,6},{4,0},{6,2},{8,12},{10,14},{12,8},{14,10},{16,20},{18,... | collective-permute-start | bytes 1572872 | tf_op jit(solution)/shard_map/ppermute | solution.py:29
  51.6 34.3 %collective-permute-start.9 = (bf16[1024,256]{1,0:T(8,128)(2,1)S(1)}, bf16[1024,256]{1,0:T(8,128)(2,1)S(1)}, u32[]{:S(2)}, u32[]{:S(2)}) collective-permute-start(bf16[1024,256]{1,0:T(8,128)(2,1)S(1)} %copy-done.13), channel_id=1, source_target_pairs={{0,2},{2,0},{4,6},{6,4},{8,10},{10,8},{12,14},{14,12},{16,18},{18,... | collective-permute-start | bytes 1572872 | tf_op jit(solution)/shard_map/ppermute | solution.py:29
  56.0 29.9 %collective-permute-start.11 = (bf16[1024,256]{1,0:T(8,128)(2,1)S(1)}, bf16[1024,256]{1,0:T(8,128)(2,1)S(1)}, u32[]{:S(2)}, u32[]{:S(2)}) collective-permute-start(bf16[1024,256]{1,0:T(8,128)(2,1)S(1)} %collective-permute-done.10.refs_3_.refs_7_.refs_6_.refs_10_), channel_id=1, source_target_pairs={{0,2},{2,0},{4,6},{6,4},{8,10},{10,8},{12,14},{14,12},{16,18},{18,... | collective-permute-start | bytes 1572872 | tf_op jit(solution)/shard_map/ppermute | solution.py:29
  103.6 26.3 %collective-permute-start.12 = (bf16[512,1024]{1,0:T(8,128)(2,1)}, bf16[512,1024]{1,0:T(8,128)(2,1)}, u32[]{:S(2)}, u32[]{:S(2)}) collective-permute-start(bf16[512,1024]{1,0:T(8,128)(2,1)} %convolution_convert_fusion.5), channel_id=1, source_target_pairs={{0,1},{1,0},{2,3},{3,2},{4,5},{5,4},{6,7},{7,6},{8,9},{9,8},{10,11... | collective-permute-start | bytes 3145736 | tf_op jit(solution)/shard_map/ppermute | solution.py:29
  105.4 46.5 %collective-permute-start.14 = (bf16[512,1024]{1,0:T(8,128)(2,1)}, bf16[512,1024]{1,0:T(8,128)(2,1)}, u32[]{:S(2)}, u32[]{:S(2)}) collective-permute-start(bf16[512,1024]{1,0:T(8,128)(2,1)} %convolution_convert_fusion.4), channel_id=1, source_target_pairs={{0,1},{1,0},{2,3},{3,2},{4,5},{5,4},{6,7},{7,6},{8,9},{9,8},{10,11... | collective-permute-start | bytes 3145736 | tf_op jit(solution)/shard_map/ppermute | solution.py:29
  172.6 26.3 %collective-permute-start.13 = (bf16[512,1024]{1,0:T(8,128)(2,1)}, bf16[512,1024]{1,0:T(8,128)(2,1)}, u32[]{:S(2)}, u32[]{:S(2)}) collective-permute-start(bf16[512,1024]{1,0:T(8,128)(2,1)} %convolution_convert_fusion.9), channel_id=1, source_target_pairs={{0,1},{1,0},{2,3},{3,2},{4,5},{5,4},{6,7},{7,6},{8,9},{9,8},{10,11... | collective-permute-start | bytes 3145736 | tf_op jit(solution)/shard_map/ppermute | solution.py:29
  177.7 42.3 %collective-permute-start.15 = (bf16[512,1024]{1,0:T(8,128)(2,1)}, bf16[512,1024]{1,0:T(8,128)(2,1)}, u32[]{:S(2)}, u32[]{:S(2)}) collective-permute-start(bf16[512,1024]{1,0:T(8,128)(2,1)} %convolution_convert_fusion.8), channel_id=1, source_target_pairs={{0,1},{1,0},{2,3},{3,2},{4,5},{5,4},{6,7},{7,6},{8,9},{9,8},{10,11... | collective-permute-start | bytes 3145736 | tf_op jit(solution)/shard_map/ppermute | solution.py:29
  262.1 241.2 %collective-permute-start.47 = (bf16[8,64,2048]{2,1,0:T(8,128)(2,1)}, bf16[8,64,2048]{2,1,0:T(8,128)(2,1)}, u32[]{:S(2)}, u32[]{:S(2)}) collective-permute-start(bf16[8,64,2048]{2,1,0:T(8,128)(2,1)} %dynamic-slice_bitcast_fusion), channel_id=1, source_target_pairs={{0,2},{2,0},{4,6},{6,4},{8,10},{10,8},{12,14},{14,12},{16,18},{18,... | collective-permute-start | bytes 6291464 | tf_op jit(solution)/shard_map/ppermute | solution.py:29
  262.1 26.3 %collective-permute-start.16 = (bf16[512,1024]{1,0:T(8,128)(2,1)}, bf16[512,1024]{1,0:T(8,128)(2,1)}, u32[]{:S(2)}, u32[]{:S(2)}) collective-permute-start(bf16[512,1024]{1,0:T(8,128)(2,1)} %convolution_convert_fusion.7), channel_id=1, source_target_pairs={{0,1},{1,0},{2,3},{3,2},{4,5},{5,4},{6,7},{7,6},{8,9},{9,8},{10,11... | collective-permute-start | bytes 3145736 | tf_op jit(solution)/shard_map/ppermute | solution.py:29
  263.9 46.6 %collective-permute-start.17 = (bf16[512,1024]{1,0:T(8,128)(2,1)}, bf16[512,1024]{1,0:T(8,128)(2,1)}, u32[]{:S(2)}, u32[]{:S(2)}) collective-permute-start(bf16[512,1024]{1,0:T(8,128)(2,1)} %convolution_convert_fusion.6), channel_id=1, source_target_pairs={{0,1},{1,0},{2,3},{3,2},{4,5},{5,4},{6,7},{7,6},{8,9},{9,8},{10,11... | collective-permute-start | bytes 3145736 | tf_op jit(solution)/shard_map/ppermute | solution.py:29
  323.1 101.8 %collective-permute-start.39 = (bf16[8,64,512]{2,1,0:T(8,128)(2,1)}, bf16[8,64,512]{2,1,0:T(8,128)(2,1)}, u32[]{:S(2)}, u32[]{:S(2)}) collective-permute-start(bf16[8,64,512]{2,1,0:T(8,128)(2,1)} %dynamic-slice_bitcast_fusion.3), channel_id=1, source_target_pairs={{0,2},{2,0},{4,6},{6,4},{8,10},{10,8},{12,14},{14,12},{16,18},{18,... | collective-permute-start | bytes 1572872 | tf_op jit(solution)/shard_map/ppermute | solution.py:29
  352.5 74.6 %collective-permute-start.28 = (bf16[1024,256]{1,0:T(8,128)(2,1)S(1)}, bf16[1024,256]{1,0:T(8,128)(2,1)S(1)}, u32[]{:S(2)}, u32[]{:S(2)}) collective-permute-start(bf16[1024,256]{1,0:T(8,128)(2,1)S(1)} %get-tuple-element.70), channel_id=1, source_target_pairs={{0,2},{2,0},{4,6},{6,4},{8,10},{10,8},{12,14},{14,12},{16,18},{18,... | collective-permute-start | bytes 1572872 | tf_op jit(solution)/shard_map/ppermute | solution.py:29
  376.8 50.6 %collective-permute-start.25 = (bf16[1024,256]{1,0:T(8,128)(2,1)S(1)}, bf16[1024,256]{1,0:T(8,128)(2,1)S(1)}, u32[]{:S(2)}, u32[]{:S(2)}) collective-permute-start(bf16[1024,256]{1,0:T(8,128)(2,1)S(1)} %get-tuple-element.66), channel_id=1, source_target_pairs={{0,2},{2,0},{4,6},{6,4},{8,10},{10,8},{12,14},{14,12},{16,18},{18,... | collective-permute-start | bytes 1572872 | tf_op jit(solution)/shard_map/ppermute | solution.py:29
  400.5 43.5 %collective-permute-start.22 = (bf16[1024,256]{1,0:T(8,128)(2,1)S(1)}, bf16[1024,256]{1,0:T(8,128)(2,1)S(1)}, u32[]{:S(2)}, u32[]{:S(2)}) collective-permute-start(bf16[1024,256]{1,0:T(8,128)(2,1)S(1)} %get-tuple-element.62), channel_id=1, source_target_pairs={{0,2},{2,0},{4,6},{6,4},{8,10},{10,8},{12,14},{14,12},{16,18},{18,... | collective-permute-start | bytes 1572872 | tf_op jit(solution)/shard_map/ppermute | solution.py:29
  425.0 34.1 %collective-permute-start.21 = (bf16[1024,256]{1,0:T(8,128)(2,1)S(1)}, bf16[1024,256]{1,0:T(8,128)(2,1)S(1)}, u32[]{:S(2)}, u32[]{:S(2)}) collective-permute-start(bf16[1024,256]{1,0:T(8,128)(2,1)S(1)} %get-tuple-element.60), channel_id=1, source_target_pairs={{0,2},{2,0},{4,6},{6,4},{8,10},{10,8},{12,14},{14,12},{16,18},{18,... | collective-permute-start | bytes 1572872 | tf_op jit(solution)/shard_map/ppermute | solution.py:29
  450.6 19.7 %collective-permute-start.24 = (bf16[1024,256]{1,0:T(8,128)(2,1)S(1)}, bf16[1024,256]{1,0:T(8,128)(2,1)S(1)}, u32[]{:S(2)}, u32[]{:S(2)}) collective-permute-start(bf16[1024,256]{1,0:T(8,128)(2,1)S(1)} %get-tuple-element.64), channel_id=1, source_target_pairs={{0,2},{2,0},{4,6},{6,4},{8,10},{10,8},{12,14},{14,12},{16,18},{18,... | collective-permute-start | bytes 1572872 | tf_op jit(solution)/shard_map/ppermute | solution.py:29
  457.1 22.5 %collective-permute-start.26 = (bf16[1024,256]{1,0:T(8,128)(2,1)S(1)}, bf16[1024,256]{1,0:T(8,128)(2,1)S(1)}, u32[]{:S(2)}, u32[]{:S(2)}) collective-permute-start(bf16[1024,256]{1,0:T(8,128)(2,1)S(1)} %add_convert_fusion.8), channel_id=1, source_target_pairs={{0,4},{2,6},{4,0},{6,2},{8,12},{10,14},{12,8},{14,10},{16,20},{18,... | collective-permute-start | bytes 1572872 | tf_op jit(solution)/shard_map/ppermute | solution.py:29
  459.1 20.8 %collective-permute-start.27 = (bf16[1024,256]{1,0:T(8,128)(2,1)S(1)}, bf16[1024,256]{1,0:T(8,128)(2,1)S(1)}, u32[]{:S(2)}, u32[]{:S(2)}) collective-permute-start(bf16[1024,256]{1,0:T(8,128)(2,1)S(1)} %get-tuple-element.68), channel_id=1, source_target_pairs={{0,2},{2,0},{4,6},{6,4},{8,10},{10,8},{12,14},{14,12},{16,18},{18,... | collective-permute-start | bytes 1572872 | tf_op jit(solution)/shard_map/ppermute | solution.py:29
  468.3 21.2 %collective-permute-start.29 = (bf16[1024,256]{1,0:T(8,128)(2,1)S(1)}, bf16[1024,256]{1,0:T(8,128)(2,1)S(1)}, u32[]{:S(2)}, u32[]{:S(2)}) collective-permute-start(bf16[1024,256]{1,0:T(8,128)(2,1)S(1)} %add_convert_fusion.6), channel_id=1, source_target_pairs={{0,4},{2,6},{4,0},{6,2},{8,12},{10,14},{12,8},{14,10},{16,20},{18,... | collective-permute-start | bytes 1572872 | tf_op jit(solution)/shard_map/ppermute | solution.py:29
  470.3 37.4 %collective-permute-start.43 = (bf16[8,64,2048]{2,1,0:T(8,128)(2,1)S(1)}, bf16[8,64,2048]{2,1,0:T(8,128)(2,1)S(1)}, u32[]{:S(2)}, u32[]{:S(2)}) collective-permute-start(bf16[8,64,2048]{2,1,0:T(8,128)(2,1)S(1)} %copy-done.52), channel_id=1, source_target_pairs={{0,2},{2,0},{4,6},{6,4},{8,10},{10,8},{12,14},{14,12},{16,18},{18,... | collective-permute-start | bytes 6291464 | tf_op jit(solution)/shard_map/ppermute | solution.py:29
  496.1 79.6 %collective-permute-start.30 = (bf16[1024,1024]{1,0:T(8,128)(2,1)}, bf16[1024,1024]{1,0:T(8,128)(2,1)}, u32[]{:S(2)}, u32[]{:S(2)}) collective-permute-start(bf16[1024,1024]{1,0:T(8,128)(2,1)} %fusion.39), channel_id=1, source_target_pairs={{0,1},{1,0},{2,3},{3,2},{4,5},{5,4},{6,7},{7,6},{8,9},{9,8},{10,11... | collective-permute-start | bytes 6291464 | tf_op jit(solution)/shard_map/ppermute | solution.py:29
  506.1 26.2 %collective-permute-start.48 = (bf16[4,64,2048]{2,1,0:T(8,128)(2,1)S(1)}, bf16[4,64,2048]{2,1,0:T(8,128)(2,1)}, u32[]{:S(2)}, u32[]{:S(2)}) collective-permute-start(bf16[4,64,2048]{2,1,0:T(8,128)(2,1)S(1)} %fusion.53), channel_id=1, source_target_pairs={{0,4},{2,6},{4,0},{6,2},{8,12},{10,14},{12,8},{14,10},{16,20},{18,... | collective-permute-start | bytes 3145736 | tf_op jit(solution)/shard_map/ppermute | solution.py:29
  510.6 41.7 %collective-permute-start.44 = (bf16[4,64,2048]{2,1,0:T(8,128)(2,1)S(1)}, bf16[4,64,2048]{2,1,0:T(8,128)(2,1)}, u32[]{:S(2)}, u32[]{:S(2)}) collective-permute-start(bf16[4,64,2048]{2,1,0:T(8,128)(2,1)S(1)} %fusion.52), channel_id=1, source_target_pairs={{0,4},{2,6},{4,0},{6,2},{8,12},{10,14},{12,8},{14,10},{16,20},{18,... | collective-permute-start | bytes 3145736 | tf_op jit(solution)/shard_map/ppermute | solution.py:29
  513.6 60.0 %collective-permute-start.31 = (bf16[8,64,1536]{2,1,0:T(8,128)(2,1)S(1)}, bf16[8,64,1536]{2,1,0:T(8,128)(2,1)S(1)}, u32[]{:S(2)}, u32[]{:S(2)}) collective-permute-start(bf16[8,64,1536]{2,1,0:T(8,128)(2,1)S(1)} %dynamic-slice_bitcast_fusion.2), channel_id=1, source_target_pairs={{0,2},{2,0},{4,6},{6,4},{8,10},{10,8},{12,14},{14,12},{16,18},{18,... | collective-permute-start | bytes 4718600 | tf_op jit(solution)/shard_map/ppermute | solution.py:29
  534.5 21.1 %collective-permute-start.49 = (bf16[2,64,2048]{2,1,0:T(8,128)(2,1)S(1)}, bf16[2,64,2048]{2,1,0:T(8,128)(2,1)S(1)}, u32[]{:S(2)}, u32[]{:S(2)}) collective-permute-start(bf16[2,64,2048]{2,1,0:T(8,128)(2,1)S(1)} %fusion.56), channel_id=1, source_target_pairs={{0,8},{2,10},{4,12},{6,14},{8,0},{10,2},{12,4},{14,6},{16,24},{18,... | collective-permute-start | bytes 1572872 | tf_op jit(solution)/shard_map/ppermute | solution.py:29
  556.5 28.2 %collective-permute-start.50 = (bf16[1,64,2048]{2,1,0:T(8,128)(2,1)}, bf16[1,64,2048]{2,1,0:T(8,128)(2,1)}, u32[]{:S(2)}, u32[]{:S(2)}) collective-permute-start(bf16[1,64,2048]{2,1,0:T(8,128)(2,1)} %dynamic-slice_convert_fusion.6), channel_id=1, source_target_pairs={{0,16},{2,18},{4,20},{6,22},{8,24},{10,26},{12,28},{14,30},{16,0},... | collective-permute-start | bytes 786440 | tf_op jit(solution)/shard_map/ppermute | solution.py:29
  572.0 33.6 %collective-permute-start.46 = (bf16[1,64,2048]{2,1,0:T(8,128)(2,1)}, bf16[1,64,2048]{2,1,0:T(8,128)(2,1)S(1)}, u32[]{:S(2)}, u32[]{:S(2)}) collective-permute-start(bf16[1,64,2048]{2,1,0:T(8,128)(2,1)} %dynamic-slice_convert_fusion.7), channel_id=1, source_target_pairs={{0,16},{2,18},{4,20},{6,22},{8,24},{10,26},{12,28},{14,30},{16,0},... | collective-permute-start | bytes 786440 | tf_op jit(solution)/shard_map/ppermute | solution.py:29
  582.5 26.0 %collective-permute-start.32 = (bf16[4,64,1536]{2,1,0:T(8,128)(2,1)}, bf16[4,64,1536]{2,1,0:T(8,128)(2,1)}, u32[]{:S(2)}, u32[]{:S(2)}) collective-permute-start(bf16[4,64,1536]{2,1,0:T(8,128)(2,1)} %fusion.54), channel_id=1, source_target_pairs={{0,4},{2,6},{4,0},{6,2},{8,12},{10,14},{12,8},{14,10},{16,20},{18,... | collective-permute-start | bytes 2359304 | tf_op jit(solution)/shard_map/ppermute | solution.py:29
  (109 other events, 1316.7 us)

commit v2 on v1

--- a/solution.py
+++ b/solution.py
@@ -34,21 +34,44 @@
     return low.astype(F32) + flip(low, "tensor", 0).astype(F32)
 
 
-def scatter_rows(rows, wire):
-    size = lax.axis_size("dp")
-    mine = lax.axis_index("dp")
-    part = rows.shape[0] // size
-    whole = rows
-    bit = 0
-    while size > 1:
-        size //= 2
-        split = whole.reshape(size, 2, part, -1)
-        own = mine >> bit & 1
-        keep = lax.dynamic_index_in_dim(split, own, 1, keepdims=False)
+def after(value, *earlier):
+    return lax.optimization_barrier((value, earlier))[0]
+
+
+class Scatter:
+    def __init__(self, rows, wire):
+        self.size = lax.axis_size("dp")
+        self.part = rows.shape[0] // self.size
+        self.whole = rows
+        self.wire = wire
+        self.bit = 0
+        self.flight = None
+        self.launch()
+
+    def launch(self):
+        if self.size == 1:
+            return
+        self.size //= 2
+        split = self.whole.reshape(self.size, 2, self.part, -1)
+        own = lax.axis_index("dp") >> self.bit & 1
+        self.keep = lax.dynamic_index_in_dim(split, own, 1, keepdims=False)
         send = lax.dynamic_index_in_dim(split, 1 - own, 1, keepdims=False)
-        whole = keep.astype(F32) + flip(send.astype(wire), "dp", bit).astype(F32)
-        bit += 1
-    return whole.reshape(part, -1)
+        self.flight = flip(send.astype(self.wire), "dp", self.bit)
+        self.bit += 1
+
+    def land(self, *earlier):
+        if self.flight is None:
+            return self.whole
+        flight = after(self.flight, *earlier) if earlier else self.flight
+        self.whole = self.keep.astype(F32) + flight.astype(F32)
+        self.flight = None
+        self.launch()
+        return self.whole
+
+    def result(self):
+        while self.flight is not None:
+            self.land()
+        return self.whole.reshape(self.part, -1)
 
 
 def layer_norm(rows, gain, shift):
@@ -294,6 +317,15 @@
     value_weight = proj_weight[:, 2, :]
     value_shift = value_bias.reshape(local)
 
+    side = lax.axis_index("tensor")
+
+    def in_order(own, other, dim):
+        return jnp.where(
+            side == 0,
+            jnp.concatenate([own, other], axis=dim),
+            jnp.concatenate([other, own], axis=dim),
+        )
+
     own_blocks, blocks = [], []
     for group in range(groups):
         cols = slice(group * LANES, (group + 1) * LANES)
@@ -304,74 +336,146 @@
         across = flip(own, "dp", 1)
         blocks.append((own, flip(own, "dp", 0), across, flip(across, "dp", 0)))
     queries = (dot(tokens, query_weight, NN) + query_bias.reshape(local)).astype(BF16)
-
-    outs = [attend(queries, group, blocks[group], scale) for group in range(groups)]
-    context = jnp.concatenate([out.astype(BF16) for out, _ in outs], axis=1)
+    out_whole = in_order(out_weight, flip(out_weight, "tensor", 0), 0)
+
+    outs, own_context, other_context = [], [], []
+    for group in range(groups):
+        out, lse = attend(queries, group, blocks[group], scale)
+        outs.append((out, lse))
+        own_context.append(out.astype(BF16))
+        other_context.append(flip(own_context[-1], "tensor", 0))
+    context = jnp.concatenate(own_context, axis=1)
+    context_whole = in_order(context, jnp.concatenate(other_context, axis=1), 1)
 
     step = rows // CHUNKS
     cuts = [slice(i * step, (i + 1) * step) for i in range(CHUNKS)]
-    attentions = [pair_sum(dot(context[cut], out_weight, NN)) + out_bias for cut in cuts]
-    firsts = [
-        jax.vjp(layer_norm, tokens[cut].astype(F32) + attention, first_gain, first_shift)
-        for cut, attention in zip(cuts, attentions)
-    ]
-    lows = [first.astype(BF16) for first, _ in firsts]
-    hiddens = [dot(low, up_weight, NN) + up_bias.reshape(-1) for low in lows]
-    actives = [jax.vjp(gelu_tanh, hidden) for hidden in hiddens]
-    active_lows = [active.astype(BF16) for active, _ in actives]
-    feeds = [pair_sum(dot(active, down_weight, NN)) + down_bias for active in active_lows]
-    seconds = [
-        jax.vjp(layer_norm, first + feed, second_gain, second_shift)
-        for (first, _), feed in zip(firsts, feeds)
-    ]
-    layer_output = jnp.concatenate([second.astype(BF16) for second, _ in seconds], axis=0)
-    second_grads = [
-        back(cotangent[cut].astype(F32)) for cut, (_, back) in zip(cuts, seconds)
-    ]
-    feed_grads = [grads[0].astype(BF16) for grads in second_grads]
-    hidden_lows = [
-        back(dot(feed_grad, down_weight, NT))[0].astype(BF16)
-        for feed_grad, (_, back) in zip(feed_grads, actives)
-    ]
-    first_grads = [
-        grads[0] + pair_sum(dot(low, up_weight, NT))
-        for grads, low in zip(second_grads, hidden_lows)
-    ]
-    feed_grad = jnp.concatenate(feed_grads, axis=0)
-    hidden_low = jnp.concatenate(hidden_lows, axis=0)
+    firsts, lows, actives, active_lows, feed_lows, feed_others = [], [], [], [], [], []
+    done = context_whole
+    for cut in cuts:
+        attention = dot(after(context_whole[cut], done), out_whole, NN) + out_bias
+        first = jax.vjp(
+            layer_norm, tokens[cut].astype(F32) + attention, first_gain, first_shift
+        )
+        low = first[0].astype(BF16)
+        hidden = dot(low, up_weight, NN) + up_bias.reshape(-1)
+        active = jax.vjp(gelu_tanh, hidden)
+        active_low = active[0].astype(BF16)
+        feed_low = dot(active_low, down_weight, NN).astype(BF16)
+        done = feed_low
+        firsts.append(first)
+        lows.append(low)
+        actives.append(active)
+        active_lows.append(active_low)
+        feed_lows.append(feed_low)
+        feed_others.append(flip(feed_low, "tensor", 0))
+    seconds, second_grads, feed_grads, hidden_lows, grad_lows, grad_others = (
+        [], [], [], [], [], [],
+    )
+    for i, cut in enumerate(cuts):
+        other = after(feed_others[i], done)
+        feed = feed_lows[i].astype(F32) + other.astype(F32) + down_bias
+        second, second_back = jax.vjp(
+            layer_norm, firsts[i][0] + feed, second_gain, second_shift
+        )
+        grads = second_back(cotangent[cut].astype(F32))
+        feed_grad = grads[0].astype(BF16)
+        hidden_low = actives[i][1](dot(feed_grad, down_weight, NT))[0].astype(BF16)
+        grad_low = dot(hidden_low, up_weight, NT).astype(BF16)
+        done = grad_low
+        seconds.append(second.astype(BF16))
+        second_grads.append(grads)
+        feed_grads.append(feed_grad)
+        hidden_lows.append(hidden_low)
+        grad_lows.append(grad_low)
+        grad_others.append(flip(grad_low, "tensor", 0))
+    layer_output = jnp.concatenate(seconds, axis=0)
+    feed_grad = after(jnp.concatenate(feed_grads, axis=0), done)
     active_low = jnp.concatenate(active_lows, axis=0)
+    down_rows = dot(feed_grad, active_low, TN).astype(BF16)
+    down_scatter = Scatter(down_rows, BF16)
+    hidden_low = after(jnp.concatenate(hidden_lows, axis=0), down_rows)
     first_low = jnp.concatenate(lows, axis=0)
-    downweight_grad = scatter_rows(dot(feed_grad, active_low, TN).astype(BF16), BF16)
-    upweight_grad = scatter_rows(dot(first_low, hidden_low, TN).astype(BF16), BF16)
+    up_rows = dot(first_low, hidden_low, TN).astype(BF16)
+    up_scatter = Scatter(up_rows, BF16)
     downbias_grad = jnp.sum(feed_grad.astype(F32), axis=0)
     upbias_grad = jnp.sum(hidden_low.astype(F32), axis=0)
     secondgain_grad = sum(grads[1] for grads in second_grads)
     secondshift_grad = sum(grads[2] for grads in second_grads)
-
-    back_grads = [back(grad) for grad, (_, back) in zip(first_grads, firsts)]
-    attention_back = jnp.concatenate([grads[0] for grads in back_grads], axis=0)
-    firstgain_grad = sum(grads[1] for grads in back_grads)
-    firstshift_grad = sum(grads[2] for grads in back_grads)
+    done = down_scatter.land(up_rows)
+
+    attention_backs, firstgain_parts, firstshift_parts = [], [], []
+    for i in range(CHUNKS):
+        other = after(grad_others[i], done)
+        grad = second_grads[i][0] + (grad_lows[i].astype(F32) + other.astype(F32))
+        grads = firsts[i][1](grad)
+        attention_backs.append(grads[0])
+        firstgain_parts.append(grads[1])
+        firstshift_parts.append(grads[2])
+    attention_back = jnp.concatenate(attention_backs, axis=0)
+    firstgain_grad = sum(firstgain_parts)
+    firstshift_grad = sum(firstshift_parts)
     attention_grad = attention_back.astype(BF16)
     outbias_grad = jnp.sum(attention_grad.astype(F32), axis=0)
-    outweight_grad = scatter_rows(dot(attention_grad, context, TN).astype(BF16), BF16)
     context_grad = dot(attention_grad, out_weight, NT).astype(BF16)
+    out_rows = dot(attention_grad, context, TN).astype(BF16)
+    out_scatter = Scatter(out_rows, BF16)
 
     query_grads, key_grads, value_grads = [], [], []
-    for group in range(groups):
+    flights, crossings = {}, {}
+
+    def core_level(group, mark):
+        own, across, beside, diagonal = flights.pop(group)
+        beside, diagonal = after(beside, mark), after(diagonal, mark)
+        here = own.astype(F32) + beside.astype(F32)
+        there = (across.astype(F32) + diagonal.astype(F32)).astype(BF16)
+        crossings[group] = (here, flip(there, "dp", 1))
+        return there
+
+    def chip_level(group, mark):
+        here, there = crossings.pop(group)
+        there = after(there, mark)
+        total = (here + there.astype(F32)).astype(BF16)
+        key_grads.append(total[:, :LANES])
+        value_grads.append(total[:, LANES:])
+        return total
+
+    def launch_back(group, *earlier):
         out, lse = outs[group]
         query_part, own, beside, across, diagonal = attend_back(
-            queries, context_grad, group, out, lse, blocks[group], scale
+            after(queries, *earlier), context_grad, group, out, lse, blocks[group], scale
         )
-        here = own.astype(F32) + flip(beside, "dp", 0).astype(F32)
-        there = across.astype(F32) + flip(diagonal, "dp", 0).astype(F32)
-        total = (here + flip(there.astype(BF16), "dp", 1).astype(F32)).astype(BF16)
         query_grads.append(query_part)
-        key_grads.append(total[:, :LANES])
-        value_grads.append(total[:, LANES:])
+        flights[group] = (own, across, flip(beside, "dp", 0), flip(diagonal, "dp", 0))
+        return query_part
+
+    mark = launch_back(0, up_scatter.land(out_rows))
+    mark = launch_back(1, down_scatter.land(mark), out_scatter.land(mark))
+    mark = launch_back(
+        2,
+        core_level(0, mark),
+        up_scatter.land(mark),
+        down_scatter.land(mark),
+        out_scatter.land(mark),
+    )
+    mark = launch_back(
+        3,
+        core_level(1, mark),
+        chip_level(0, mark),
+        up_scatter.land(mark),
+        down_scatter.land(mark),
+        out_scatter.land(mark),
+    )
+    core_level(2, mark)
+    core_level(3, mark)
+    chip_level(1, mark)
+    chip_level(2, mark)
+    chip_level(3, mark)
+    outweight_grad = out_scatter.result()
+    upweight_grad = up_scatter.result()
+    downweight_grad = down_scatter.result()
     joined_grads = jnp.concatenate(query_grads + key_grads + value_grads, axis=1)
     flat_proj = jnp.concatenate([query_weight, key_weight, value_weight], axis=1)
-    proj_grad = scatter_rows(dot(tokens, joined_grads, TN).astype(BF16), BF16)
+    proj_grad = Scatter(dot(tokens, joined_grads, TN).astype(BF16), BF16).result()
     bias_grads = jnp.sum(joined_grads.astype(F32), axis=0)
     tokens_grad = attention_back + pair_sum(dot(joined_grads, flat_proj, NT))
 
@@ -394,7 +498,7 @@
         (by_dp(secondgain_grad, 1), 0),
         (by_dp(secondshift_grad, 1), 0),
     ]
-    packed = scatter_rows(jnp.concatenate([part for part, _ in small], axis=1), F32)[0]
+    packed = Scatter(jnp.concatenate([part for part, _ in small], axis=1), F32).result()[0]
     vectors, at = [], 0
     for part, leading in small:
         piece = packed[at : at + part.shape[1]]

time: 641 us -> 523 us (0.82)
  waiting for transfers between devices: 257 us -> 147 us
    ppermute x51 -> x54, waiting for transfers between devices: 257 us -> 147 us  [flip(): return lax.ppermute(value, axis, pairs)]
    ppermute x51 -> x54, starting transfers between devices: 49.4 us -> 43 us  [flip(): return lax.ppermute(value, axis, pairs)]
    add x19 -> x20, other arithmetic: 12.7 us -> 14.7 us  [the longest x18 14.7 us: land(): self.whole = self.keep.astype(F32) + flight.astype(F32)]
    unnamed x195 -> x222, local copies, waits for them, and re-layouts: 27.8 us -> 27.5 us
  transfers between devices with their start and end apart: 51 -> 54, of which waited for: 23 -> 20; matrix products, arithmetic and copies ran while one was open for 13% -> 25% of each run, Pallas kernels for 22% -> 29%
where the time goes in v2:
time: 523 us; the launch traced here: 514 us
  Pallas kernels  149 us (28%)
  waiting for transfers between devices  147 us (28%)
  matrix products  72.9 us (14%)
  other arithmetic  53.8 us (10%)
  local copies, waits for them, and re-layouts  45.5 us (9%)
  starting transfers between devices  43 us (8%)
    ppermute x54, waiting for transfers between devices, flip(): return lax.ppermute(value, axis, pairs)  147 us
    pallas_call x4, Pallas kernels, attend_back(): pl.pallas_call(functools.partial(backward_kernel, scale, span // 2), grid...  93 us
    dot_general x21, matrix products, dot(): return lax.dot_general(left, right, dims, preferred_element_type=F32)  72.9 us
    pallas_call x4, Pallas kernels, attend(): pl.pallas_call(functools.partial(forward_kernel, scale, span // 2), grid=...  55.9 us
    ppermute x54, starting transfers between devices, flip(): return lax.ppermute(value, axis, pairs)  43 us
    unnamed x222, local copies, waits for them, and re-layouts  27.5 us
    add x18, other arithmetic, land(): self.whole = self.keep.astype(F32) + flight.astype(F32)  14.7 us
  transfers between devices with their start and end apart: 54, of which 20 were waited for; matrix products, arithmetic and copies ran while one was open for 25% of the time, Pallas kernels for 29%

profile of v2, /device:TPU:0, one launch (start us, length us, event | category | flops | bytes accessed | tf_op | source)
XLA Modules:
  0.0 513.8 jit_solution(10669876188114367952)
XLA Ops:
  18.1 5.6 %collective-permute-done.1.refs_3_.refs_7_.refs_6_.refs_10_ = bf16[1024,256]{1,0:T(8,128)(2,1)} collective-permute-done((bf16[1024,256]{1,0:T(8,128)(2,1)S(1)}, bf16[1024,256]{1,0:T(8,128)(2,1)}, u32[]{:S(2)}, u32[]{:S(2)}) %collective-permute-start.1) | collective-permute-done | bytes 524320 | tf_op jit(solution)/shard_map/ppermute | solution.py:29
  30.0 4.8 collective-permute-done.4.refs_3_.refs_7_.refs_6_.refs_10_
  36.9 14.3 %attend.4 = (f32[1024,128]{1,0:T(8,128)S(1)}, f32[2,1024]{1,0:T(2,128)S(1)}) custom-call(bf16[1024,512]{1,0:T(8,128)(2,1)S(1)} %add_convert_fusion.2.refs_0_, bf16[1024,256]{1,0:T(8,128)(2,1)S(1)} %copy-done.19, bf16[1024,256]{1,0:T(8,128)(2,1)} %collective-permute-done.refs_2_.refs_6_.refs_5_.refs_9_, ...), custom_call_target="tpu_custom_call" | custom-call | flops 8589934592 | bytes 3145728 | tf_op jit(solution)/shard_map/attend/pallas_call | solution.py:137
  57.0 14.3 %attend.5 = (f32[1024,128]{1,0:T(8,128)S(1)}, f32[2,1024]{1,0:T(2,128)S(1)}) custom-call(bf16[1024,512]{1,0:T(8,128)(2,1)S(1)} %add_convert_fusion.2.refs_0_, bf16[1024,256]{1,0:T(8,128)(2,1)S(1)} %fusion.50.refs_1_.refs_5_.refs_4_.refs_8_, bf16[1024,256]{1,0:T(8,128)(2,1)} %collective-permute-done.3.refs_2_.refs_6_.refs_5_.refs_9_, ...), custom_call_target="tpu_custom_call" | custom-call | flops 8589934592 | bytes 3145728 | tf_op jit(solution)/shard_map/attend/pallas_call | solution.py:137
  71.3 13.6 %attend.6 = (f32[1024,128]{1,0:T(8,128)S(1)}, f32[2,1024]{1,0:T(2,128)S(1)}) custom-call(bf16[1024,512]{1,0:T(8,128)(2,1)S(1)} %add_convert_fusion.2.refs_0_, bf16[1024,256]{1,0:T(8,128)(2,1)S(1)} %fusion.49.refs_1_.refs_5_.refs_4_.refs_8_, bf16[1024,256]{1,0:T(8,128)(2,1)S(1)} %collective-permute-done.6.refs_2_.refs_6_.refs_5_.refs_9_, ...), custom_call_target="tpu_custom_call" | custom-call | flops 8589934592 | bytes 3145728 | tf_op jit(solution)/shard_map/attend/pallas_call | solution.py:137
  89.2 13.8 %attend.7 = (f32[1024,128]{1,0:T(8,128)S(1)}, f32[2,1024]{1,0:T(2,128)S(1)}) custom-call(bf16[1024,512]{1,0:T(8,128)(2,1)S(1)} %add_convert_fusion.2.refs_0_, bf16[1024,256]{1,0:T(8,128)(2,1)S(1)} %fusion.48.refs_1_.refs_5_.refs_4_.refs_8_, bf16[1024,256]{1,0:T(8,128)(2,1)S(1)} %collective-permute-done.9.refs_2_.refs_6_.refs_5_.refs_9_, ...), custom_call_target="tpu_custom_call" | custom-call | flops 8589934592 | bytes 3145728 | tf_op jit(solution)/shard_map/attend/pallas_call | solution.py:137
  105.6 5.1 collective-permute-done.15
  128.7 5.2 %multiply_convert_fusion = (bf16[512,2048]{1,0:T(8,128)(2,1)S(1)}, f32[512,2048]{1,0:T(8,128)}) fusion(f32[2048]{0:T(1024)S(1)} %add.461, bf16[512,1024]{1,0:T(8,128)(2,1)S(1)} %fusion.43, bf16[1024,2048]{1,0:T(8,128)(2,1)S(1)} %copy-done.87), kind=kOutput, calls=%fused_computation.31 | convolution fusion | flops 2157969408 | bytes 11542528 | tf_op jit(solution)/shard_map/dot_general | solution.py:24
  137.6 12.2 %collective-permute-done.17 = bf16[512,1024]{1,0:T(8,128)(2,1)S(1)} collective-permute-done((bf16[512,1024]{1,0:T(8,128)(2,1)S(1)}, bf16[512,1024]{1,0:T(8,128)(2,1)S(1)}, u32[]{:S(2)}, u32[]{:S(2)}) %collective-permute-start.17) | collective-permute-done | bytes 1048608 | tf_op jit(solution)/shard_map/ppermute | solution.py:29
  155.8 6.3 %fusion.6 = bf16[512,2048]{1,0:T(8,128)(2,1)} fusion(f32[512,2048]{1,0:T(8,128)S(1)} %get-tuple-element.283, f32[2048]{0:T(1024)S(1)} %add.461, bf16[512,1024]{1,0:T(8,128)(2,1)S(1)} %add_convert_fusion.4, bf16[2048,1024]{1,0:T(8,128)(2,1)S(1)} %copy-done.85), kind=kOutput, calls=%fused_computation.12 | convolution fusion | flops 2169503744 | bytes 11542528 | tf_op jit(solution)/shard_map/dot_general | solution.py:24
  162.8 6.4 %convolution_convert_fusion.5 = bf16[512,1024]{1,0:T(8,128)(2,1)} fusion(bf16[512,2048]{1,0:T(8,128)(2,1)} %fusion.6, bf16[1024,2048]{1,0:T(8,128)(2,1)} %param.23), kind=kOutput, calls=%fused_computation.105 | convolution fusion | flops 2148007936 | bytes 7340032 | tf_op jit(solution)/shard_map/dot_general | solution.py:24
  178.8 3.9 fusion.102
  186.8 4.8 fusion.13
  191.7 3.4 convolution_convert_fusion.4
  196.6 5.0 fusion.18
  211.2 7.4 %convolution_convert_fusion.1 = bf16[1024,2048]{1,0:T(8,128)(2,1)S(1)} fusion(bf16[1024,2048]{1,0:T(8,128)(2,1)} %pad_maximum_fusion, bf16[512,1024]{1,0:T(8,128)(2,1)} %copy-done.68, bf16[512,1024]{1,0:T(8,128)(2,1)} %copy-done.67), kind=kOutput, calls=%fused_computation.35 | convolution fusion | flops 4301258752 | bytes 10485760 | tf_op jit(solution)/shard_map/dot_general | solution.py:24
  226.0 5.3 %multiply_reduce_fusion.1 = (f32[1024]{0:T(1024)S(1)}, f32[512]{0:T(512)S(1)}, f32[1024]{0:T(1024)S(1)}, f32[512,1024]{1,0:T(8,128)S(1)}, f32[1024]{0:T(1024)S(1...) fusion(f32[512,1024]{1,0:T(8,128)S(1)} %copy-done.35, f32[512]{0:T(512)S(1)} %fusion.84, ...), kind=kLoop, calls=%fused_computation.71 | loop fusion | flops 13626368 | bytes 16814080 | tf_op jit(solution)/shard_map/transpose(jvp())/reduce_sum | solution.py:81
  244.3 23.6 %attend_back.4 = (bf16[1024,128]{1,0:T(8,128)(2,1)S(1)}, bf16[1024,256]{1,0:T(8,128)(2,1)S(1)}, bf16[1024,256]{1,0:T(8,128)(2,1)S(1)}, bf16[1024,256]{1,0:T(8,128)(2,1)S(1)}, bf16[1024,256]{1,0:T(8,128)(2,1)S(1)}) custom-call(bf16[1024,512]{1,0:T(8,128)(2,1)S(1)} %copy-done.32, bf16[1024,512]{1,0:T(8,128)(2,1)S(1)} %convolution_convert_fusion.2.refs_1_, ...), custom_call_target="tpu_custom_call" | custom-call | flops 15032385536 | bytes 5767168 | tf_op jit(solution)/shard_map/attend_back/pallas_call | solution.py:260
  277.4 24.1 %attend_back.5 = (bf16[1024,128]{1,0:T(8,128)(2,1)S(1)}, bf16[1024,256]{1,0:T(8,128)(2,1)S(1)}, bf16[1024,256]{1,0:T(8,128)(2,1)S(1)}, bf16[1024,256]{1,0:T(8,128)(2,1)S(1)}, bf16[1024,256]{1,0:T(8,128)(2,1)S(1)}) custom-call(bf16[1024,512]{1,0:T(8,128)(2,1)S(1)} %copy-done.33, bf16[1024,512]{1,0:T(8,128)(2,1)S(1)} %copy-done.30, f32[1024,128]{1,0:T(8,128)S(1)} %copy-done.5, ...), custom_call_target="tpu_custom_call" | custom-call | flops 15032385536 | bytes 5767168 | tf_op jit(solution)/shard_map/attend_back/pallas_call | solution.py:260
  307.1 11.8 %collective-permute-done.27 = bf16[2,64,2048]{2,1,0:T(8,128)(2,1)S(1)} collective-permute-done((bf16[2,64,2048]{2,1,0:T(8,128)(2,1)S(1)}, bf16[2,64,2048]{2,1,0:T(8,128)(2,1)S(1)}, u32[]{:S(2)}, u32[]{:S(2)}) %collective-permute-start.27) | collective-permute-done | bytes 524320 | tf_op jit(solution)/shard_map/ppermute | solution.py:29
  320.7 22.6 %attend_back.6 = (bf16[1024,128]{1,0:T(8,128)(2,1)S(1)}, bf16[1024,256]{1,0:T(8,128)(2,1)S(1)}, bf16[1024,256]{1,0:T(8,128)(2,1)S(1)}, bf16[1024,256]{1,0:T(8,128)(2,1)S(1)}, bf16[1024,256]{1,0:T(8,128)(2,1)S(1)}) custom-call(bf16[1024,512]{1,0:T(8,128)(2,1)S(1)} %copy-done.33, bf16[1024,512]{1,0:T(8,128)(2,1)S(1)} %copy-done.30, f32[1024,128]{1,0:T(8,128)S(1)} %copy-done.3, ...), custom_call_target="tpu_custom_call" | custom-call | flops 15032385536 | bytes 5767168 | tf_op jit(solution)/shard_map/attend_back/pallas_call | solution.py:260
  348.8 7.3 %collective-permute-done.33 = bf16[1,64,2048]{2,1,0:T(8,128)(2,1)S(1)} collective-permute-done((bf16[1,64,2048]{2,1,0:T(8,128)(2,1)S(1)}, bf16[1,64,2048]{2,1,0:T(8,128)(2,1)S(1)}, u32[]{:S(2)}, u32[]{:S(2)}) %collective-permute-start.33) | collective-permute-done | bytes 262176 | tf_op jit(solution)/shard_map/ppermute | solution.py:29
  357.0 22.8 %attend_back.7 = (bf16[1024,128]{1,0:T(8,128)(2,1)S(1)}, bf16[1024,256]{1,0:T(8,128)(2,1)S(1)}, bf16[1024,256]{1,0:T(8,128)(2,1)S(1)}, bf16[1024,256]{1,0:T(8,128)(2,1)S(1)}, bf16[1024,256]{1,0:T(8,128)(2,1)S(1)}) custom-call(bf16[1024,512]{1,0:T(8,128)(2,1)S(1)} %copy-done.33, bf16[1024,512]{1,0:T(8,128)(2,1)S(1)} %copy-done.30, f32[1024,128]{1,0:T(8,128)S(1)} %copy-done.1, ...), custom_call_target="tpu_custom_call" | custom-call | flops 15032385536 | bytes 5767168 | tf_op jit(solution)/shard_map/attend_back/pallas_call | solution.py:260
  383.3 12.2 %collective-permute-done.39 = bf16[1024,256]{1,0:T(8,128)(2,1)S(1)} collective-permute-done((bf16[1024,256]{1,0:T(8,128)(2,1)S(1)}, bf16[1024,256]{1,0:T(8,128)(2,1)S(1)}, u32[]{:S(2)}, u32[]{:S(2)}) %collective-permute-start.39) | collective-permute-done | bytes 524320 | tf_op jit(solution)/shard_map/ppermute | solution.py:29
  395.7 10.1 %collective-permute-done.42 = bf16[1024,256]{1,0:T(8,128)(2,1)S(1)} collective-permute-done((bf16[1024,256]{1,0:T(8,128)(2,1)S(1)}, bf16[1024,256]{1,0:T(8,128)(2,1)S(1)}, u32[]{:S(2)}, u32[]{:S(2)}) %collective-permute-start.42) | collective-permute-done | bytes 524320 | tf_op jit(solution)/shard_map/ppermute | solution.py:29
  407.7 4.6 fusion.39
  412.8 3.7 convolution_convert_fusion
  426.5 32.9 %collective-permute-done.43 = bf16[1024,1024]{1,0:T(8,128)(2,1)} collective-permute-done((bf16[1024,1024]{1,0:T(8,128)(2,1)}, bf16[1024,1024]{1,0:T(8,128)(2,1)}, u32[]{:S(2)}, u32[]{:S(2)}) %collective-permute-start.43) | collective-permute-done | bytes 2097184 | tf_op jit(solution)/shard_map/ppermute | solution.py:29
  459.4 5.4 %convert_reduce_fusion.3 = (f32[1024]{0:T(1024)S(1)}, f32[1024,1024]{1,0:T(8,128)}) fusion(f32[512,1024]{1,0:T(8,128)} %copy-done.52, f32[512,1024]{1,0:T(8,128)S(1)} %copy-done.51, bf16[1024,1024]{1,0:T(8,128)(2,1)} %collective-permute-done.43, bf16[1024,1024]{1,0:T(8,128)(2,1)} %fusion.39), kind=kLoop, calls=%fused_computation.29 | loop fusion | flops 10484736 | bytes 12587008 | tf_op jit(solution)/shard_map/reduce_sum | solution.py:418
  476.7 12.6 %collective-permute-done.45 = bf16[4,64,1536]{2,1,0:T(8,128)(2,1)S(1)} collective-permute-done((bf16[4,64,1536]{2,1,0:T(8,128)(2,1)S(1)}, bf16[4,64,1536]{2,1,0:T(8,128)(2,1)S(1)}, u32[]{:S(2)}, u32[]{:S(2)}) %collective-permute-start.45) | collective-permute-done | bytes 786464 | tf_op jit(solution)/shard_map/ppermute | solution.py:29
  493.4 8.2 %collective-permute-done.46 = bf16[2,64,1536]{2,1,0:T(8,128)(2,1)S(1)} collective-permute-done((bf16[2,64,1536]{2,1,0:T(8,128)(2,1)S(1)}, bf16[2,64,1536]{2,1,0:T(8,128)(2,1)S(1)}, u32[]{:S(2)}, u32[]{:S(2)}) %collective-permute-start.46) | collective-permute-done | bytes 393248 | tf_op jit(solution)/shard_map/ppermute | solution.py:29
  503.8 8.6 %collective-permute-done.47 = bf16[1,64,1536]{2,1,0:T(8,128)(2,1)S(1)} collective-permute-done((bf16[1,64,1536]{2,1,0:T(8,128)(2,1)S(1)}, bf16[1,64,1536]{2,1,0:T(8,128)(2,1)S(1)}, u32[]{:S(2)}, u32[]{:S(2)}) %collective-permute-start.47) | collective-permute-done | bytes 196640 | tf_op jit(solution)/shard_map/ppermute | solution.py:29
  (466 shorter events, 169.1 us)
Async XLA Ops:
  13.2 21.6 %collective-permute-start.4 = (bf16[1024,256]{1,0:T(8,128)(2,1)S(1)}, bf16[1024,256]{1,0:T(8,128)(2,1)S(1)}, u32[]{:S(2)}, u32[]{:S(2)}) collective-permute-start(bf16[1024,256]{1,0:T(8,128)(2,1)S(1)} %fusion.50.refs_1_.refs_5_.refs_4_.refs_8_), channel_id=1, source_target_pairs={{0,4},{2,6},{4,0},{6,2},{8,12},{10,14},{12,8},{14,10},{16,20},{18,... | collective-permute-start | bytes 1572872 | tf_op jit(solution)/shard_map/ppermute | solution.py:29
  13.4 37.8 %collective-permute-start.3 = (bf16[1024,256]{1,0:T(8,128)(2,1)S(1)}, bf16[1024,256]{1,0:T(8,128)(2,1)}, u32[]{:S(2)}, u32[]{:S(2)}) collective-permute-start(bf16[1024,256]{1,0:T(8,128)(2,1)S(1)} %fusion.50.refs_1_.refs_5_.refs_4_.refs_8_), channel_id=1, source_target_pairs={{0,2},{2,0},{4,6},{6,4},{8,10},{10,8},{12,14},{14,12},{16,18},{18,... | collective-permute-start | bytes 1572872 | tf_op jit(solution)/shard_map/ppermute | solution.py:29
  16.3 35.5 %collective-permute-start.7 = (bf16[1024,256]{1,0:T(8,128)(2,1)S(1)}, bf16[1024,256]{1,0:T(8,128)(2,1)S(1)}, u32[]{:S(2)}, u32[]{:S(2)}) collective-permute-start(bf16[1024,256]{1,0:T(8,128)(2,1)S(1)} %fusion.49.refs_1_.refs_5_.refs_4_.refs_8_), channel_id=1, source_target_pairs={{0,4},{2,6},{4,0},{6,2},{8,12},{10,14},{12,8},{14,10},{16,20},{18,... | collective-permute-start | bytes 1572872 | tf_op jit(solution)/shard_map/ppermute | solution.py:29
  29.4 41.8 %collective-permute-start.6 = (bf16[1024,256]{1,0:T(8,128)(2,1)S(1)}, bf16[1024,256]{1,0:T(8,128)(2,1)S(1)}, u32[]{:S(2)}, u32[]{:S(2)}) collective-permute-start(bf16[1024,256]{1,0:T(8,128)(2,1)S(1)} %fusion.49.refs_1_.refs_5_.refs_4_.refs_8_), channel_id=1, source_target_pairs={{0,2},{2,0},{4,6},{6,4},{8,10},{10,8},{12,14},{14,12},{16,18},{18,... | collective-permute-start | bytes 1572872 | tf_op jit(solution)/shard_map/ppermute | solution.py:29
  34.8 21.6 %collective-permute-start.10 = (bf16[1024,256]{1,0:T(8,128)(2,1)S(1)}, bf16[1024,256]{1,0:T(8,128)(2,1)S(1)}, u32[]{:S(2)}, u32[]{:S(2)}) collective-permute-start(bf16[1024,256]{1,0:T(8,128)(2,1)S(1)} %fusion.48.refs_1_.refs_5_.refs_4_.refs_8_), channel_id=1, source_target_pairs={{0,4},{2,6},{4,0},{6,2},{8,12},{10,14},{12,8},{14,10},{16,20},{18,... | collective-permute-start | bytes 1572872 | tf_op jit(solution)/shard_map/ppermute | solution.py:29
  51.2 36.2 %collective-permute-start.9 = (bf16[1024,256]{1,0:T(8,128)(2,1)S(1)}, bf16[1024,256]{1,0:T(8,128)(2,1)S(1)}, u32[]{:S(2)}, u32[]{:S(2)}) collective-permute-start(bf16[1024,256]{1,0:T(8,128)(2,1)S(1)} %fusion.48.refs_1_.refs_5_.refs_4_.refs_8_), channel_id=1, source_target_pairs={{0,2},{2,0},{4,6},{6,4},{8,10},{10,8},{12,14},{14,12},{16,18},{18,... | collective-permute-start | bytes 1572872 | tf_op jit(solution)/shard_map/ppermute | solution.py:29
  51.8 60.0 %collective-permute-start.16 = (bf16[512,1024]{1,0:T(8,128)(2,1)S(1)}, bf16[512,1024]{1,0:T(8,128)(2,1)S(1)}, u32[]{:S(2)}, u32[]{:S(2)}) collective-permute-start(bf16[512,1024]{1,0:T(8,128)(2,1)S(1)} %copy-done.92), channel_id=1, source_target_pairs={{0,1},{1,0},{2,3},{3,2},{4,5},{5,4},{6,7},{7,6},{8,9},{9,8},{10,11... | collective-permute-start | bytes 3145736 | tf_op jit(solution)/shard_map/ppermute | solution.py:29
  56.5 32.7 %collective-permute-start.11 = (bf16[1024,256]{1,0:T(8,128)(2,1)S(1)}, bf16[1024,256]{1,0:T(8,128)(2,1)S(1)}, u32[]{:S(2)}, u32[]{:S(2)}) collective-permute-start(bf16[1024,256]{1,0:T(8,128)(2,1)S(1)} %collective-permute-done.10.refs_3_.refs_7_.refs_6_.refs_10_), channel_id=1, source_target_pairs={{0,2},{2,0},{4,6},{6,4},{8,10},{10,8},{12,14},{14,12},{16,18},{18,... | collective-permute-start | bytes 1572872 | tf_op jit(solution)/shard_map/ppermute | solution.py:29
  85.3 20.1 %collective-permute-start.14 = (bf16[1024,128]{1,0:T(8,128)(2,1)S(1)}, bf16[1024,128]{1,0:T(8,128)(2,1)S(1)}, u32[]{:S(2)}, u32[]{:S(2)}) collective-permute-start(bf16[1024,128]{1,0:T(8,128)(2,1)S(1)} %get-tuple-element.232), channel_id=1, source_target_pairs={{0,1},{1,0},{2,3},{3,2},{4,5},{5,4},{6,7},{7,6},{8,9},{9,8},{10,11... | collective-permute-start | bytes 786440 | tf_op jit(solution)/shard_map/ppermute | solution.py:29
  123.7 26.1 %collective-permute-start.17 = (bf16[512,1024]{1,0:T(8,128)(2,1)S(1)}, bf16[512,1024]{1,0:T(8,128)(2,1)S(1)}, u32[]{:S(2)}, u32[]{:S(2)}) collective-permute-start(bf16[512,1024]{1,0:T(8,128)(2,1)S(1)} %convolution_convert_fusion.7), channel_id=1, source_target_pairs={{0,1},{1,0},{2,3},{3,2},{4,5},{5,4},{6,7},{7,6},{8,9},{9,8},{10,11... | collective-permute-start | bytes 3145736 | tf_op jit(solution)/shard_map/ppermute | solution.py:29
  137.2 35.2 %collective-permute-start.18 = (bf16[512,1024]{1,0:T(8,128)(2,1)}, bf16[512,1024]{1,0:T(8,128)(2,1)}, u32[]{:S(2)}, u32[]{:S(2)}) collective-permute-start(bf16[512,1024]{1,0:T(8,128)(2,1)} %convolution_convert_fusion.6), channel_id=1, source_target_pairs={{0,1},{1,0},{2,3},{3,2},{4,5},{5,4},{6,7},{7,6},{8,9},{9,8},{10,11... | collective-permute-start | bytes 3145736 | tf_op jit(solution)/shard_map/ppermute | solution.py:29
  169.2 56.8 %collective-permute-start.19 = (bf16[512,1024]{1,0:T(8,128)(2,1)}, bf16[512,1024]{1,0:T(8,128)(2,1)}, u32[]{:S(2)}, u32[]{:S(2)}) collective-permute-start(bf16[512,1024]{1,0:T(8,128)(2,1)} %convolution_convert_fusion.5), channel_id=1, source_target_pairs={{0,1},{1,0},{2,3},{3,2},{4,5},{5,4},{6,7},{7,6},{8,9},{9,8},{10,11... | collective-permute-start | bytes 3145736 | tf_op jit(solution)/shard_map/ppermute | solution.py:29
  195.0 30.9 %collective-permute-start.21 = (bf16[512,1024]{1,0:T(8,128)(2,1)}, bf16[512,1024]{1,0:T(8,128)(2,1)}, u32[]{:S(2)}, u32[]{:S(2)}) collective-permute-start(bf16[512,1024]{1,0:T(8,128)(2,1)} %convolution_convert_fusion.4), channel_id=1, source_target_pairs={{0,1},{1,0},{2,3},{3,2},{4,5},{5,4},{6,7},{7,6},{8,9},{9,8},{10,11... | collective-permute-start | bytes 3145736 | tf_op jit(solution)/shard_map/ppermute | solution.py:29
  218.8 22.6 %collective-permute-start.22 = (bf16[8,64,2048]{2,1,0:T(8,128)(2,1)S(1)}, bf16[8,64,2048]{2,1,0:T(8,128)(2,1)S(1)}, u32[]{:S(2)}, u32[]{:S(2)}) collective-permute-start(bf16[8,64,2048]{2,1,0:T(8,128)(2,1)S(1)} %dynamic-slice_bitcast_fusion), channel_id=1, source_target_pairs={{0,2},{2,0},{4,6},{6,4},{8,10},{10,8},{12,14},{14,12},{16,18},{18,... | collective-permute-start | bytes 6291464 | tf_op jit(solution)/shard_map/ppermute | solution.py:29
  237.2 35.5 %collective-permute-start.24 = (bf16[8,64,512]{2,1,0:T(8,128)(2,1)}, bf16[8,64,512]{2,1,0:T(8,128)(2,1)}, u32[]{:S(2)}, u32[]{:S(2)}) collective-permute-start(bf16[8,64,512]{2,1,0:T(8,128)(2,1)} %dynamic-slice_bitcast_fusion.3), channel_id=1, source_target_pairs={{0,2},{2,0},{4,6},{6,4},{8,10},{10,8},{12,14},{14,12},{16,18},{18,... | collective-permute-start | bytes 1572872 | tf_op jit(solution)/shard_map/ppermute | solution.py:29
  238.6 37.2 %collective-permute-start.23 = (bf16[4,64,2048]{2,1,0:T(8,128)(2,1)}, bf16[4,64,2048]{2,1,0:T(8,128)(2,1)}, u32[]{:S(2)}, u32[]{:S(2)}) collective-permute-start(bf16[4,64,2048]{2,1,0:T(8,128)(2,1)} %fusion.52), channel_id=1, source_target_pairs={{0,4},{2,6},{4,0},{6,2},{8,12},{10,14},{12,8},{14,10},{16,20},{18,... | collective-permute-start | bytes 3145736 | tf_op jit(solution)/shard_map/ppermute | solution.py:29
  269.7 35.9 %collective-permute-start.25 = (bf16[1024,256]{1,0:T(8,128)(2,1)}, bf16[1024,256]{1,0:T(8,128)(2,1)S(1)}, u32[]{:S(2)}, u32[]{:S(2)}) collective-permute-start(bf16[1024,256]{1,0:T(8,128)(2,1)} %copy-done.28), channel_id=1, source_target_pairs={{0,2},{2,0},{4,6},{6,4},{8,10},{10,8},{12,14},{14,12},{16,18},{18,... | collective-permute-start | bytes 1572872 | tf_op jit(solution)/shard_map/ppermute | solution.py:29
  269.7 36.6 %collective-permute-start.30 = (bf16[1024,256]{1,0:T(8,128)(2,1)}, bf16[1024,256]{1,0:T(8,128)(2,1)}, u32[]{:S(2)}, u32[]{:S(2)}) collective-permute-start(bf16[1024,256]{1,0:T(8,128)(2,1)} %copy-done.27), channel_id=1, source_target_pairs={{0,2},{2,0},{4,6},{6,4},{8,10},{10,8},{12,14},{14,12},{16,18},{18,... | collective-permute-start | bytes 1572872 | tf_op jit(solution)/shard_map/ppermute | solution.py:29
  272.1 33.2 %collective-permute-start.26 = (bf16[4,64,2048]{2,1,0:T(8,128)(2,1)S(1)}, bf16[4,64,2048]{2,1,0:T(8,128)(2,1)S(1)}, u32[]{:S(2)}, u32[]{:S(2)}) collective-permute-start(bf16[4,64,2048]{2,1,0:T(8,128)(2,1)S(1)} %fusion.53), channel_id=1, source_target_pairs={{0,4},{2,6},{4,0},{6,2},{8,12},{10,14},{12,8},{14,10},{16,20},{18,... | collective-permute-start | bytes 3145736 | tf_op jit(solution)/shard_map/ppermute | solution.py:29
  274.2 28.7 %collective-permute-start.28 = (bf16[4,64,512]{2,1,0:T(8,128)(2,1)S(1)}, bf16[4,64,512]{2,1,0:T(8,128)(2,1)S(1)}, u32[]{:S(2)}, u32[]{:S(2)}) collective-permute-start(bf16[4,64,512]{2,1,0:T(8,128)(2,1)S(1)} %fusion.77), channel_id=1, source_target_pairs={{0,4},{2,6},{4,0},{6,2},{8,12},{10,14},{12,8},{14,10},{16,20},{18,... | collective-permute-start | bytes 786440 | tf_op jit(solution)/shard_map/ppermute | solution.py:29
  303.0 43.0 %collective-permute-start.34 = (bf16[2,64,512]{2,1,0:T(8,128)(2,1)S(1)}, bf16[2,64,512]{2,1,0:T(8,128)(2,1)S(1)}, u32[]{:S(2)}, u32[]{:S(2)}) collective-permute-start(bf16[2,64,512]{2,1,0:T(8,128)(2,1)S(1)} %fusion.78), channel_id=1, source_target_pairs={{0,8},{2,10},{4,12},{6,14},{8,0},{10,2},{12,4},{14,6},{16,24},{18,... | collective-permute-start | bytes 393224 | tf_op jit(solution)/shard_map/ppermute | solution.py:29
  305.2 40.7 %collective-permute-start.29 = (bf16[1024,256]{1,0:T(8,128)(2,1)S(1)}, bf16[1024,256]{1,0:T(8,128)(2,1)S(1)}, u32[]{:S(2)}, u32[]{:S(2)}) collective-permute-start(bf16[1024,256]{1,0:T(8,128)(2,1)S(1)} %get-tuple-element.109), channel_id=1, source_target_pairs={{0,2},{2,0},{4,6},{6,4},{8,10},{10,8},{12,14},{14,12},{16,18},{18,... | collective-permute-start | bytes 1572872 | tf_op jit(solution)/shard_map/ppermute | solution.py:29
  305.6 37.7 %collective-permute-start.35 = (bf16[1024,256]{1,0:T(8,128)(2,1)S(1)}, bf16[1024,256]{1,0:T(8,128)(2,1)S(1)}, u32[]{:S(2)}, u32[]{:S(2)}) collective-permute-start(bf16[1024,256]{1,0:T(8,128)(2,1)S(1)} %get-tuple-element.122), channel_id=1, source_target_pairs={{0,2},{2,0},{4,6},{6,4},{8,10},{10,8},{12,14},{14,12},{16,18},{18,... | collective-permute-start | bytes 1572872 | tf_op jit(solution)/shard_map/ppermute | solution.py:29
  306.4 39.6 %collective-permute-start.31 = (bf16[1024,256]{1,0:T(8,128)(2,1)S(1)}, bf16[1024,256]{1,0:T(8,128)(2,1)S(1)}, u32[]{:S(2)}, u32[]{:S(2)}) collective-permute-start(bf16[1024,256]{1,0:T(8,128)(2,1)S(1)} %add_convert_fusion.12), channel_id=1, source_target_pairs={{0,4},{2,6},{4,0},{6,2},{8,12},{10,14},{12,8},{14,10},{16,20},{18,... | collective-permute-start | bytes 1572872 | tf_op jit(solution)/shard_map/ppermute | solution.py:29
  318.9 27.1 %collective-permute-start.32 = (bf16[2,64,2048]{2,1,0:T(8,128)(2,1)S(1)}, bf16[2,64,2048]{2,1,0:T(8,128)(2,1)S(1)}, u32[]{:S(2)}, u32[]{:S(2)}) collective-permute-start(bf16[2,64,2048]{2,1,0:T(8,128)(2,1)S(1)} %fusion.63), channel_id=1, source_target_pairs={{0,8},{2,10},{4,12},{6,14},{8,0},{10,2},{12,4},{14,6},{16,24},{18,... | collective-permute-start | bytes 1572872 | tf_op jit(solution)/shard_map/ppermute | solution.py:29
  346.3 34.1 %collective-permute-start.36 = (bf16[1024,256]{1,0:T(8,128)(2,1)S(1)}, bf16[1024,256]{1,0:T(8,128)(2,1)S(1)}, u32[]{:S(2)}, u32[]{:S(2)}) collective-permute-start(bf16[1024,256]{1,0:T(8,128)(2,1)S(1)} %add_convert_fusion.11), channel_id=1, source_target_pairs={{0,4},{2,6},{4,0},{6,2},{8,12},{10,14},{12,8},{14,10},{16,20},{18,... | collective-permute-start | bytes 1572872 | tf_op jit(solution)/shard_map/ppermute | solution.py:29
  347.0 36.3 %collective-permute-start.37 = (bf16[1024,256]{1,0:T(8,128)(2,1)S(1)}, bf16[1024,256]{1,0:T(8,128)(2,1)S(1)}, u32[]{:S(2)}, u32[]{:S(2)}) collective-permute-start(bf16[1024,256]{1,0:T(8,128)(2,1)S(1)} %get-tuple-element.126), channel_id=1, source_target_pairs={{0,2},{2,0},{4,6},{6,4},{8,10},{10,8},{12,14},{14,12},{16,18},{18,... | collective-permute-start | bytes 1572872 | tf_op jit(solution)/shard_map/ppermute | solution.py:29
  347.0 33.5 %collective-permute-start.38 = (bf16[1024,256]{1,0:T(8,128)(2,1)S(1)}, bf16[1024,256]{1,0:T(8,128)(2,1)S(1)}, u32[]{:S(2)}, u32[]{:S(2)}) collective-permute-start(bf16[1024,256]{1,0:T(8,128)(2,1)S(1)} %get-tuple-element.129), channel_id=1, source_target_pairs={{0,2},{2,0},{4,6},{6,4},{8,10},{10,8},{12,14},{14,12},{16,18},{18,... | collective-permute-start | bytes 1572872 | tf_op jit(solution)/shard_map/ppermute | solution.py:29
  382.6 23.2 %collective-permute-start.42 = (bf16[1024,256]{1,0:T(8,128)(2,1)S(1)}, bf16[1024,256]{1,0:T(8,128)(2,1)S(1)}, u32[]{:S(2)}, u32[]{:S(2)}) collective-permute-start(bf16[1024,256]{1,0:T(8,128)(2,1)S(1)} %add_convert_fusion.6), channel_id=1, source_target_pairs={{0,4},{2,6},{4,0},{6,2},{8,12},{10,14},{12,8},{14,10},{16,20},{18,... | collective-permute-start | bytes 1572872 | tf_op jit(solution)/shard_map/ppermute | solution.py:29
  412.3 47.1 %collective-permute-start.43 = (bf16[1024,1024]{1,0:T(8,128)(2,1)}, bf16[1024,1024]{1,0:T(8,128)(2,1)}, u32[]{:S(2)}, u32[]{:S(2)}) collective-permute-start(bf16[1024,1024]{1,0:T(8,128)(2,1)} %fusion.39), channel_id=1, source_target_pairs={{0,1},{1,0},{2,3},{3,2},{4,5},{5,4},{6,7},{7,6},{8,9},{9,8},{10,11... | collective-permute-start | bytes 6291464 | tf_op jit(solution)/shard_map/ppermute | solution.py:29
  417.9 47.3 %collective-permute-start.44 = (bf16[8,64,1536]{2,1,0:T(8,128)(2,1)}, bf16[8,64,1536]{2,1,0:T(8,128)(2,1)}, u32[]{:S(2)}, u32[]{:S(2)}) collective-permute-start(bf16[8,64,1536]{2,1,0:T(8,128)(2,1)} %dynamic-slice_bitcast_fusion.2), channel_id=1, source_target_pairs={{0,2},{2,0},{4,6},{6,4},{8,10},{10,8},{12,14},{14,12},{16,18},{18,... | collective-permute-start | bytes 4718600 | tf_op jit(solution)/shard_map/ppermute | solution.py:29
  418.8 52.8 %collective-permute-start.53 = (bf16[1,64,2048]{2,1,0:T(8,128)(2,1)}, bf16[1,64,2048]{2,1,0:T(8,128)(2,1)}, u32[]{:S(2)}, u32[]{:S(2)}) collective-permute-start(bf16[1,64,2048]{2,1,0:T(8,128)(2,1)} %dynamic-slice_convert_fusion.6), channel_id=1, source_target_pairs={{0,16},{2,18},{4,20},{6,22},{8,24},{10,26},{12,28},{14,30},{16,0},... | collective-permute-start | bytes 786440 | tf_op jit(solution)/shard_map/ppermute | solution.py:29
  (122 other events, 1293.4 us)

commit v3 on v2

--- a/solution.py
+++ b/solution.py
@@ -18,6 +18,7 @@
 NN = (((1,), (0,)), ((), ()))
 NT = (((1,), (1,)), ((), ()))
 TN = (((0,), (0,)), ((), ()))
+MESH = pl.DeviceIdType.MESH
 
 
 def dot(left, right, dims):
@@ -34,44 +35,133 @@
     return low.astype(F32) + flip(low, "tensor", 0).astype(F32)
 
 
+def partner(axis, bit):
+    place = lax.axis_index(axis)
+    return {axis: place + (1 - 2 * (place // (1 << bit) % 2)) * (1 << bit)}
+
+
+def greet(links):
+    barrier = pltpu.get_barrier_semaphore()
+    for axis, bit in links:
+        pl.semaphore_signal(
+            barrier, inc=1, device_id=partner(axis, bit), device_id_type=MESH
+        )
+    pl.semaphore_wait(barrier, len(links))
+
+
+def send(source, target, semaphores, index, axis, bit):
+    return pltpu.make_async_remote_copy(
+        src_ref=source,
+        dst_ref=target,
+        send_sem=semaphores.at[0, index],
+        recv_sem=semaphores.at[1, index],
+        device_id=partner(axis, bit),
+        device_id_type=MESH,
+    )
+
+
+def exchange_kernel(links, *refs):
+    count = len(links)
+    semaphores = refs[-1]
+    greet(sorted(set(links)))
+    copies = [
+        send(refs[i], refs[count + i], semaphores, i, *links[i]) for i in range(count)
+    ]
+    for copy in copies:
+        copy.start()
+    for copy in copies:
+        copy.wait()
+
+
+def exchange(cargo, collective_id):
+    links = [link for _, link in cargo]
+    values = [value for value, _ in cargo]
+    anywhere = pl.BlockSpec(memory_space=pl.ANY)
+    return pl.pallas_call(
+        functools.partial(exchange_kernel, links),
+        in_specs=[anywhere] * len(values),
+        out_specs=[anywhere] * len(values),
+        out_shape=[jax.ShapeDtypeStruct(v.shape, v.dtype) for v in values],
+        scratch_shapes=[pltpu.SemaphoreType.DMA((2, len(values)))],
+        compiler_params=pltpu.CompilerParams(
+            collective_id=collective_id, has_side_effects=True
+        ),
+        cost_estimate=pl.CostEstimate(
+            flops=0, bytes_accessed=16 << 20, transcendentals=0
+        ),
+        name="exchange",
+    )(*values)
+
+
 def after(value, *earlier):
     return lax.optimization_barrier((value, earlier))[0]
 
 
 class Scatter:
-    def __init__(self, rows, wire):
-        self.size = lax.axis_size("dp")
-        self.part = rows.shape[0] // self.size
+    def __init__(self, rows, wire, far_first=False):
+        size = lax.axis_size("dp")
+        bits = size.bit_length() - 1
+        self.part = rows.shape[0] // size
         self.whole = rows
         self.wire = wire
-        self.bit = 0
-        self.flight = None
-        self.launch()
-
-    def launch(self):
-        if self.size == 1:
+        self.left = list(range(bits))[::-1]
+        self.order = list(range(bits))
+        if far_first and bits > 2:
+            self.order = [0] + self.order[2:] + [1]
+        self.split()
+
+    def split(self, ready=None):
+        self.cargo = None
+        if not self.order:
             return
-        self.size //= 2
-        split = self.whole.reshape(self.size, 2, self.part, -1)
-        own = lax.axis_index("dp") >> self.bit & 1
-        self.keep = lax.dynamic_index_in_dim(split, own, 1, keepdims=False)
-        send = lax.dynamic_index_in_dim(split, 1 - own, 1, keepdims=False)
-        self.flight = flip(send.astype(self.wire), "dp", self.bit)
-        self.bit += 1
-
-    def land(self, *earlier):
-        if self.flight is None:
-            return self.whole
-        flight = after(self.flight, *earlier) if earlier else self.flight
-        self.whole = self.keep.astype(F32) + flight.astype(F32)
-        self.flight = None
-        self.launch()
+        bit = self.order.pop(0)
+        high = 1 << self.left.index(bit)
+        self.left.remove(bit)
+        if ready is None:
+            view = self.whole.reshape(high, 2, -1, self.whole.shape[-1])
+            own = lax.axis_index("dp") >> bit & 1
+            ready = [
+                lax.dynamic_index_in_dim(view, side, 1, keepdims=False).reshape(
+                    -1, view.shape[-1]
+                )
+                for side in (own, 1 - own)
+            ]
+        self.keep = ready[0]
+        self.cargo = (ready[1].astype(self.wire), ("dp", bit))
+
+    def land(self, arrived):
+        self.whole = self.keep.astype(F32) + arrived.astype(F32)
+        self.split()
         return self.whole
 
+    def fly(self):
+        value, (axis, bit) = self.cargo
+        return flip(value, axis, bit)
+
     def result(self):
-        while self.flight is not None:
-            self.land()
-        return self.whole.reshape(self.part, -1)
+        return self.whole
+
+
+class Columns(Scatter):
+    def __init__(self, other, cols):
+        self.part, self.wire = other.part, other.wire
+        self.left, self.order = list(other.left), list(other.order)
+        link = other.cargo[1]
+        self.keep = other.keep[:, cols]
+        self.cargo = (other.cargo[0][:, cols], link)
+
+
+class Ready(Scatter):
+    def __init__(self, keep, out, far_first):
+        size = lax.axis_size("dp")
+        bits = size.bit_length() - 1
+        self.part = 2 * keep.shape[0] // size
+        self.wire = out.dtype
+        self.left = list(range(bits))[::-1]
+        self.order = list(range(bits))
+        if far_first and bits > 2:
+            self.order = [0] + self.order[2:] + [1]
+        self.split([keep, out])
 
 
 def layer_norm(rows, gain, shift):
@@ -169,19 +259,36 @@
     return high, middle, rest - middle
 
 
-def backward_kernel(scale, tile, *refs):
+def backward_kernel(scale, tile, links, *refs):
+    count = len(links)
     q_ref, g_ref, o_ref, lse_ref = refs[:4]
     k_refs = refs[4 : 4 + SOURCES]
     v_refs = refs[4 + SOURCES : 4 + 2 * SOURCES]
-    dq_ref = refs[4 + 2 * SOURCES]
-    d_refs = refs[5 + 2 * SOURCES : 5 + 3 * SOURCES]
-    qt_ref, gt_ref, dqt_ref, k_ref, v_ref, d_ref = refs[5 + 3 * SOURCES :]
+    tokens_ref = refs[4 + 2 * SOURCES]
+    refs = refs[5 + 2 * SOURCES :]
+    cargo_refs, refs = refs[:count], refs[count:]
+    joined_ref, sums_ref, keep_ref, out_ref = refs[:4]
+    landing_refs, refs = refs[4 : 4 + count], refs[4 + count :]
+    qt_ref, gt_ref, dqt_ref, k_ref, v_ref, d_ref = refs[:6]
+    diagonal_ref, cross_ref, beside_ref = refs[6:9]
+    diagonal_in, cross_in, beside_in, product_ref, semaphores = refs[9:]
     step = pl.program_id(0)
     rows = q_ref.shape[0]
     span = k_ref.shape[0]
+    own_links = [("dp", 0), ("dp", 1)]
+    copies = [
+        send(cargo_refs[i], landing_refs[i], semaphores, i, *links[i])
+        for i in range(count)
+    ]
+    diagonal_copy = send(diagonal_ref, diagonal_in, semaphores, count, "dp", 0)
+    cross_copy = send(cross_ref, cross_in, semaphores, count + 1, "dp", 1)
+    beside_copy = send(beside_ref, beside_in, semaphores, count + 2, "dp", 0)
 
     @pl.when(step == 0)
     def _():
+        greet(sorted(set(own_links + links)))
+        for copy in copies:
+            copy.start()
         q = q_ref[...] * scale
         g = g_ref[...]
         products = jnp.transpose(g.astype(F32) * o_ref[...])
@@ -205,9 +312,21 @@
                 ).astype(BF16)
         dqt_ref[...] = jnp.zeros_like(dqt_ref)
 
+    @pl.when(step == 1)
+    def _():
+        diagonal_copy.start()
+
+    @pl.when(step == 2)
+    def _():
+        cross_copy.start()
+
+    @pl.when(step == 3)
+    def _():
+        beside_copy.start()
+
     for source in range(SOURCES):
 
-        @pl.when(step == source)
+        @pl.when(step == SOURCES - 1 - source)
         def _():
             k_ref[...] = k_refs[source][...]
             v_ref[...] = v_refs[source][...]
@@ -241,24 +360,59 @@
             first, parts[0][1], parts[1][1]
         ).astype(BF16)
 
-    for source in range(SOURCES):
-
-        @pl.when(step == source)
-        def _():
-            d_refs[source][...] = d_ref[...]
-
-    @pl.when(step == SOURCES - 1)
+    @pl.when(step == 0)
     def _():
-        dq_ref[...] = (jnp.transpose(dqt_ref[...]) * scale).astype(BF16)
-
-
-def attend_back(queries, grads, group, context, lse, blocks, scale):
+        diagonal_ref[...] = d_ref[...]
+
+    @pl.when(step == 1)
+    def _():
+        diagonal_copy.wait()
+        cross_ref[...] = (
+            d_ref[...].astype(F32) + diagonal_in[...].astype(F32)
+        ).astype(BF16)
+
+    @pl.when(step == 2)
+    def _():
+        beside_ref[...] = d_ref[...]
+
+    @pl.when(step == 3)
+    def _():
+        joined_ref[:, :LANES] = (jnp.transpose(dqt_ref[...]) * scale).astype(BF16)
+        beside_copy.wait()
+        cross_copy.wait()
+        joined_ref[:, LANES:] = (
+            d_ref[...].astype(F32)
+            + beside_in[...].astype(F32)
+            + cross_in[...].astype(F32)
+        ).astype(BF16)
+        joined = joined_ref[...]
+        sums_ref[...] = jnp.sum(joined.astype(F32), axis=0, keepdims=True)
+        pairs, _, part, _ = product_ref.shape
+        for pair in range(0, pairs, 2):
+            band = tokens_ref[2 * pair * part : 2 * (pair + 2) * part, :]
+            product_ref[pair : pair + 2] = (
+                dot(band, joined, NN).astype(BF16).reshape(2, 2, part, 3 * LANES)
+            )
+        side = lax.axis_index("dp") % 2
+        keep_ref[...] = product_ref[:, side].reshape(keep_ref.shape)
+        out_ref[...] = product_ref[:, 1 - side].reshape(out_ref.shape)
+        for copy in copies:
+            copy.wait()
+
+
+def attend_back(
+    queries, grads, tokens, group, context, lse, blocks, scale, cargo, collective_id
+):
     rows = queries.shape[0]
     span = blocks[0].shape[0]
     keys = SOURCES * span
+    size, width = lax.axis_size("dp"), tokens.shape[0]
     whole = lambda i: (0, 0)
+    links = [link for _, link in cargo]
+    values = [value for value, _ in cargo]
+    anywhere = pl.BlockSpec(memory_space=pl.ANY)
     return pl.pallas_call(
-        functools.partial(backward_kernel, scale, span // 2),
+        functools.partial(backward_kernel, scale, span // 2, links),
         grid=(SOURCES,),
         in_specs=[
             pl.BlockSpec((rows, LANES), lambda i: (0, group)),
@@ -267,27 +421,90 @@
             pl.BlockSpec((2, rows), whole),
         ]
         + [pl.BlockSpec((span, LANES), whole)] * SOURCES
-        + [pl.BlockSpec((span, LANES), lambda i: (0, 1))] * SOURCES,
-        out_specs=[pl.BlockSpec((rows, LANES), whole)]
-        + [pl.BlockSpec((span, 2 * LANES), whole)] * SOURCES,
-        out_shape=[jax.ShapeDtypeStruct((rows, LANES), BF16)]
-        + [jax.ShapeDtypeStruct((span, 2 * LANES), BF16)] * SOURCES,
+        + [pl.BlockSpec((span, LANES), lambda i: (0, 1))] * SOURCES
+        + [pl.BlockSpec(tokens.shape, whole)]
+        + [anywhere] * len(values),
+        out_specs=[
+            pl.BlockSpec((rows, 3 * LANES), whole),
+            pl.BlockSpec((1, 3 * LANES), whole),
+            pl.BlockSpec((width // 2, 3 * LANES), whole),
+            pl.BlockSpec((width // 2, 3 * LANES), whole),
+        ]
+        + [anywhere] * len(values),
+        out_shape=[
+            jax.ShapeDtypeStruct((rows, 3 * LANES), BF16),
+            jax.ShapeDtypeStruct((1, 3 * LANES), F32),
+            jax.ShapeDtypeStruct((width // 2, 3 * LANES), BF16),
+            jax.ShapeDtypeStruct((width // 2, 3 * LANES), BF16),
+        ]
+        + [jax.ShapeDtypeStruct(v.shape, v.dtype) for v in values],
         scratch_shapes=[
             pltpu.VMEM((2, 2 * LANES, rows), BF16),
             pltpu.VMEM((2, 2 * LANES, rows), BF16),
             pltpu.VMEM((LANES, rows), F32),
             pltpu.VMEM((span, LANES), BF16),
             pltpu.VMEM((span, LANES), BF16),
-            pltpu.VMEM((span, 2 * LANES), BF16),
-        ],
-        compiler_params=pltpu.CompilerParams(vmem_limit_bytes=40 << 20),
+        ]
+        + [pltpu.VMEM((span, 2 * LANES), BF16)] * 7
+        + [pltpu.VMEM((size // 2, 2, width // size, 3 * LANES), BF16)]
+        + [pltpu.SemaphoreType.DMA((2, len(values) + 3))],
+        compiler_params=pltpu.CompilerParams(
+            vmem_limit_bytes=60 << 20,
+            collective_id=collective_id,
+            has_side_effects=True,
+        ),
         cost_estimate=pl.CostEstimate(
             flops=28 * rows * keys * LANES,
             bytes_accessed=8 * keys * LANES + 12 * rows * LANES,
             transcendentals=2 * rows * keys,
         ),
         name="attend_back",
-    )(queries, grads, context, lse, *blocks, *blocks)
+    )(queries, grads, context, lse, *blocks, *blocks, tokens, *values)
+
+
+def merge_kernel(count, *refs):
+    sides = []
+    for base in (0, 3 * count):
+        total = None
+        for group in range(count):
+            rows = refs[base + group]
+            first, second = refs[base + count + 2 * group : base + count + 2 * group + 2]
+            for value in (
+                dot(rows[:, :LANES], first[...], NT),
+                dot(rows[:, LANES:], second[...], NT),
+            ):
+                total = value if total is None else total + value
+        sides.append(total)
+    result = sides[0] + sides[1]
+    for ref in refs[6 * count : -1]:
+        result = result + ref[...]
+    refs[-1][...] = result
+
+
+def merge(own, own_weights, other, other_weights, *extra):
+    count = len(own)
+    rows, width = own[0].shape[0], own_weights[0].shape[0]
+    tile = rows // 4
+    row_spec = pl.BlockSpec((tile, 3 * LANES), lambda i: (i, 0))
+    sum_spec = pl.BlockSpec((tile, width), lambda i: (i, 0))
+    weight_specs = [
+        pl.BlockSpec((width, LANES), lambda i: (0, 0)),
+        pl.BlockSpec((width, 2 * LANES), lambda i: (0, 0)),
+    ] * count
+    return pl.pallas_call(
+        functools.partial(merge_kernel, count),
+        grid=(rows // tile,),
+        in_specs=([row_spec] * count + weight_specs) * 2 + [sum_spec] * len(extra),
+        out_specs=sum_spec,
+        out_shape=jax.ShapeDtypeStruct((rows, width), F32),
+        compiler_params=pltpu.CompilerParams(vmem_limit_bytes=48 << 20),
+        cost_estimate=pl.CostEstimate(
+            flops=12 * count * rows * width * LANES,
+            bytes_accessed=8 * rows * width,
+            transcendentals=0,
+        ),
+        name="merge",
+    )(*own, *own_weights, *other, *other_weights, *extra)
 
 
 def body(
@@ -326,10 +543,11 @@
             jnp.concatenate([other, own], axis=dim),
         )
 
-    own_blocks, blocks = [], []
+    own_blocks, blocks, weights = [], [], []
     for group in range(groups):
         cols = slice(group * LANES, (group + 1) * LANES)
         weight = jnp.concatenate([key_weight[:, cols], value_weight[:, cols]], axis=1)
+        weights.append((query_weight[:, cols], weight))
         shift = jnp.concatenate([jnp.zeros((LANES,), F32), value_shift[cols]])
         own_blocks.append((dot(tokens, weight, NN) + shift).astype(BF16))
     for own in own_blocks:
@@ -339,7 +557,11 @@
     out_whole = in_order(out_weight, flip(out_weight, "tensor", 0), 0)
 
     outs, own_context, other_context = [], [], []
+    across = ("tensor", 0)
+    last_weights = [flip(part, "tensor", 0) for part in weights[-1]]
     for group in range(groups):
+        if group == groups - 1:
+            queries = after(queries, out_whole, *last_weights)
         out, lse = attend(queries, group, blocks[group], scale)
         outs.append((out, lse))
         own_context.append(out.astype(BF16))
@@ -393,15 +615,22 @@
     active_low = jnp.concatenate(active_lows, axis=0)
     down_rows = dot(feed_grad, active_low, TN).astype(BF16)
     down_scatter = Scatter(down_rows, BF16)
+    down_flight = down_scatter.fly()
     hidden_low = after(jnp.concatenate(hidden_lows, axis=0), down_rows)
     first_low = jnp.concatenate(lows, axis=0)
     up_rows = dot(first_low, hidden_low, TN).astype(BF16)
-    up_scatter = Scatter(up_rows, BF16)
+    up_scatter = Scatter(up_rows, BF16, True)
+    up_flight = up_scatter.fly()
     downbias_grad = jnp.sum(feed_grad.astype(F32), axis=0)
     upbias_grad = jnp.sum(hidden_low.astype(F32), axis=0)
     secondgain_grad = sum(grads[1] for grads in second_grads)
     secondshift_grad = sum(grads[2] for grads in second_grads)
-    done = down_scatter.land(up_rows)
+    done = down_scatter.land(after(down_flight, up_rows))
+    middle = down_rows.shape[1] // 2
+    down_parts = [
+        Columns(down_scatter, slice(None, middle)),
+        Columns(down_scatter, slice(middle, None)),
+    ]
 
     attention_backs, firstgain_parts, firstshift_parts = [], [], []
     for i in range(CHUNKS):
@@ -419,65 +648,7 @@
     context_grad = dot(attention_grad, out_weight, NT).astype(BF16)
     out_rows = dot(attention_grad, context, TN).astype(BF16)
     out_scatter = Scatter(out_rows, BF16)
-
-    query_grads, key_grads, value_grads = [], [], []
-    flights, crossings = {}, {}
-
-    def core_level(group, mark):
-        own, across, beside, diagonal = flights.pop(group)
-        beside, diagonal = after(beside, mark), after(diagonal, mark)
-        here = own.astype(F32) + beside.astype(F32)
-        there = (across.astype(F32) + diagonal.astype(F32)).astype(BF16)
-        crossings[group] = (here, flip(there, "dp", 1))
-        return there
-
-    def chip_level(group, mark):
-        here, there = crossings.pop(group)
-        there = after(there, mark)
-        total = (here + there.astype(F32)).astype(BF16)
-        key_grads.append(total[:, :LANES])
-        value_grads.append(total[:, LANES:])
-        return total
-
-    def launch_back(group, *earlier):
-        out, lse = outs[group]
-        query_part, own, beside, across, diagonal = attend_back(
-            after(queries, *earlier), context_grad, group, out, lse, blocks[group], scale
-        )
-        query_grads.append(query_part)
-        flights[group] = (own, across, flip(beside, "dp", 0), flip(diagonal, "dp", 0))
-        return query_part
-
-    mark = launch_back(0, up_scatter.land(out_rows))
-    mark = launch_back(1, down_scatter.land(mark), out_scatter.land(mark))
-    mark = launch_back(
-        2,
-        core_level(0, mark),
-        up_scatter.land(mark),
-        down_scatter.land(mark),
-        out_scatter.land(mark),
-    )
-    mark = launch_back(
-        3,
-        core_level(1, mark),
-        chip_level(0, mark),
-        up_scatter.land(mark),
-        down_scatter.land(mark),
-        out_scatter.land(mark),
-    )
-    core_level(2, mark)
-    core_level(3, mark)
-    chip_level(1, mark)
-    chip_level(2, mark)
-    chip_level(3, mark)
-    outweight_grad = out_scatter.result()
-    upweight_grad = up_scatter.result()
-    downweight_grad = down_scatter.result()
-    joined_grads = jnp.concatenate(query_grads + key_grads + value_grads, axis=1)
-    flat_proj = jnp.concatenate([query_weight, key_weight, value_weight], axis=1)
-    proj_grad = Scatter(dot(tokens, joined_grads, TN).astype(BF16), BF16).result()
-    bias_grads = jnp.sum(joined_grads.astype(F32), axis=0)
-    tokens_grad = attention_back + pair_sum(dot(joined_grads, flat_proj, NT))
+    up_scatter.land(after(up_flight, out_rows))
 
     size = lax.axis_size("dp")
 
@@ -486,10 +657,16 @@
             vector.reshape(leading, size, -1).transpose(1, 0, 2).reshape(size, -1)
         )
 
+    def unpack(packed, pieces):
+        vectors, at = [], 0
+        for part, leading in pieces:
+            piece = packed[at : at + part.shape[1]]
+            at += part.shape[1]
+            vectors.append(piece.reshape(leading, -1) if leading else piece)
+        return vectors
+
     units = up_bias.shape[0]
-    small = [
-        (by_dp(bias_grads[:local], heads), heads),
-        (by_dp(bias_grads[2 * local :], heads), heads),
+    early = [
         (by_dp(outbias_grad, 1), 0),
         (by_dp(firstgain_grad, 1), 0),
         (by_dp(firstshift_grad, 1), 0),
@@ -498,12 +675,85 @@
         (by_dp(secondgain_grad, 1), 0),
         (by_dp(secondshift_grad, 1), 0),
     ]
-    packed = Scatter(jnp.concatenate([part for part, _ in small], axis=1), F32).result()[0]
-    vectors, at = [], 0
-    for part, leading in small:
-        piece = packed[at : at + part.shape[1]]
-        at += part.shape[1]
-        vectors.append(piece.reshape(leading, -1) if leading else piece)
+    early_scatter = Scatter(jnp.concatenate([part for part, _ in early], axis=1), F32)
+
+    tokens_turned = tokens.T
+    trips = [[] for _ in range(groups)]
+    for group in range(groups - 1):
+        query_trip = group if group == 0 else min(group, groups - 1)
+        pair_trip = max(0, group - 1) if group < groups - 2 else groups - 1
+        trips[query_trip].append((group, 0))
+        trips[pair_trip].append((group, 1))
+    other_weights = [[None, None] for _ in range(groups - 1)] + [last_weights]
+    joined, others, sums, proj_scatters = [], [], [], []
+    active = [up_scatter, out_scatter, early_scatter, down_parts[0]]
+    for group in range(groups):
+        cargo = [scatter.cargo for scatter in active]
+        cargo += [(weights[place][piece], across) for place, piece in trips[group]]
+        if group > 0:
+            cargo.append((joined[-1], across))
+        out, lse = outs[group]
+        rows_back, row_sums, keep, outgoing, *arrived = attend_back(
+            queries,
+            context_grad,
+            tokens_turned,
+            group,
+            out,
+            lse,
+            blocks[group],
+            scale,
+            cargo,
+            group,
+        )
+        for scatter in active:
+            scatter.land(arrived.pop(0))
+        for place, piece in trips[group]:
+            other_weights[place][piece] = arrived.pop(0)
+        if group > 0:
+            others.append(arrived.pop(0))
+        joined.append(rows_back)
+        sums.append(row_sums.reshape(3, LANES))
+        proj_scatters.append(Ready(keep, outgoing, group < groups - 1))
+        active.append(proj_scatters[-1])
+        if group == 0:
+            active.append(down_parts[1])
+        active = [scatter for scatter in active if scatter.cargo is not None]
+    sums = jnp.stack(sums, axis=1).reshape(3, local)
+    late = [(by_dp(sums[0], heads), heads), (by_dp(sums[2], heads), heads)]
+    late_scatter = Scatter(jnp.concatenate([part for part, _ in late], axis=1), F32)
+    active.append(late_scatter)
+    others.append(flip(joined[-1], "tensor", 0))
+
+    def spread(parts):
+        return [piece for pair in parts for piece in pair]
+
+    partial = merge(
+        joined[:-1], spread(weights[:-1]), others[:-1], spread(other_weights[:-1])
+    )
+    stage = groups
+    while active:
+        arrived = exchange([scatter.cargo for scatter in active], stage)
+        stage += 1
+        for scatter, value in zip(active, arrived):
+            scatter.land(value)
+        active = [scatter for scatter in active if scatter.cargo is not None]
+    tokens_grad = merge(
+        joined[-1:],
+        spread(weights[-1:]),
+        others[-1:],
+        spread(other_weights[-1:]),
+        partial,
+        attention_back,
+    )
+    outweight_grad = out_scatter.result()
+    upweight_grad = up_scatter.result()
+    downweight_grad = jnp.concatenate([part.result() for part in down_parts], axis=1)
+    proj_grad = jnp.stack(
+        [scatter.result().reshape(-1, 3, LANES) for scatter in proj_scatters], axis=2
+    )
+    vectors = unpack(late_scatter.result()[0], late) + unpack(
+        early_scatter.result()[0], early
+    )
     return (
         layer_output,
         tokens_grad,

time: 523 us -> 523 us (level)
  waiting for transfers between devices: 147 us -> 35.6 us
  Pallas kernels: 149 us -> 239 us
  local copies, waits for them, and re-layouts: 45.5 us -> 88.1 us
  starting transfers between devices: 43 us -> 24 us
  other arithmetic: 53.8 us -> 67.5 us
  matrix products: 72.9 us -> 60.9 us
    ppermute x54 -> x26, waiting for transfers between devices: 147 us -> 35.6 us  [flip(): return lax.ppermute(value, axis, pairs)]
    pallas_call x4 -> x10, Pallas kernels: 93 us -> 183 us  [the longest x4 139 us: attend_back(): pl.pallas_call(functools.partial(backward_kernel, scale, span // 2, links...]
    ppermute x54 -> x26, starting transfers between devices: 43 us -> 24 us  [flip(): return lax.ppermute(value, axis, pairs)]
    dynamic_slice x0 -> x21, local copies, waits for them, and re-layouts: none -> 15.8 us  [split(): lax.dynamic_index_in_dim(view, side, 1, keepdims=False)]
    add x18 -> x38, other arithmetic: 14.7 us -> 29.1 us  [land(): self.whole = self.keep.astype(F32) + arrived.astype(F32)]
    convert_element_type x12 -> x23, local copies, waits for them, and re-layouts: 4.24 us -> 17.5 us  [split(): self.cargo = (ready[1].astype(self.wire), ('dp', bit))]
    dot_general x21 -> x19, matrix products: 72.9 us -> 60.9 us  [dot(): return lax.dot_general(left, right, dims, preferred_element_type=F32)]
    unnamed x222 -> x284, local copies, waits for them, and re-layouts: 27.5 us -> 38 us
  transfers between devices with their start and end apart: 54 -> 26, of which waited for: 20 -> 8; matrix products, arithmetic and copies ran while one was open for 25% -> 21% of each run, Pallas kernels for 29% -> 13%
where the time goes in v3:
time: 523 us; the launch traced here: 518 us
  Pallas kernels  239 us (46%)
  local copies, waits for them, and re-layouts  88.1 us (17%)
  other arithmetic  67.5 us (13%)
  matrix products  60.9 us (12%)
  waiting for transfers between devices  35.6 us (7%)
  starting transfers between devices  24 us (5%)
    pallas_call x4, Pallas kernels, attend_back(): pl.pallas_call(functools.partial(backward_kernel, scale, span // 2, links...  139 us
    dot_general x19, matrix products, dot(): return lax.dot_general(left, right, dims, preferred_element_type=F32)  60.9 us
    pallas_call x4, Pallas kernels, attend(): pl.pallas_call(functools.partial(forward_kernel, scale, span // 2), grid=...  56.3 us
    unnamed x284, local copies, waits for them, and re-layouts  38 us
    ppermute x26, waiting for transfers between devices, flip(): return lax.ppermute(value, axis, pairs)  35.6 us
    add x38, other arithmetic, land(): self.whole = self.keep.astype(F32) + arrived.astype(F32)  29.1 us
    pallas_call x4, Pallas kernels, exchange(): pl.pallas_call(functools.partial(exchange_kernel, links), in_specs=[anywh...  27.5 us
    ppermute x26, starting transfers between devices, flip(): return lax.ppermute(value, axis, pairs)  24 us
  transfers between devices with their start and end apart: 26, of which 8 were waited for; matrix products, arithmetic and copies ran while one was open for 21% of the time, Pallas kernels for 13%

profile of v3, /device:TPU:0, one launch (start us, length us, event | category | flops | bytes accessed | tf_op | source)
XLA Modules:
  0.0 518.2 jit_solution(2565660311105756970)
XLA Ops:
  7.0 3.0 collective-permute-start.1
  23.8 4.2 copy.108
  30.1 3.2 add_convert_fusion.2.refs_0_
  36.2 14.3 %attend.4 = (f32[1024,128]{1,0:T(8,128)S(1)}, f32[2,1024]{1,0:T(2,128)S(1)}) custom-call(bf16[1024,512]{1,0:T(8,128)(2,1)S(1)} %add_convert_fusion.2.refs_0_, bf16[1024,256]{1,0:T(8,128)(2,1)S(1)} %copy-done.21, bf16[1024,256]{1,0:T(8,128)(2,1)} %collective-permute-done.refs_2_.refs_6_.refs_5_.refs_9_, ...), custom_call_target="tpu_custom_call" | custom-call | flops 8589934592 | bytes 3145728 | tf_op jit(solution)/shard_map/attend/pallas_call | solution.py:227
  53.2 14.7 %attend.5 = (f32[1024,128]{1,0:T(8,128)S(1)}, f32[2,1024]{1,0:T(2,128)S(1)}) custom-call(bf16[1024,512]{1,0:T(8,128)(2,1)S(1)} %add_convert_fusion.2.refs_0_, bf16[1024,256]{1,0:T(8,128)(2,1)S(1)} %fusion.40.refs_1_.refs_5_.refs_4_.refs_8_, bf16[1024,256]{1,0:T(8,128)(2,1)} %collective-permute-done.3.refs_2_.refs_6_.refs_5_.refs_9_, ...), custom_call_target="tpu_custom_call" | custom-call | flops 8589934592 | bytes 3145728 | tf_op jit(solution)/shard_map/attend/pallas_call | solution.py:227
  70.6 13.5 %attend.6 = (f32[1024,128]{1,0:T(8,128)S(1)}, f32[2,1024]{1,0:T(2,128)S(1)}) custom-call(bf16[1024,512]{1,0:T(8,128)(2,1)S(1)} %add_convert_fusion.2.refs_0_, bf16[1024,256]{1,0:T(8,128)(2,1)S(1)} %fusion.39.refs_1_.refs_5_.refs_4_.refs_8_, bf16[1024,256]{1,0:T(8,128)(2,1)S(1)} %collective-permute-done.6.refs_2_.refs_6_.refs_5_.refs_9_, ...), custom_call_target="tpu_custom_call" | custom-call | flops 8589934592 | bytes 3145728 | tf_op jit(solution)/shard_map/attend/pallas_call | solution.py:227
  85.3 8.3 %collective-permute-done.11.refs_5_ = bf16[1024,256]{1,0:T(8,128)(2,1)S(1)} collective-permute-done((bf16[1024,256]{1,0:T(8,128)(2,1)S(1)}, bf16[1024,256]{1,0:T(8,128)(2,1)S(1)}, u32[]{:S(2)}, u32[]{:S(2)}) %collective-permute-start.11) | collective-permute-done | bytes 524320 | tf_op jit(solution)/shard_map/ppermute | solution.py:30
  97.6 13.8 %attend.7 = (f32[1024,128]{1,0:T(8,128)S(1)}, f32[2,1024]{1,0:T(2,128)S(1)}) custom-call(bf16[1024,512]{1,0:T(8,128)(2,1)S(1)} %add_convert_fusion.2.refs_0_, bf16[1024,256]{1,0:T(8,128)(2,1)S(1)} %fusion.38.refs_1_.refs_5_.refs_4_.refs_8_, bf16[1024,256]{1,0:T(8,128)(2,1)S(1)} %collective-permute-done.12.refs_2_.refs_6_.refs_5_.refs_9_, ...), custom_call_target="tpu_custom_call" | custom-call | flops 8589934592 | bytes 3145728 | tf_op jit(solution)/shard_map/attend/pallas_call | solution.py:227
  113.2 5.0 collective-permute-done.18
  124.3 5.2 %multiply_convert_fusion.1 = (bf16[512,2048]{1,0:T(8,128)(2,1)S(1)}, f32[512,2048]{1,0:T(8,128)}) fusion(f32[2048]{0:T(1024)S(1)} %add.512, bf16[512,1024]{1,0:T(8,128)(2,1)S(1)} %fusion.32, bf16[1024,2048]{1,0:T(8,128)(2,1)S(1)} %copy-done.131), kind=kOutput, calls=%fused_computation.30 | convolution fusion | flops 2157969408 | bytes 11542528 | tf_op jit(solution)/shard_map/dot_general | solution.py:25
  135.6 3.3 multiply_convert_fusion
  143.7 14.3 %collective-permute-done.19 = bf16[512,1024]{1,0:T(8,128)(2,1)S(1)} collective-permute-done((bf16[512,1024]{1,0:T(8,128)(2,1)S(1)}, bf16[512,1024]{1,0:T(8,128)(2,1)S(1)}, u32[]{:S(2)}, u32[]{:S(2)}) %collective-permute-start.19) | collective-permute-done | bytes 1048608 | tf_op jit(solution)/shard_map/ppermute | solution.py:30
  164.9 6.6 %fusion.6 = bf16[512,2048]{1,0:T(8,128)(2,1)S(1)} fusion(f32[512,2048]{1,0:T(8,128)} %get-tuple-element.330, f32[2048]{0:T(1024)S(1)} %add.512, bf16[512,1024]{1,0:T(8,128)(2,1)S(1)} %add_convert_fusion.4, bf16[2048,1024]{1,0:T(8,128)(2,1)S(1)} %copy-done.130), kind=kOutput, calls=%fused_computation.11 | convolution fusion | flops 2169503744 | bytes 11542528 | tf_op jit(solution)/shard_map/dot_general | solution.py:25
  171.5 3.4 convolution_convert_fusion.4
  176.4 4.0 collective-permute-done.20
  186.0 4.8 fusion.13
  190.8 3.4 convolution_convert_fusion.3
  194.2 5.2 fusion.18
  211.6 7.4 %convolution_convert_fusion = bf16[1024,2048]{1,0:T(8,128)(2,1)S(1)} fusion(bf16[1024,2048]{1,0:T(8,128)(2,1)} %pad_maximum_fusion, bf16[512,1024]{1,0:T(8,128)(2,1)} %copy-done.69, bf16[512,1024]{1,0:T(8,128)(2,1)} %copy-done.68), kind=kOutput, calls=%fused_computation.32 | convolution fusion | flops 4301258752 | bytes 10485760 | tf_op jit(solution)/shard_map/dot_general | solution.py:25
  223.3 4.6 convert_add_fusion.1
  230.4 3.9 multiply_reduce_fusion.1
  256.6 35.8 %attend_back.4 = (bf16[1024,384]{1,0:T(8,128)(2,1)}, f32[1,384]{1,0:T(1,128)}, bf16[512,384]{1,0:T(8,128)(2,1)}, bf16[512,384]{1,0:T(8,128)(2,1)}, bf16[256,2048...) custom-call(bf16[1024,512]{1,0:T(8,128)(2,1)} %copy-done.31, ...), custom_call_target="tpu_custom_call" | custom-call | flops 15032385536 | bytes 5767168 | tf_op jit(solution)/shard_map/attend_back/pallas_call | solution.py:414
  294.4 3.2 constant_dynamic-slice_fusion.26
  304.3 36.6 %attend_back.5 = (bf16[1024,384]{1,0:T(8,128)(2,1)}, f32[1,384]{1,0:T(1,128)}, bf16[512,384]{1,0:T(8,128)(2,1)}, bf16[512,384]{1,0:T(8,128)(2,1)}, bf16[128,2048...) custom-call(bf16[1024,512]{1,0:T(8,128)(2,1)} %copy-done.31, ...), custom_call_target="tpu_custom_call" | custom-call | flops 15032385536 | bytes 5767168 | tf_op jit(solution)/shard_map/attend_back/pallas_call | solution.py:414
  351.7 31.5 %attend_back.6 = (bf16[1024,384]{1,0:T(8,128)(2,1)}, f32[1,384]{1,0:T(1,128)}, bf16[512,384]{1,0:T(8,128)(2,1)}, bf16[512,384]{1,0:T(8,128)(2,1)}, bf16[64,2048]...) custom-call(bf16[1024,512]{1,0:T(8,128)(2,1)} %copy-done.31, ...), custom_call_target="tpu_custom_call" | custom-call | flops 15032385536 | bytes 5767168 | tf_op jit(solution)/shard_map/attend_back/pallas_call | solution.py:414
  388.8 34.6 %attend_back.7 = (bf16[1024,384]{1,0:T(8,128)(2,1)}, f32[1,384]{1,0:T(1,128)}, bf16[512,384]{1,0:T(8,128)(2,1)}, bf16[512,384]{1,0:T(8,128)(2,1)}, bf16[64,512]{...) custom-call(bf16[1024,512]{1,0:T(8,128)(2,1)} %copy-done.31, ...), custom_call_target="tpu_custom_call" | custom-call | flops 15032385536 | bytes 5767168 | tf_op jit(solution)/shard_map/attend_back/pallas_call | solution.py:414
  429.4 9.7 %exchange.4 = (bf16[64,384]{1,0:T(8,128)(2,1)}, bf16[128,384]{1,0:T(8,128)(2,1)}, bf16[256,384]{1,0:T(8,128)(2,1)}, bf16[512,384]{1,0:T(8,128)(2,1)}, f32[8,64]{1,0:T(8,128)}) custom-call(bf16[64,384]{1,0:T(8,128)(2,1)} %fusion.58.refs_0_, bf16[128,384]{1,0:T(8,128)(2,1)} %fusion.55.refs_1_, bf16[256,384]{1,0:T(8,128)(2,1)} %bitcast.313, ...), custom_call_target="tpu_custom_call" | custom-call | bytes 16777216 | tf_op jit(solution)/shard_map/exchange/pallas_call | solution.py:80
  443.1 7.4 %exchange.5 = (bf16[64,384]{1,0:T(8,128)(2,1)}, bf16[128,384]{1,0:T(8,128)(2,1)}, bf16[256,384]{1,0:T(8,128)(2,1)}, f32[4,64]{1,0:T(4,128)}) custom-call(bf16[64,384]{1,0:T(8,128)(2,1)} %fusion.59.refs_0_, bf16[128,384]{1,0:T(8,128)(2,1)} %fusion.56.refs_1_, bf16[256,384]{1,0:T(8,128)(2,1)} %bitcast.314, f32[4,64]{1,0:T(4,128)} %bitcast.337), custom_call_target="tpu_custom_call" | custom-call | bytes 16777216 | tf_op jit(solution)/shard_map/exchange/pallas_call | solution.py:80
  462.5 5.0 exchange.6
  471.8 5.4 %exchange.7 = (bf16[64,384]{1,0:T(8,128)(2,1)}, f32[1,64]{1,0:T(1,128)}) custom-call(bf16[64,384]{1,0:T(8,128)(2,1)} %fusion.61.refs_0_, f32[1,64]{1,0:T(1,128)} %constant_dynamic-slice_fusion.4.refs_1_), custom_call_target="tpu_custom_call" | custom-call | bytes 16777216 | tf_op jit(solution)/shard_map/exchange/pallas_call | solution.py:80
  494.3 9.7 %merge.2.refs_6_ = f32[1024,1024]{1,0:T(8,128)} custom-call(bf16[1024,384]{1,0:T(8,128)(2,1)S(1)} %copy-done.27, bf16[1024,384]{1,0:T(8,128)(2,1)} %get-tuple-element.129.refs_21_.refs_1_, bf16[1024,384]{1,0:T(8,128)(2,1)} %get-tuple-element.137.refs_20_.refs_2_, bf16[1024,128]{1,0:T(8,128)(2,1)S(1)} %copy-done.14, bf16[1024,256]{1,0:T(8,128)(2,1)S(1)} %copy-done.5, ...), custom_call_target="tpu_custom_call" | custom-call | flops 4831838208 | bytes 8388608 | tf_op jit(solution)/shard_map/merge/pallas_call | solution.py:494
  510.9 7.1 %merge.3 = f32[1024,1024]{1,0:T(8,128)} custom-call(bf16[1024,384]{1,0:T(8,128)(2,1)S(1)} %copy-done, bf16[1024,128]{1,0:T(8,128)(2,1)S(1)} %get-tuple-element.278.refs_1_, bf16[1024,256]{1,0:T(8,128)(2,1)S(1)} %pad_maximum_fusion.7.refs_2_, bf16[1024,384]{1,0:T(8,128)(2,1)S(1)} %collective-permute-done.25.refs_3_, bf16[1024,128]{1,0:T(8,128)(2,1)S(1)} %copy-done.11, ...), custom_call_target="tpu_custom_call" | custom-call | flops 1610612736 | bytes 8388608 | tf_op jit(solution)/shard_map/merge/pallas_call | solution.py:494
  (529 shorter events, 183.2 us)
Async XLA Ops:
  7.0 15.9 %collective-permute-start.1 = (bf16[1024,256]{1,0:T(8,128)(2,1)S(1)}, bf16[1024,256]{1,0:T(8,128)(2,1)}, u32[]{:S(2)}, u32[]{:S(2)}) collective-permute-start(bf16[1024,256]{1,0:T(8,128)(2,1)S(1)} %fusion.41.refs_1_.refs_5_.refs_4_.refs_8_), channel_id=1, source_target_pairs={{0,4},{2,6},{4,0},{6,2},{8,12},{10,14},{12,8},{14,10},{16,20},{18,... | collective-permute-start | bytes 1572872 | tf_op jit(solution)/shard_map/ppermute | solution.py:30
  10.1 23.2 %collective-permute-start = (bf16[1024,256]{1,0:T(8,128)(2,1)S(1)}, bf16[1024,256]{1,0:T(8,128)(2,1)}, u32[]{:S(2)}, u32[]{:S(2)}) collective-permute-start(bf16[1024,256]{1,0:T(8,128)(2,1)S(1)} %fusion.41.refs_1_.refs_5_.refs_4_.refs_8_), channel_id=1, source_target_pairs={{0,2},{2,0},{4,6},{6,4},{8,10},{10,8},{12,14},{14,12},{16,18},{18,... | collective-permute-start | bytes 1572872 | tf_op jit(solution)/shard_map/ppermute | solution.py:30
  12.5 40.7 %copy-start.18 = (bf16[1024,256]{1,0:T(8,128)(2,1)}, bf16[1024,256]{1,0:T(8,128)(2,1)S(1)}, u32[]{:S(2)}) copy-start(bf16[1024,256]{1,0:T(8,128)(2,1)S(1)} %fusion.40.refs_1_.refs_5_.refs_4_.refs_8_) | copy-start | bytes 1572868
  12.6 21.6 %collective-permute-start.4 = (bf16[1024,256]{1,0:T(8,128)(2,1)S(1)}, bf16[1024,256]{1,0:T(8,128)(2,1)}, u32[]{:S(2)}, u32[]{:S(2)}) collective-permute-start(bf16[1024,256]{1,0:T(8,128)(2,1)S(1)} %fusion.40.refs_1_.refs_5_.refs_4_.refs_8_), channel_id=1, source_target_pairs={{0,4},{2,6},{4,0},{6,2},{8,12},{10,14},{12,8},{14,10},{16,20},{18,... | collective-permute-start | bytes 1572872 | tf_op jit(solution)/shard_map/ppermute | solution.py:30
  12.7 38.4 %collective-permute-start.3 = (bf16[1024,256]{1,0:T(8,128)(2,1)S(1)}, bf16[1024,256]{1,0:T(8,128)(2,1)}, u32[]{:S(2)}, u32[]{:S(2)}) collective-permute-start(bf16[1024,256]{1,0:T(8,128)(2,1)S(1)} %fusion.40.refs_1_.refs_5_.refs_4_.refs_8_), channel_id=1, source_target_pairs={{0,2},{2,0},{4,6},{6,4},{8,10},{10,8},{12,14},{14,12},{16,18},{18,... | collective-permute-start | bytes 1572872 | tf_op jit(solution)/shard_map/ppermute | solution.py:30
  15.6 55.0 %copy-start.16 = (bf16[1024,256]{1,0:T(8,128)(2,1)}, bf16[1024,256]{1,0:T(8,128)(2,1)S(1)}, u32[]{:S(2)}) copy-start(bf16[1024,256]{1,0:T(8,128)(2,1)S(1)} %fusion.39.refs_1_.refs_5_.refs_4_.refs_8_) | copy-start | bytes 1572868
  15.6 36.0 %collective-permute-start.7 = (bf16[1024,256]{1,0:T(8,128)(2,1)S(1)}, bf16[1024,256]{1,0:T(8,128)(2,1)S(1)}, u32[]{:S(2)}, u32[]{:S(2)}) collective-permute-start(bf16[1024,256]{1,0:T(8,128)(2,1)S(1)} %fusion.39.refs_1_.refs_5_.refs_4_.refs_8_), channel_id=1, source_target_pairs={{0,4},{2,6},{4,0},{6,2},{8,12},{10,14},{12,8},{14,10},{16,20},{18,... | collective-permute-start | bytes 1572872 | tf_op jit(solution)/shard_map/ppermute | solution.py:30
  22.4 75.2 %copy-start.15 = (bf16[1024,256]{1,0:T(8,128)(2,1)}, bf16[1024,256]{1,0:T(8,128)(2,1)S(1)}, u32[]{:S(2)}) copy-start(bf16[1024,256]{1,0:T(8,128)(2,1)S(1)} %fusion.38.refs_1_.refs_5_.refs_4_.refs_8_) | copy-start | bytes 1572868
  23.0 13.3 %collective-permute-start.2 = (bf16[1024,256]{1,0:T(8,128)(2,1)}, bf16[1024,256]{1,0:T(8,128)(2,1)}, u32[]{:S(2)}, u32[]{:S(2)}) collective-permute-start(bf16[1024,256]{1,0:T(8,128)(2,1)} %collective-permute-done.1.refs_3_.refs_7_.refs_6_.refs_10_), channel_id=1, source_target_pairs={{0,2},{2,0},{4,6},{6,4},{8,10},{10,8},{12,14},{14,12},{16,18},{18,... | collective-permute-start | bytes 1572872 | tf_op jit(solution)/shard_map/ppermute | solution.py:30
  33.3 64.3 %copy-start.31 = (bf16[1024,512]{1,0:T(8,128)(2,1)}, bf16[1024,512]{1,0:T(8,128)(2,1)S(1)}, u32[]{:S(2)}) copy-start(bf16[1024,512]{1,0:T(8,128)(2,1)S(1)} %add_convert_fusion.2.refs_0_) | copy-start | bytes 3145732
  33.3 35.3 %collective-permute-start.6 = (bf16[1024,256]{1,0:T(8,128)(2,1)S(1)}, bf16[1024,256]{1,0:T(8,128)(2,1)S(1)}, u32[]{:S(2)}, u32[]{:S(2)}) collective-permute-start(bf16[1024,256]{1,0:T(8,128)(2,1)S(1)} %fusion.39.refs_1_.refs_5_.refs_4_.refs_8_), channel_id=1, source_target_pairs={{0,2},{2,0},{4,6},{6,4},{8,10},{10,8},{12,14},{14,12},{16,18},{18,... | collective-permute-start | bytes 1572872 | tf_op jit(solution)/shard_map/ppermute | solution.py:30
  34.2 34.9 %collective-permute-start.13 = (bf16[1024,256]{1,0:T(8,128)(2,1)S(1)}, bf16[1024,256]{1,0:T(8,128)(2,1)S(1)}, u32[]{:S(2)}, u32[]{:S(2)}) collective-permute-start(bf16[1024,256]{1,0:T(8,128)(2,1)S(1)} %fusion.38.refs_1_.refs_5_.refs_4_.refs_8_), channel_id=1, source_target_pairs={{0,4},{2,6},{4,0},{6,2},{8,12},{10,14},{12,8},{14,10},{16,20},{18,... | collective-permute-start | bytes 1572872 | tf_op jit(solution)/shard_map/ppermute | solution.py:30
  36.2 17.0 %collective-permute-start.5 = (bf16[1024,256]{1,0:T(8,128)(2,1)}, bf16[1024,256]{1,0:T(8,128)(2,1)S(1)}, u32[]{:S(2)}, u32[]{:S(2)}) collective-permute-start(bf16[1024,256]{1,0:T(8,128)(2,1)} %collective-permute-done.4.refs_3_.refs_7_.refs_6_.refs_10_), channel_id=1, source_target_pairs={{0,2},{2,0},{4,6},{6,4},{8,10},{10,8},{12,14},{14,12},{16,18},{18,... | collective-permute-start | bytes 1572872 | tf_op jit(solution)/shard_map/ppermute | solution.py:30
  51.2 46.4 %collective-permute-start.12 = (bf16[1024,256]{1,0:T(8,128)(2,1)S(1)}, bf16[1024,256]{1,0:T(8,128)(2,1)S(1)}, u32[]{:S(2)}, u32[]{:S(2)}) collective-permute-start(bf16[1024,256]{1,0:T(8,128)(2,1)S(1)} %fusion.38.refs_1_.refs_5_.refs_4_.refs_8_), channel_id=1, source_target_pairs={{0,2},{2,0},{4,6},{6,4},{8,10},{10,8},{12,14},{14,12},{16,18},{18,... | collective-permute-start | bytes 1572872 | tf_op jit(solution)/shard_map/ppermute | solution.py:30
  51.6 32.7 %collective-permute-start.9 = (bf16[512,1024]{1,0:T(8,128)(2,1)S(1)}, bf16[512,1024]{1,0:T(8,128)(2,1)S(1)}, u32[]{:S(2)}, u32[]{:S(2)}) collective-permute-start(bf16[512,1024]{1,0:T(8,128)(2,1)S(1)} %copy-done.65), channel_id=1, source_target_pairs={{0,1},{1,0},{2,3},{3,2},{4,5},{5,4},{6,7},{7,6},{8,9},{9,8},{10,11... | collective-permute-start | bytes 3145736 | tf_op jit(solution)/shard_map/ppermute | solution.py:30
  53.2 17.4 %collective-permute-start.8 = (bf16[1024,256]{1,0:T(8,128)(2,1)S(1)}, bf16[1024,256]{1,0:T(8,128)(2,1)S(1)}, u32[]{:S(2)}, u32[]{:S(2)}) collective-permute-start(bf16[1024,256]{1,0:T(8,128)(2,1)S(1)} %collective-permute-done.7.refs_3_.refs_7_.refs_6_.refs_10_), channel_id=1, source_target_pairs={{0,2},{2,0},{4,6},{6,4},{8,10},{10,8},{12,14},{14,12},{16,18},{18,... | collective-permute-start | bytes 1572872 | tf_op jit(solution)/shard_map/ppermute | solution.py:30
  68.6 16.8 %collective-permute-start.10 = (bf16[1024,128]{1,0:T(8,128)(2,1)S(1)}, bf16[1024,128]{1,0:T(8,128)(2,1)S(1)}, u32[]{:S(2)}, u32[]{:S(2)}) collective-permute-start(bf16[1024,128]{1,0:T(8,128)(2,1)S(1)} %get-tuple-element.278.refs_1_), channel_id=1, source_target_pairs={{0,1},{1,0},{2,3},{3,2},{4,5},{5,4},{6,7},{7,6},{8,9},{9,8},{10,11... | collective-permute-start | bytes 786440 | tf_op jit(solution)/shard_map/ppermute | solution.py:30
  69.1 24.6 %collective-permute-start.11 = (bf16[1024,256]{1,0:T(8,128)(2,1)S(1)}, bf16[1024,256]{1,0:T(8,128)(2,1)S(1)}, u32[]{:S(2)}, u32[]{:S(2)}) collective-permute-start(bf16[1024,256]{1,0:T(8,128)(2,1)S(1)} %pad_maximum_fusion.7.refs_2_), channel_id=1, source_target_pairs={{0,1},{1,0},{2,3},{3,2},{4,5},{5,4},{6,7},{7,6},{8,9},{9,8},{10,11... | collective-permute-start | bytes 1572872 | tf_op jit(solution)/shard_map/ppermute | solution.py:30
  70.6 27.0 %collective-permute-start.14 = (bf16[1024,256]{1,0:T(8,128)(2,1)S(1)}, bf16[1024,256]{1,0:T(8,128)(2,1)S(1)}, u32[]{:S(2)}, u32[]{:S(2)}) collective-permute-start(bf16[1024,256]{1,0:T(8,128)(2,1)S(1)} %collective-permute-done.13.refs_3_.refs_7_.refs_6_.refs_10_), channel_id=1, source_target_pairs={{0,2},{2,0},{4,6},{6,4},{8,10},{10,8},{12,14},{14,12},{16,18},{18,... | collective-permute-start | bytes 1572872 | tf_op jit(solution)/shard_map/ppermute | solution.py:30
  94.0 19.1 %collective-permute-start.17 = (bf16[1024,128]{1,0:T(8,128)(2,1)S(1)}, bf16[1024,128]{1,0:T(8,128)(2,1)S(1)}, u32[]{:S(2)}, u32[]{:S(2)}) collective-permute-start(bf16[1024,128]{1,0:T(8,128)(2,1)S(1)} %get-tuple-element.257), channel_id=1, source_target_pairs={{0,1},{1,0},{2,3},{3,2},{4,5},{5,4},{6,7},{7,6},{8,9},{9,8},{10,11... | collective-permute-start | bytes 786440 | tf_op jit(solution)/shard_map/ppermute | solution.py:30
  95.6 17.3 %collective-permute-start.16 = (bf16[1024,128]{1,0:T(8,128)(2,1)S(1)}, bf16[1024,128]{1,0:T(8,128)(2,1)S(1)}, u32[]{:S(2)}, u32[]{:S(2)}) collective-permute-start(bf16[1024,128]{1,0:T(8,128)(2,1)S(1)} %get-tuple-element.259), channel_id=1, source_target_pairs={{0,1},{1,0},{2,3},{3,2},{4,5},{5,4},{6,7},{7,6},{8,9},{9,8},{10,11... | collective-permute-start | bytes 786440 | tf_op jit(solution)/shard_map/ppermute | solution.py:30
  96.1 16.7 %collective-permute-start.15 = (bf16[1024,128]{1,0:T(8,128)(2,1)S(1)}, bf16[1024,128]{1,0:T(8,128)(2,1)S(1)}, u32[]{:S(2)}, u32[]{:S(2)}) collective-permute-start(bf16[1024,128]{1,0:T(8,128)(2,1)S(1)} %get-tuple-element.261), channel_id=1, source_target_pairs={{0,1},{1,0},{2,3},{3,2},{4,5},{5,4},{6,7},{7,6},{8,9},{9,8},{10,11... | collective-permute-start | bytes 786440 | tf_op jit(solution)/shard_map/ppermute | solution.py:30
  111.6 6.6 %collective-permute-start.18 = (bf16[1024,128]{1,0:T(8,128)(2,1)S(1)}, bf16[1024,128]{1,0:T(8,128)(2,1)S(1)}, u32[]{:S(2)}, u32[]{:S(2)}) collective-permute-start(bf16[1024,128]{1,0:T(8,128)(2,1)S(1)} %get-tuple-element.255), channel_id=1, source_target_pairs={{0,1},{1,0},{2,3},{3,2},{4,5},{5,4},{6,7},{7,6},{8,9},{9,8},{10,11... | collective-permute-start | bytes 786440 | tf_op jit(solution)/shard_map/ppermute | solution.py:30
  131.8 26.1 %collective-permute-start.19 = (bf16[512,1024]{1,0:T(8,128)(2,1)S(1)}, bf16[512,1024]{1,0:T(8,128)(2,1)S(1)}, u32[]{:S(2)}, u32[]{:S(2)}) collective-permute-start(bf16[512,1024]{1,0:T(8,128)(2,1)S(1)} %convolution_convert_fusion.6), channel_id=1, source_target_pairs={{0,1},{1,0},{2,3},{3,2},{4,5},{5,4},{6,7},{7,6},{8,9},{9,8},{10,11... | collective-permute-start | bytes 3145736 | tf_op jit(solution)/shard_map/ppermute | solution.py:30
  134.8 45.6 %copy-start.39 = (f32[512,1024]{1,0:T(8,128)}, f32[512,1024]{1,0:T(8,128)S(1)}, u32[]{:S(2)}) copy-start(f32[512,1024]{1,0:T(8,128)S(1)} %get-tuple-element.332) | copy-start | bytes 6291460
  143.1 37.3 %collective-permute-start.20 = (bf16[512,1024]{1,0:T(8,128)(2,1)S(1)}, bf16[512,1024]{1,0:T(8,128)(2,1)S(1)}, u32[]{:S(2)}, u32[]{:S(2)}) collective-permute-start(bf16[512,1024]{1,0:T(8,128)(2,1)S(1)} %convolution_convert_fusion.5), channel_id=1, source_target_pairs={{0,1},{1,0},{2,3},{3,2},{4,5},{5,4},{6,7},{7,6},{8,9},{9,8},{10,11... | collective-permute-start | bytes 3145736 | tf_op jit(solution)/shard_map/ppermute | solution.py:30
  174.9 55.5 %collective-permute-start.21 = (bf16[512,1024]{1,0:T(8,128)(2,1)}, bf16[512,1024]{1,0:T(8,128)(2,1)}, u32[]{:S(2)}, u32[]{:S(2)}) collective-permute-start(bf16[512,1024]{1,0:T(8,128)(2,1)} %convolution_convert_fusion.4), channel_id=1, source_target_pairs={{0,1},{1,0},{2,3},{3,2},{4,5},{5,4},{6,7},{7,6},{8,9},{9,8},{10,11... | collective-permute-start | bytes 3145736 | tf_op jit(solution)/shard_map/ppermute | solution.py:30
  202.0 20.5 %collective-permute-start.22 = (bf16[512,2048]{1,0:T(8,128)(2,1)}, bf16[512,2048]{1,0:T(8,128)(2,1)}, u32[]{:S(2)}, u32[]{:S(2)}) collective-permute-start(bf16[512,2048]{1,0:T(8,128)(2,1)} %bitcast.9), channel_id=1, source_target_pairs={{0,2},{2,0},{4,6},{6,4},{8,10},{10,8},{12,14},{14,12},{16,18},{18,... | collective-permute-start | bytes 6291464 | tf_op jit(solution)/shard_map/ppermute | solution.py:30
  204.5 25.9 %collective-permute-start.23 = (bf16[512,1024]{1,0:T(8,128)(2,1)}, bf16[512,1024]{1,0:T(8,128)(2,1)}, u32[]{:S(2)}, u32[]{:S(2)}) collective-permute-start(bf16[512,1024]{1,0:T(8,128)(2,1)} %convolution_convert_fusion.3), channel_id=1, source_target_pairs={{0,1},{1,0},{2,3},{3,2},{4,5},{5,4},{6,7},{7,6},{8,9},{9,8},{10,11... | collective-permute-start | bytes 3145736 | tf_op jit(solution)/shard_map/ppermute | solution.py:30
  220.7 23.0 %collective-permute-start.24 = (bf16[512,2048]{1,0:T(8,128)(2,1)S(1)}, bf16[512,2048]{1,0:T(8,128)(2,1)S(1)}, u32[]{:S(2)}, u32[]{:S(2)}) collective-permute-start(bf16[512,2048]{1,0:T(8,128)(2,1)S(1)} %bitcast.289), channel_id=1, source_target_pairs={{0,2},{2,0},{4,6},{6,4},{8,10},{10,8},{12,14},{14,12},{16,18},{18,... | collective-permute-start | bytes 6291464 | tf_op jit(solution)/shard_map/ppermute | solution.py:30
  388.8 36.1 %copy-start.104 = (bf16[512,384]{1,0:T(8,128)(2,1)S(1)}, bf16[512,384]{1,0:T(8,128)(2,1)}, u32[]{:S(2)}) copy-start(bf16[512,384]{1,0:T(8,128)(2,1)} %get-tuple-element.150) | copy-start | bytes 1179652
  481.0 29.9 %collective-permute-start.25 = (bf16[1024,384]{1,0:T(8,128)(2,1)S(1)}, bf16[1024,384]{1,0:T(8,128)(2,1)S(1)}, u32[]{:S(2)}, u32[]{:S(2)}) collective-permute-start(bf16[1024,384]{1,0:T(8,128)(2,1)S(1)} %copy-done), channel_id=1, source_target_pairs={{0,1},{1,0},{2,3},{3,2},{4,5},{5,4},{6,7},{7,6},{8,9},{9,8},{10,11... | collective-permute-start | bytes 2359304 | tf_op jit(solution)/shard_map/ppermute | solution.py:30
  (129 other events, 865.6 us)

commit v4 on v3

--- a/solution.py
+++ b/solution.py
@@ -60,41 +60,19 @@
     )
 
 
-def exchange_kernel(links, *refs):
-    count = len(links)
-    semaphores = refs[-1]
-    greet(sorted(set(links)))
-    copies = [
-        send(refs[i], refs[count + i], semaphores, i, *links[i]) for i in range(count)
-    ]
-    for copy in copies:
-        copy.start()
-    for copy in copies:
-        copy.wait()
-
-
-def exchange(cargo, collective_id):
-    links = [link for _, link in cargo]
-    values = [value for value, _ in cargo]
-    anywhere = pl.BlockSpec(memory_space=pl.ANY)
-    return pl.pallas_call(
-        functools.partial(exchange_kernel, links),
-        in_specs=[anywhere] * len(values),
-        out_specs=[anywhere] * len(values),
-        out_shape=[jax.ShapeDtypeStruct(v.shape, v.dtype) for v in values],
-        scratch_shapes=[pltpu.SemaphoreType.DMA((2, len(values)))],
-        compiler_params=pltpu.CompilerParams(
-            collective_id=collective_id, has_side_effects=True
-        ),
-        cost_estimate=pl.CostEstimate(
-            flops=0, bytes_accessed=16 << 20, transcendentals=0
-        ),
-        name="exchange",
-    )(*values)
-
-
 def after(value, *earlier):
     return lax.optimization_barrier((value, earlier))[0]
+
+
+def sides(value, bit, left):
+    view = value.reshape(1 << left.index(bit), 2, -1, value.shape[-1])
+    own = lax.axis_index("dp") >> bit & 1
+    return [
+        lax.dynamic_index_in_dim(view, side, 1, keepdims=False).reshape(
+            -1, view.shape[-1]
+        )
+        for side in (own, 1 - own)
+    ]
 
 
 class Scatter:
@@ -115,24 +93,23 @@
         if not self.order:
             return
         bit = self.order.pop(0)
-        high = 1 << self.left.index(bit)
+        if ready is None:
+            ready = sides(self.whole, bit, self.left)
         self.left.remove(bit)
-        if ready is None:
-            view = self.whole.reshape(high, 2, -1, self.whole.shape[-1])
-            own = lax.axis_index("dp") >> bit & 1
-            ready = [
-                lax.dynamic_index_in_dim(view, side, 1, keepdims=False).reshape(
-                    -1, view.shape[-1]
-                )
-                for side in (own, 1 - own)
-            ]
         self.keep = ready[0]
         self.cargo = (ready[1].astype(self.wire), ("dp", bit))
 
+    def gather(self, arrived):
+        self.whole = self.keep.astype(F32) + arrived.astype(F32)
+        return self.whole
+
     def land(self, arrived):
-        self.whole = self.keep.astype(F32) + arrived.astype(F32)
-        self.split()
-        return self.whole
+        if not self.order:
+            self.cargo = None
+            return self.gather(arrived)
+        bit = self.order[0]
+        kept, sent = sides(self.keep, bit, self.left), sides(arrived, bit, self.left)
+        self.split([a.astype(F32) + b.astype(F32) for a, b in zip(kept, sent)])
 
     def fly(self):
         value, (axis, bit) = self.cargo
@@ -143,12 +120,13 @@
 
 
 class Columns(Scatter):
-    def __init__(self, other, cols):
+    def __init__(self, other, cols, far_first=False):
         self.part, self.wire = other.part, other.wire
         self.left, self.order = list(other.left), list(other.order)
-        link = other.cargo[1]
-        self.keep = other.keep[:, cols]
-        self.cargo = (other.cargo[0][:, cols], link)
+        if far_first and len(self.order) > 1:
+            self.order = self.order[1:] + self.order[:1]
+        self.whole = other.whole[:, cols]
+        self.split()
 
 
 class Ready(Scatter):
@@ -271,24 +249,33 @@
     landing_refs, refs = refs[4 : 4 + count], refs[4 + count :]
     qt_ref, gt_ref, dqt_ref, k_ref, v_ref, d_ref = refs[:6]
     diagonal_ref, cross_ref, beside_ref = refs[6:9]
-    diagonal_in, cross_in, beside_in, product_ref, semaphores = refs[9:]
+    diagonal_in, cross_in, beside_in, product_ref, turned_ref, semaphores, local = refs[9:]
+    turned_copy = pltpu.make_async_copy(tokens_ref, turned_ref, local.at[0])
     step = pl.program_id(0)
     rows = q_ref.shape[0]
-    span = k_ref.shape[0]
     own_links = [("dp", 0), ("dp", 1)]
     copies = [
         send(cargo_refs[i], landing_refs[i], semaphores, i, *links[i])
         for i in range(count)
     ]
-    diagonal_copy = send(diagonal_ref, diagonal_in, semaphores, count, "dp", 0)
-    cross_copy = send(cross_ref, cross_in, semaphores, count + 1, "dp", 1)
-    beside_copy = send(beside_ref, beside_in, semaphores, count + 2, "dp", 0)
+    halves = [slice(half * tile, (half + 1) * tile) for half in range(2)]
+
+    def part_copies(source, target, first, bit):
+        return [
+            send(source.at[rows], target.at[rows], semaphores, count + first + i, "dp", bit)
+            for i, rows in enumerate(halves)
+        ]
+
+    diagonal_copies = part_copies(diagonal_ref, diagonal_in, 0, 0)
+    cross_copies = part_copies(cross_ref, cross_in, 2, 1)
+    beside_copies = part_copies(beside_ref, beside_in, 4, 0)
 
     @pl.when(step == 0)
     def _():
         greet(sorted(set(own_links + links)))
         for copy in copies:
             copy.start()
+        turned_copy.start()
         q = q_ref[...] * scale
         g = g_ref[...]
         products = jnp.transpose(g.astype(F32) * o_ref[...])
@@ -312,84 +299,82 @@
                 ).astype(BF16)
         dqt_ref[...] = jnp.zeros_like(dqt_ref)
 
-    @pl.when(step == 1)
-    def _():
-        diagonal_copy.start()
-
-    @pl.when(step == 2)
-    def _():
-        cross_copy.start()
-
-    @pl.when(step == 3)
-    def _():
-        beside_copy.start()
+    for first, later in ((1, diagonal_copies), (3, cross_copies), (5, beside_copies)):
+        for half in range(2):
+
+            @pl.when(step == first + half)
+            def _():
+                later[half].start()
 
     for source in range(SOURCES):
-
-        @pl.when(step == SOURCES - 1 - source)
+        for half in range(2):
+
+            @pl.when(step == 2 * (SOURCES - 1 - source) + half)
+            def _():
+                k_ref[...] = k_refs[source][halves[half], :]
+                v_ref[...] = v_refs[source][halves[half], :]
+
+    k = k_ref[...]
+    v = v_ref[...]
+    one = jnp.ones_like(k)
+    k_wide = jnp.concatenate([k, one], 1)
+    v_wide = jnp.concatenate([v, one], 1)
+    kt = jnp.transpose(k)
+    parts = []
+    for head in range(2):
+        probs = jnp.exp(dot(k_wide, qt_ref[head], NN))
+        centred = dot(v_wide, gt_ref[head], NN)
+        score_grad = (probs * centred).astype(BF16)
+        parts.append(
+            (
+                dot(score_grad, q_ref[...], NN),
+                dot(probs.astype(BF16), g_ref[...], NN),
+            )
+        )
+        dqt_ref[head * HALF : (head + 1) * HALF, :] += dot(
+            kt[head * HALF : (head + 1) * HALF, :], score_grad, NN
+        )
+    first = head_lanes(k.shape, 0)
+    d_ref[:, :LANES] = (jnp.where(first, parts[0][0], parts[1][0]) * scale).astype(BF16)
+    d_ref[:, LANES:] = jnp.where(first, parts[0][1], parts[1][1]).astype(BF16)
+
+    for half in range(2):
+        band = halves[half]
+
+        @pl.when(step == half)
         def _():
-            k_ref[...] = k_refs[source][...]
-            v_ref[...] = v_refs[source][...]
-
-    for start in range(0, span, tile):
-        k = k_ref[start : start + tile, :]
-        v = v_ref[start : start + tile, :]
-        one = jnp.ones_like(k)
-        k_wide = jnp.concatenate([k, one], 1)
-        v_wide = jnp.concatenate([v, one], 1)
-        kt = jnp.transpose(k)
-        parts = []
-        for head in range(2):
-            probs = jnp.exp(dot(k_wide, qt_ref[head], NN))
-            centred = dot(v_wide, gt_ref[head], NN)
-            score_grad = (probs * centred).astype(BF16)
-            parts.append(
-                (
-                    dot(score_grad, q_ref[...], NN),
-                    dot(probs.astype(BF16), g_ref[...], NN),
-                )
-            )
-            dqt_ref[head * HALF : (head + 1) * HALF, :] += dot(
-                kt[head * HALF : (head + 1) * HALF, :], score_grad, NN
-            )
-        first = head_lanes(k.shape, 0)
-        d_ref[start : start + tile, :LANES] = (
-            jnp.where(first, parts[0][0], parts[1][0]) * scale
-        ).astype(BF16)
-        d_ref[start : start + tile, LANES:] = jnp.where(
-            first, parts[0][1], parts[1][1]
-        ).astype(BF16)
-
-    @pl.when(step == 0)
-    def _():
-        diagonal_ref[...] = d_ref[...]
-
-    @pl.when(step == 1)
-    def _():
-        diagonal_copy.wait()
-        cross_ref[...] = (
-            d_ref[...].astype(F32) + diagonal_in[...].astype(F32)
-        ).astype(BF16)
-
-    @pl.when(step == 2)
-    def _():
-        beside_ref[...] = d_ref[...]
-
-    @pl.when(step == 3)
+            diagonal_ref[band, :] = d_ref[...]
+
+        @pl.when(step == 2 + half)
+        def _():
+            diagonal_copies[half].wait()
+            cross_ref[band, :] = (
+                d_ref[...].astype(F32) + diagonal_in[band, :].astype(F32)
+            ).astype(BF16)
+
+        @pl.when(step == 4 + half)
+        def _():
+            beside_ref[band, :] = d_ref[...]
+
+        @pl.when(step == 6 + half)
+        def _():
+            beside_copies[half].wait()
+            cross_copies[half].wait()
+            joined_ref[band, LANES:] = (
+                d_ref[...].astype(F32)
+                + beside_in[band, :].astype(F32)
+                + cross_in[band, :].astype(F32)
+            ).astype(BF16)
+
+    @pl.when(step == 7)
     def _():
         joined_ref[:, :LANES] = (jnp.transpose(dqt_ref[...]) * scale).astype(BF16)
-        beside_copy.wait()
-        cross_copy.wait()
-        joined_ref[:, LANES:] = (
-            d_ref[...].astype(F32)
-            + beside_in[...].astype(F32)
-            + cross_in[...].astype(F32)
-        ).astype(BF16)
         joined = joined_ref[...]
         sums_ref[...] = jnp.sum(joined.astype(F32), axis=0, keepdims=True)
+        turned_copy.wait()
         pairs, _, part, _ = product_ref.shape
         for pair in range(0, pairs, 2):
-            band = tokens_ref[2 * pair * part : 2 * (pair + 2) * part, :]
+            band = turned_ref[2 * pair * part : 2 * (pair + 2) * part, :]
             product_ref[pair : pair + 2] = (
                 dot(band, joined, NN).astype(BF16).reshape(2, 2, part, 3 * LANES)
             )
@@ -413,7 +398,7 @@
     anywhere = pl.BlockSpec(memory_space=pl.ANY)
     return pl.pallas_call(
         functools.partial(backward_kernel, scale, span // 2, links),
-        grid=(SOURCES,),
+        grid=(2 * SOURCES,),
         in_specs=[
             pl.BlockSpec((rows, LANES), lambda i: (0, group)),
             pl.BlockSpec((rows, LANES), lambda i: (0, group)),
@@ -422,8 +407,7 @@
         ]
         + [pl.BlockSpec((span, LANES), whole)] * SOURCES
         + [pl.BlockSpec((span, LANES), lambda i: (0, 1))] * SOURCES
-        + [pl.BlockSpec(tokens.shape, whole)]
-        + [anywhere] * len(values),
+        + [anywhere] * (1 + len(values)),
         out_specs=[
             pl.BlockSpec((rows, 3 * LANES), whole),
             pl.BlockSpec((1, 3 * LANES), whole),
@@ -442,12 +426,14 @@
             pltpu.VMEM((2, 2 * LANES, rows), BF16),
             pltpu.VMEM((2, 2 * LANES, rows), BF16),
             pltpu.VMEM((LANES, rows), F32),
-            pltpu.VMEM((span, LANES), BF16),
-            pltpu.VMEM((span, LANES), BF16),
+            pltpu.VMEM((span // 2, LANES), BF16),
+            pltpu.VMEM((span // 2, LANES), BF16),
+            pltpu.VMEM((span // 2, 2 * LANES), BF16),
         ]
-        + [pltpu.VMEM((span, 2 * LANES), BF16)] * 7
+        + [pltpu.VMEM((span, 2 * LANES), BF16)] * 6
         + [pltpu.VMEM((size // 2, 2, width // size, 3 * LANES), BF16)]
-        + [pltpu.SemaphoreType.DMA((2, len(values) + 3))],
+        + [pltpu.VMEM(tokens.shape, BF16)]
+        + [pltpu.SemaphoreType.DMA((2, len(values) + 6)), pltpu.SemaphoreType.DMA((1,))],
         compiler_params=pltpu.CompilerParams(
             vmem_limit_bytes=60 << 20,
             collective_id=collective_id,
@@ -462,49 +448,189 @@
     )(queries, grads, context, lse, *blocks, *blocks, tokens, *values)
 
 
-def merge_kernel(count, *refs):
-    sides = []
-    for base in (0, 3 * count):
-        total = None
-        for group in range(count):
-            rows = refs[base + group]
-            first, second = refs[base + count + 2 * group : base + count + 2 * group + 2]
-            for value in (
-                dot(rows[:, :LANES], first[...], NT),
-                dot(rows[:, LANES:], second[...], NT),
-            ):
-                total = value if total is None else total + value
-        sides.append(total)
-    result = sides[0] + sides[1]
-    for ref in refs[6 * count : -1]:
-        result = result + ref[...]
-    refs[-1][...] = result
-
-
-def merge(own, own_weights, other, other_weights, *extra):
-    count = len(own)
-    rows, width = own[0].shape[0], own_weights[0].shape[0]
-    tile = rows // 4
-    row_spec = pl.BlockSpec((tile, 3 * LANES), lambda i: (i, 0))
-    sum_spec = pl.BlockSpec((tile, width), lambda i: (i, 0))
-    weight_specs = [
-        pl.BlockSpec((width, LANES), lambda i: (0, 0)),
-        pl.BlockSpec((width, 2 * LANES), lambda i: (0, 0)),
-    ] * count
+def tail_kernel(plans, widths, *refs):
+    chains = len(plans)
+    groups = len(widths)
+    pieces = sum(len(part) for part in widths)
+    last = groups - 1
+    last_piece = widths[last][-1]
+    wide = 3 * LANES
+
+    def take(number):
+        nonlocal refs
+        taken, refs = refs[:number], refs[number:]
+        return taken
+
+    joined_refs, other_refs = take(groups), take(last)
+    own_weights, other_weights, base_refs = take(pieces), take(pieces - 1), take(CHUNKS)
+    keep_refs, cargo_refs = take(chains), take(chains)
+    total_ref = take(1)[0]
+    result_refs = take(chains)
+    rows_refs, weight_refs, last_rows, last_weights = take(2), take(2), take(2), take(2)
+    base_ref = take(1)[0]
+    hops = [[take(3) for _ in plan] for plan in plans]
+    semaphores, local = refs
+    links = sorted({("dp", bit) for plan in plans for bit, _, _ in plan} | {("tensor", 0)})
+    greet(links)
+    last_copy = send(joined_refs[last], last_rows[1], semaphores, 0, "tensor", 0)
+    last_copy.start()
+    weight_copy = send(
+        own_weights[pieces - 1],
+        last_weights[1].at[:, wide - last_piece :],
+        semaphores,
+        1,
+        "tensor",
+        0,
+    )
+    weight_copy.start()
+    count = 2
+    flights = []
+    for chain, plan in enumerate(plans):
+        flights.append([])
+        for level, (bit, _, _) in enumerate(plan):
+            land, out, _ = hops[chain][level]
+            source = cargo_refs[chain] if level == 0 else out
+            flights[chain].append(send(source, land, semaphores, count, "dp", bit))
+            count += 1
+        flights[chain][0].start()
+    loads = []
+
+    def load(source, target):
+        copy = pltpu.make_async_copy(source, target, local.at[len(loads)])
+        copy.start()
+        loads.append(copy)
+
+    for group in range(last):
+        cols = slice(group * wide, (group + 1) * wide)
+        load(joined_refs[group], rows_refs[0].at[:, cols])
+        load(other_refs[group], rows_refs[1].at[:, cols])
+    for side, parts in enumerate((list(own_weights), list(other_weights))):
+        for group in range(groups):
+            target = last_weights[side] if group == last else weight_refs[side]
+            base = 0 if group == last else group * wide
+            for piece in widths[group]:
+                if not parts:
+                    continue
+                load(parts.pop(0), target.at[:, base : base + piece])
+                base += piece
+    load(joined_refs[last], last_rows[0])
+    for part in range(CHUNKS):
+        height = base_refs[part].shape[0]
+        load(base_refs[part], base_ref.at[part * height : (part + 1) * height, :])
+
+    def advance(level):
+        for chain, plan in enumerate(plans):
+            if level >= len(plan):
+                continue
+            flights[chain][level].wait()
+            land = hops[chain][level][0]
+            keep = keep_refs[chain] if level == 0 else None
+            if level == 0:
+                held = keep[...].astype(F32)
+            else:
+                bit, high, low = plan[level]
+                own = lax.axis_index("dp") // (1 << bit) % 2
+                held = hops[chain][level][2][:, own].reshape(land.shape)
+            whole = held + land[...].astype(F32)
+            if level == len(plan) - 1:
+                result_refs[chain][...] = whole
+                continue
+            bit, high, low = plan[level + 1]
+            _, out, split = hops[chain][level + 1]
+            own = lax.axis_index("dp") // (1 << bit) % 2
+            split[...] = whole.reshape(split.shape)
+            out[...] = split[:, 1 - own].reshape(out.shape).astype(out.dtype)
+        for flight in flights:
+            if level + 1 < len(flight):
+                flight[level + 1].start()
+
+    for copy in loads:
+        copy.wait()
+    tile = total_ref.shape[0] // 4
+
+    def early(index, carry):
+        band = pl.ds(pl.multiple_of(index * tile, tile), tile)
+        total_ref[band, :] = dot(rows_refs[0][band, :], weight_refs[0][...], NT) + dot(
+            rows_refs[1][band, :], weight_refs[1][...], NT
+        )
+        return carry
+
+    def late(index, carry):
+        band = pl.ds(pl.multiple_of(index * tile, tile), tile)
+        last_part = dot(last_rows[0][band, :], last_weights[0][...], NT) + dot(
+            last_rows[1][band, :], last_weights[1][...], NT
+        )
+        total_ref[band, :] = base_ref[band, :] + (total_ref[band, :] + last_part)
+        return carry
+
+    depth = max(len(plan) for plan in plans)
+    lax.fori_loop(0, 2, early, 0)
+    advance(0)
+    lax.fori_loop(2, 4, early, 0)
+    for level in range(1, depth - 1):
+        advance(level)
+    last_copy.wait()
+    weight_copy.wait()
+    lax.fori_loop(0, 4, late, 0)
+    advance(depth - 1)
+
+
+def tail(joined, others, own_weights, other_weights, base, chains, collective_id):
+    groups = len(joined)
+    rows, wide = joined[0].shape
+    width = own_weights[0][0].shape[0]
+    widths = [[piece.shape[1] for piece in part] for part in own_weights]
+    own_weights = [piece for part in own_weights for piece in part]
+    other_weights = [piece for part in other_weights for piece in part]
+    size = lax.axis_size("dp")
+    plans, scratch, results = [], [], []
+    for chain in chains:
+        left = list(chain.left)
+        high_bits = sorted(left + [chain.cargo[1][1]], reverse=True)
+        count, part, cols = chain.keep.shape[0], chain.part, chain.keep.shape[1]
+        plan = []
+        for bit in [chain.cargo[1][1]] + chain.order:
+            high = 1 << high_bits.index(bit)
+            high_bits.remove(bit)
+            held = part << len(high_bits)
+            low = held // high
+            plan.append((bit, high, low))
+            scratch += [
+                pltpu.VMEM((held, cols), chain.wire),
+                pltpu.VMEM((held, cols), chain.wire),
+                pltpu.VMEM((high, 2, low, cols), F32),
+            ]
+        plans.append(plan)
+        results.append(jax.ShapeDtypeStruct((part, cols), F32))
+    anywhere = pl.BlockSpec(memory_space=pl.ANY)
+    inside = pl.BlockSpec(memory_space=pltpu.VMEM)
+    values = [*joined, *others, *own_weights, *other_weights, *base]
+    loads = 2 * (groups - 1) + 2 * len(own_weights) + CHUNKS
+    hops = sum(len(plan) for plan in plans)
     return pl.pallas_call(
-        functools.partial(merge_kernel, count),
-        grid=(rows // tile,),
-        in_specs=([row_spec] * count + weight_specs) * 2 + [sum_spec] * len(extra),
-        out_specs=sum_spec,
-        out_shape=jax.ShapeDtypeStruct((rows, width), F32),
-        compiler_params=pltpu.CompilerParams(vmem_limit_bytes=48 << 20),
+        functools.partial(tail_kernel, plans, widths),
+        in_specs=[anywhere] * len(values)
+        + [inside] * len(chains)
+        + [anywhere] * len(chains),
+        out_specs=[inside] * (1 + len(chains)),
+        out_shape=[jax.ShapeDtypeStruct((rows, width), F32)] + results,
+        scratch_shapes=[pltpu.VMEM((rows, (groups - 1) * wide), BF16)] * 2
+        + [pltpu.VMEM((width, (groups - 1) * wide), BF16)] * 2
+        + [pltpu.VMEM((rows, wide), BF16)] * 2
+        + [pltpu.VMEM((width, wide), BF16)] * 2
+        + [pltpu.VMEM((rows, width), F32)]
+        + scratch
+        + [pltpu.SemaphoreType.DMA((2, hops + 2)), pltpu.SemaphoreType.DMA((loads,))],
+        compiler_params=pltpu.CompilerParams(
+            vmem_limit_bytes=60 << 20, collective_id=collective_id, has_side_effects=True
+        ),
         cost_estimate=pl.CostEstimate(
-            flops=12 * count * rows * width * LANES,
-            bytes_accessed=8 * rows * width,
+            flops=12 * groups * rows * width * LANES,
+            bytes_accessed=32 << 20,
             transcendentals=0,
         ),
-        name="merge",
-    )(*own, *own_weights, *other, *other_weights, *extra)
+        name="tail",
+    )(*values, *[c.keep for c in chains], *[c.cargo[0] for c in chains])
 
 
 def body(
@@ -547,21 +673,30 @@
     for group in range(groups):
         cols = slice(group * LANES, (group + 1) * LANES)
         weight = jnp.concatenate([key_weight[:, cols], value_weight[:, cols]], axis=1)
-        weights.append((query_weight[:, cols], weight))
+        pieces = [query_weight[:, cols], weight]
+        if group > 0:
+            pieces[1:] = [key_weight[:, cols], value_weight[:, cols]]
+        weights.append(pieces)
         shift = jnp.concatenate([jnp.zeros((LANES,), F32), value_shift[cols]])
         own_blocks.append((dot(tokens, weight, NN) + shift).astype(BF16))
     for own in own_blocks:
         across = flip(own, "dp", 1)
         blocks.append((own, flip(own, "dp", 0), across, flip(across, "dp", 0)))
     queries = (dot(tokens, query_weight, NN) + query_bias.reshape(local)).astype(BF16)
-    out_whole = in_order(out_weight, flip(out_weight, "tensor", 0), 0)
+    out_other = flip(out_weight, "tensor", 0)
+    out_whole = in_order(out_weight, out_other, 0)
 
     outs, own_context, other_context = [], [], []
     across = ("tensor", 0)
-    last_weights = [flip(part, "tensor", 0) for part in weights[-1]]
+    ahead = jnp.concatenate([weights[1][2], *weights[3][:2]], axis=1)
+    ahead = flip(ahead, "tensor", 0)
     for group in range(groups):
+        if group > 0:
+            queries = after(queries, outs[-1][1])
+        if group == groups - 2:
+            queries = after(queries, out_other)
         if group == groups - 1:
-            queries = after(queries, out_whole, *last_weights)
+            queries = after(queries, ahead)
         out, lse = attend(queries, group, blocks[group], scale)
         outs.append((out, lse))
         own_context.append(out.astype(BF16))
@@ -625,11 +760,11 @@
     upbias_grad = jnp.sum(hidden_low.astype(F32), axis=0)
     secondgain_grad = sum(grads[1] for grads in second_grads)
     secondshift_grad = sum(grads[2] for grads in second_grads)
-    done = down_scatter.land(after(down_flight, up_rows))
+    done = down_scatter.gather(after(down_flight, up_rows))
     middle = down_rows.shape[1] // 2
     down_parts = [
         Columns(down_scatter, slice(None, middle)),
-        Columns(down_scatter, slice(middle, None)),
+        Columns(down_scatter, slice(middle, None), True),
     ]
 
     attention_backs, firstgain_parts, firstshift_parts = [], [], []
@@ -678,13 +813,9 @@
     early_scatter = Scatter(jnp.concatenate([part for part, _ in early], axis=1), F32)
 
     tokens_turned = tokens.T
-    trips = [[] for _ in range(groups)]
-    for group in range(groups - 1):
-        query_trip = group if group == 0 else min(group, groups - 1)
-        pair_trip = max(0, group - 1) if group < groups - 2 else groups - 1
-        trips[query_trip].append((group, 0))
-        trips[pair_trip].append((group, 1))
-    other_weights = [[None, None] for _ in range(groups - 1)] + [last_weights]
+    trips = [[(0, 0), (0, 1), (2, 0), (1, 1)], [(1, 0)], [(2, 1)], [(2, 2)]]
+    ahead = [ahead[:, i * LANES : (i + 1) * LANES] for i in range(3)]
+    other_weights = [[None] * 2, [None, None, ahead[0]], [None] * 3, ahead[1:]]
     joined, others, sums, proj_scatters = [], [], [], []
     active = [up_scatter, out_scatter, early_scatter, down_parts[0]]
     for group in range(groups):
@@ -715,36 +846,21 @@
         sums.append(row_sums.reshape(3, LANES))
         proj_scatters.append(Ready(keep, outgoing, group < groups - 1))
         active.append(proj_scatters[-1])
-        if group == 0:
+        if group == 1:
             active.append(down_parts[1])
         active = [scatter for scatter in active if scatter.cargo is not None]
     sums = jnp.stack(sums, axis=1).reshape(3, local)
     late = [(by_dp(sums[0], heads), heads), (by_dp(sums[2], heads), heads)]
-    late_scatter = Scatter(jnp.concatenate([part for part, _ in late], axis=1), F32)
+    late_rows = jnp.concatenate([part for part, _ in late], axis=1)
+    late_rows = jnp.pad(late_rows[:, None, :], ((0, 0), (0, 7), (0, 0)))
+    late_scatter = Scatter(late_rows.reshape(8 * size, -1), F32)
     active.append(late_scatter)
-    others.append(flip(joined[-1], "tensor", 0))
-
-    def spread(parts):
-        return [piece for pair in parts for piece in pair]
-
-    partial = merge(
-        joined[:-1], spread(weights[:-1]), others[:-1], spread(other_weights[:-1])
+
+    tokens_grad, *ends = tail(
+        joined, others, weights, other_weights, attention_backs, active, groups
     )
-    stage = groups
-    while active:
-        arrived = exchange([scatter.cargo for scatter in active], stage)
-        stage += 1
-        for scatter, value in zip(active, arrived):
-            scatter.land(value)
-        active = [scatter for scatter in active if scatter.cargo is not None]
-    tokens_grad = merge(
-        joined[-1:],
-        spread(weights[-1:]),
-        others[-1:],
-        spread(other_weights[-1:]),
-        partial,
-        attention_back,
-    )
+    for scatter, value in zip(active, ends):
+        scatter.whole = value
     outweight_grad = out_scatter.result()
     upweight_grad = up_scatter.result()
     downweight_grad = jnp.concatenate([part.result() for part in down_parts], axis=1)

time: 523 us -> 468 us (0.89)
  local copies, waits for them, and re-layouts: 88.1 us -> 56.5 us
  Pallas kernels: 239 us -> 215 us
  starting transfers between devices: 24 us -> 17.4 us
  waiting for transfers between devices: 35.6 us -> 41.6 us
    convert_element_type x23 -> x2, local copies, waits for them, and re-layouts: 17.5 us -> 1.77 us  [split(): self.cargo = (ready[1].astype(self.wire), ('dp', bit))]
    unnamed x284 -> x215, local copies, waits for them, and re-layouts: 38 us -> 24.7 us
    pallas_call x6 -> x1, Pallas kernels: 44.3 us -> 32.1 us  [tail(): pl.pallas_call(functools.partial(tail_kernel, plans, widths), in_specs=[a...]
    pallas_call x4, Pallas kernels: 139 us -> 128 us  [attend_back(): pl.pallas_call(functools.partial(backward_kernel, scale, span // 2, links...]
    dynamic_slice x21 -> x7, local copies, waits for them, and re-layouts: 15.8 us -> 6.15 us  [sides(): lax.dynamic_index_in_dim(view, side, 1, keepdims=False)]
    convert_element_type x0 -> x7, other arithmetic: none -> 6.92 us  [split(): self.cargo = (ready[1].astype(self.wire), ('dp', bit))]
    ppermute x26 -> x24, starting transfers between devices: 24 us -> 17.4 us  [flip(): return lax.ppermute(value, axis, pairs)]
    ppermute x26 -> x24, waiting for transfers between devices: 35.6 us -> 41.6 us  [flip(): return lax.ppermute(value, axis, pairs)]
  transfers between devices with their start and end apart: 26 -> 24, of which waited for: 8 -> 8; matrix products, arithmetic and copies ran while one was open for 21% -> 23% of each run, Pallas kernels for 13% -> 12%
where the time goes in v4:
time: 468 us; the launch traced here: 464 us
  Pallas kernels  215 us (46%)
  other arithmetic  70.5 us (15%)
  matrix products  61 us (13%)
  local copies, waits for them, and re-layouts  56.5 us (12%)
  waiting for transfers between devices  41.6 us (9%)
  starting transfers between devices  17.4 us (4%)
    pallas_call x4, Pallas kernels, attend_back(): pl.pallas_call(functools.partial(backward_kernel, scale, span // 2, links...  128 us
    dot_general x19, matrix products, dot(): return lax.dot_general(left, right, dims, preferred_element_type=F32)  61 us
    pallas_call x4, Pallas kernels, attend(): pl.pallas_call(functools.partial(forward_kernel, scale, span // 2), grid=...  54.9 us
    ppermute x24, waiting for transfers between devices, flip(): return lax.ppermute(value, axis, pairs)  41.6 us
    pallas_call x1, Pallas kernels, tail(): pl.pallas_call(functools.partial(tail_kernel, plans, widths), in_specs=[a...  32.1 us
    unnamed x215, local copies, waits for them, and re-layouts  24.7 us
    add x14, other arithmetic, land(): self.split([a.astype(F32) + b.astype(F32) for a, b in zip(kept, sent)])  18.4 us
    ppermute x24, starting transfers between devices, flip(): return lax.ppermute(value, axis, pairs)  17.4 us
  transfers between devices with their start and end apart: 24, of which 8 were waited for; matrix products, arithmetic and copies ran while one was open for 23% of the time, Pallas kernels for 12%

profile of v4, /device:TPU:0, one launch (start us, length us, event | category | flops | bytes accessed | tf_op | source)
XLA Modules:
  0.0 463.9 jit_solution(7247907936467951078)
XLA Ops:
  1.6 3.0 slice_bitcast_fusion.2
  7.2 3.0 collective-permute-start.4
  19.6 4.2 copy.102
  25.8 3.2 add_convert_fusion.3.refs_0_
  29.1 4.3 collective-permute-done.1.refs_3_.refs_7_.refs_6_.refs_10_
  42.5 14.1 %attend.4 = (f32[1024,128]{1,0:T(8,128)S(1)}, f32[2,1024]{1,0:T(2,128)S(1)}) custom-call(bf16[1024,512]{1,0:T(8,128)(2,1)S(1)} %add_convert_fusion.3.refs_0_, bf16[1024,256]{1,0:T(8,128)(2,1)S(1)} %fusion.41.refs_1_.refs_5_.refs_4_.refs_8_, bf16[1024,256]{1,0:T(8,128)(2,1)} %collective-permute-done.refs_2_.refs_6_.refs_5_.refs_9_, ...), custom_call_target="tpu_custom_call" | custom-call | flops 8589934592 | bytes 3145728 | tf_op jit(solution)/shard_map/attend/pallas_call | solution.py:205
  57.2 6.6 %collective-permute-done.12.refs_3_.refs_7_.refs_6_.refs_10_ = bf16[1024,256]{1,0:T(8,128)(2,1)S(1)} collective-permute-done((bf16[1024,256]{1,0:T(8,128)(2,1)S(1)}, bf16[1024,256]{1,0:T(8,128)(2,1)S(1)}, u32[]{:S(2)}, u32[]{:S(2)}) %collective-permute-start.12) | collective-permute-done | bytes 524320 | tf_op jit(solution)/shard_map/ppermute | solution.py:30
  64.3 13.5 %attend.5 = (f32[1024,128]{1,0:T(8,128)S(1)}, f32[2,1024]{1,0:T(2,128)S(1)}) custom-call(bf16[1024,512]{1,0:T(8,128)(2,1)S(1)} %add_convert_fusion.3.refs_0_, bf16[1024,256]{1,0:T(8,128)(2,1)S(1)} %fusion.40.refs_1_.refs_5_.refs_4_.refs_8_, bf16[1024,256]{1,0:T(8,128)(2,1)S(1)} %collective-permute-done.3.refs_2_.refs_6_.refs_5_.refs_9_, ...), custom_call_target="tpu_custom_call" | custom-call | flops 8589934592 | bytes 3145728 | tf_op jit(solution)/shard_map/attend/pallas_call | solution.py:205
  78.5 13.8 %attend.6 = (f32[1024,128]{1,0:T(8,128)S(1)}, f32[2,1024]{1,0:T(2,128)S(1)}) custom-call(bf16[1024,512]{1,0:T(8,128)(2,1)S(1)} %add_convert_fusion.3.refs_0_, bf16[1024,256]{1,0:T(8,128)(2,1)S(1)} %fusion.39.refs_1_.refs_5_.refs_4_.refs_8_, bf16[1024,256]{1,0:T(8,128)(2,1)S(1)} %collective-permute-done.7.refs_2_.refs_6_.refs_5_.refs_9_, ...), custom_call_target="tpu_custom_call" | custom-call | flops 8589934592 | bytes 3145728 | tf_op jit(solution)/shard_map/attend/pallas_call | solution.py:205
  95.2 13.5 %attend.7 = (f32[1024,128]{1,0:T(8,128)S(1)}, f32[2,1024]{1,0:T(2,128)S(1)}) custom-call(bf16[1024,512]{1,0:T(8,128)(2,1)S(1)} %add_convert_fusion.3.refs_0_, bf16[1024,256]{1,0:T(8,128)(2,1)S(1)} %fusion.38.refs_1_.refs_5_.refs_4_.refs_8_, bf16[1024,256]{1,0:T(8,128)(2,1)S(1)} %collective-permute-done.11.refs_2_.refs_6_.refs_5_.refs_9_, ...), custom_call_target="tpu_custom_call" | custom-call | flops 8589934592 | bytes 3145728 | tf_op jit(solution)/shard_map/attend/pallas_call | solution.py:205
  113.8 4.2 collective-permute-done.17
  123.7 5.2 %multiply_convert_fusion.1 = (bf16[512,2048]{1,0:T(8,128)(2,1)S(1)}, f32[512,2048]{1,0:T(8,128)}) fusion(f32[2048]{0:T(1024)S(1)} %add.686, bf16[512,1024]{1,0:T(8,128)(2,1)S(1)} %fusion.32, bf16[1024,2048]{1,0:T(8,128)(2,1)S(1)} %copy-done.93), kind=kOutput, calls=%fused_computation.28 | convolution fusion | flops 2157969408 | bytes 11542528 | tf_op jit(solution)/shard_map/dot_general | solution.py:25
  135.9 3.3 multiply_convert_fusion
  143.4 15.3 %collective-permute-done.18 = bf16[512,1024]{1,0:T(8,128)(2,1)S(1)} collective-permute-done((bf16[512,1024]{1,0:T(8,128)(2,1)S(1)}, bf16[512,1024]{1,0:T(8,128)(2,1)S(1)}, u32[]{:S(2)}, u32[]{:S(2)}) %collective-permute-start.18) | collective-permute-done | bytes 1048608 | tf_op jit(solution)/shard_map/ppermute | solution.py:30
  164.9 6.6 %fusion.6 = bf16[512,2048]{1,0:T(8,128)(2,1)S(1)} fusion(f32[512,2048]{1,0:T(8,128)} %get-tuple-element.366, f32[2048]{0:T(1024)S(1)} %add.686, bf16[512,1024]{1,0:T(8,128)(2,1)S(1)} %add_convert_fusion.5, bf16[2048,1024]{1,0:T(8,128)(2,1)S(1)} %copy-done.92), kind=kOutput, calls=%fused_computation.11 | convolution fusion | flops 2169503744 | bytes 11542528 | tf_op jit(solution)/shard_map/dot_general | solution.py:25
  171.4 3.4 convolution_convert_fusion.4
  175.1 6.1 %collective-permute-done.19 = bf16[512,1024]{1,0:T(8,128)(2,1)S(1)} collective-permute-done((bf16[512,1024]{1,0:T(8,128)(2,1)S(1)}, bf16[512,1024]{1,0:T(8,128)(2,1)S(1)}, u32[]{:S(2)}, u32[]{:S(2)}) %collective-permute-start.19) | collective-permute-done | bytes 1048608 | tf_op jit(solution)/shard_map/ppermute | solution.py:30
  186.6 4.8 %fusion.13 = bf16[512,2048]{1,0:T(8,128)(2,1)S(1)} fusion(f32[512,2048]{1,0:T(8,128)S(1)} %get-tuple-element.370, f32[2048]{0:T(1024)S(1)} %add.686, bf16[512,1024]{1,0:T(8,128)(2,1)S(1)} %add_convert_fusion.4, bf16[2048,1024]{1,0:T(8,128)(2,1)S(1)} %copy-done.92), kind=kOutput, calls=%fused_computation.18 | convolution fusion | flops 2169503744 | bytes 11542528 | tf_op jit(solution)/shard_map/dot_general | solution.py:25
  191.5 3.5 convolution_convert_fusion.3
  194.9 5.1 %fusion.18 = bf16[1024,2048]{1,0:T(8,128)(2,1)S(1)} fusion(bf16[1024,1024]{1,0:T(8,128)(2,1)S(1)} %pad_maximum_fusion.2, bf16[512,2048]{1,0:T(8,128)(2,1)S(1)} %copy-done.100, bf16[512,2048]{1,0:T(8,128)(2,1)S(1)} %copy-done.98), kind=kOutput, calls=%fused_computation.29 | convolution fusion | flops 4305453056 | bytes 10485760 | tf_op jit(solution)/shard_map/dot_general | solution.py:25
  212.5 7.4 %convolution_convert_fusion = bf16[1024,2048]{1,0:T(8,128)(2,1)S(1)} fusion(bf16[1024,2048]{1,0:T(8,128)(2,1)} %pad_maximum_fusion, bf16[512,1024]{1,0:T(8,128)(2,1)} %copy-done.48, bf16[512,1024]{1,0:T(8,128)(2,1)} %copy-done.47), kind=kOutput, calls=%fused_computation.30 | convolution fusion | flops 4301258752 | bytes 10485760 | tf_op jit(solution)/shard_map/dot_general | solution.py:25
  225.0 4.6 convert_add_fusion
  231.0 3.9 multiply_reduce_fusion.1
  234.9 3.1 fusion.94
  238.2 3.4 fusion.95
  253.6 3.2 convert_add_fusion.1
  256.8 34.5 %attend_back.4 = (bf16[1024,384]{1,0:T(8,128)(2,1)}, f32[1,384]{1,0:T(1,128)}, bf16[512,384]{1,0:T(8,128)(2,1)}, bf16[512,384]{1,0:T(8,128)(2,1)}, bf16[256,2048...) custom-call(bf16[1024,512]{1,0:T(8,128)(2,1)} %copy-done.20, ...), custom_call_target="tpu_custom_call" | custom-call | flops 15032385536 | bytes 5767168 | tf_op jit(solution)/shard_map/attend_back/pallas_call | solution.py:399
  297.0 31.8 %attend_back.5 = (bf16[1024,384]{1,0:T(8,128)(2,1)}, f32[1,384]{1,0:T(1,128)}, bf16[512,384]{1,0:T(8,128)(2,1)}, bf16[512,384]{1,0:T(8,128)(2,1)}, bf16[128,2048...) custom-call(bf16[1024,512]{1,0:T(8,128)(2,1)} %copy-done.20, ...), custom_call_target="tpu_custom_call" | custom-call | flops 15032385536 | bytes 5767168 | tf_op jit(solution)/shard_map/attend_back/pallas_call | solution.py:399
  336.3 30.5 %attend_back.6 = (bf16[1024,384]{1,0:T(8,128)(2,1)}, f32[1,384]{1,0:T(1,128)}, bf16[512,384]{1,0:T(8,128)(2,1)}, bf16[512,384]{1,0:T(8,128)(2,1)}, bf16[64,2048]...) custom-call(bf16[1024,512]{1,0:T(8,128)(2,1)} %copy-done.20, ...), custom_call_target="tpu_custom_call" | custom-call | flops 15032385536 | bytes 5767168 | tf_op jit(solution)/shard_map/attend_back/pallas_call | solution.py:399
  374.3 30.8 %attend_back.7 = (bf16[1024,384]{1,0:T(8,128)(2,1)}, f32[1,384]{1,0:T(1,128)}, bf16[512,384]{1,0:T(8,128)(2,1)}, bf16[512,384]{1,0:T(8,128)(2,1)}, bf16[64,512]{...) custom-call(bf16[1024,512]{1,0:T(8,128)(2,1)} %copy-done.20, ...), custom_call_target="tpu_custom_call" | custom-call | flops 15032385536 | bytes 5767168 | tf_op jit(solution)/shard_map/attend_back/pallas_call | solution.py:399
  418.5 32.1 %tail.1 = (f32[1024,1024]{1,0:T(8,128)}, f32[64,384]{1,0:T(8,128)}, f32[64,384]{1,0:T(8,128)}, f32[64,1024]{1,0:T(8,128)}, f32[64,384]{1,0:T(8,128)}, /*index=5*/f32[64,384]{1,0:T(8,128)}, f32[8,64]{1,0:T(8,128)}) custom-call(bf16[1024,384]{1,0:T(8,128)(2,1)} %get-tuple-element.115.refs_19_.refs_0_, bf16[1024,384]{1,0:T(8,128)(2,1)} %get-tuple-element.121.refs_21_.refs_1_, ...), custom_call_target="tpu_custom_call" | custom-call | flops 6442450944 | bytes 33554432 | tf_op jit(solution)/shard_map/tail/pallas_call | solution.py:610
  458.9 4.8 %copy.168 = f32[1024,1024]{1,0:T(8,128)} copy(f32[1024,1024]{1,0:T(8,128)} %get-tuple-element.391) | data formatting | bytes 8388608
  (403 shorter events, 134.7 us)
Async XLA Ops:
  7.2 57.1 %copy-start.5 = (bf16[1024,256]{1,0:T(8,128)(2,1)}, bf16[1024,256]{1,0:T(8,128)(2,1)S(1)}, u32[]{:S(2)}) copy-start(bf16[1024,256]{1,0:T(8,128)(2,1)S(1)} %fusion.40.refs_1_.refs_5_.refs_4_.refs_8_) | copy-start | bytes 1572868
  7.2 32.0 %collective-permute-start.4 = (bf16[1024,256]{1,0:T(8,128)(2,1)S(1)}, bf16[1024,256]{1,0:T(8,128)(2,1)S(1)}, u32[]{:S(2)}, u32[]{:S(2)}) collective-permute-start(bf16[1024,256]{1,0:T(8,128)(2,1)S(1)} %fusion.40.refs_1_.refs_5_.refs_4_.refs_8_), channel_id=1, source_target_pairs={{0,4},{2,6},{4,0},{6,2},{8,12},{10,14},{12,8},{14,10},{16,20},{18,... | collective-permute-start | bytes 1572872 | tf_op jit(solution)/shard_map/ppermute | solution.py:30
  10.2 46.3 %collective-permute-start.3 = (bf16[1024,256]{1,0:T(8,128)(2,1)S(1)}, bf16[1024,256]{1,0:T(8,128)(2,1)S(1)}, u32[]{:S(2)}, u32[]{:S(2)}) collective-permute-start(bf16[1024,256]{1,0:T(8,128)(2,1)S(1)} %fusion.40.refs_1_.refs_5_.refs_4_.refs_8_), channel_id=1, source_target_pairs={{0,2},{2,0},{4,6},{6,4},{8,10},{10,8},{12,14},{14,12},{16,18},{18,... | collective-permute-start | bytes 1572872 | tf_op jit(solution)/shard_map/ppermute | solution.py:30
  12.8 20.6 %collective-permute-start.1 = (bf16[1024,256]{1,0:T(8,128)(2,1)S(1)}, bf16[1024,256]{1,0:T(8,128)(2,1)S(1)}, u32[]{:S(2)}, u32[]{:S(2)}) collective-permute-start(bf16[1024,256]{1,0:T(8,128)(2,1)S(1)} %fusion.41.refs_1_.refs_5_.refs_4_.refs_8_), channel_id=1, source_target_pairs={{0,4},{2,6},{4,0},{6,2},{8,12},{10,14},{12,8},{14,10},{16,20},{18,... | collective-permute-start | bytes 1572872 | tf_op jit(solution)/shard_map/ppermute | solution.py:30
  12.9 27.8 %collective-permute-start = (bf16[1024,256]{1,0:T(8,128)(2,1)S(1)}, bf16[1024,256]{1,0:T(8,128)(2,1)}, u32[]{:S(2)}, u32[]{:S(2)}) collective-permute-start(bf16[1024,256]{1,0:T(8,128)(2,1)S(1)} %fusion.41.refs_1_.refs_5_.refs_4_.refs_8_), channel_id=1, source_target_pairs={{0,2},{2,0},{4,6},{6,4},{8,10},{10,8},{12,14},{14,12},{16,18},{18,... | collective-permute-start | bytes 1572872 | tf_op jit(solution)/shard_map/ppermute | solution.py:30
  15.4 20.0 %collective-permute-start.10 = (bf16[1024,384]{1,0:T(8,128)(2,1)}, bf16[1024,384]{1,0:T(8,128)(2,1)}, u32[]{:S(2)}, u32[]{:S(2)}) collective-permute-start(bf16[1024,384]{1,0:T(8,128)(2,1)} %pad_maximum_fusion.4), channel_id=1, source_target_pairs={{0,1},{1,0},{2,3},{3,2},{4,5},{5,4},{6,7},{7,6},{8,9},{9,8},{10,11... | collective-permute-start | bytes 2359304 | tf_op jit(solution)/shard_map/ppermute | solution.py:30
  19.5 75.7 %copy-start.4 = (bf16[1024,256]{1,0:T(8,128)(2,1)}, bf16[1024,256]{1,0:T(8,128)(2,1)S(1)}, u32[]{:S(2)}) copy-start(bf16[1024,256]{1,0:T(8,128)(2,1)S(1)} %fusion.38.refs_1_.refs_5_.refs_4_.refs_8_) | copy-start | bytes 1572868
  29.1 66.1 %copy-start.20 = (bf16[1024,512]{1,0:T(8,128)(2,1)}, bf16[1024,512]{1,0:T(8,128)(2,1)S(1)}, u32[]{:S(2)}) copy-start(bf16[1024,512]{1,0:T(8,128)(2,1)S(1)} %add_convert_fusion.3.refs_0_) | copy-start | bytes 3145732
  33.4 7.8 %collective-permute-start.2 = (bf16[1024,256]{1,0:T(8,128)(2,1)S(1)}, bf16[1024,256]{1,0:T(8,128)(2,1)S(1)}, u32[]{:S(2)}, u32[]{:S(2)}) collective-permute-start(bf16[1024,256]{1,0:T(8,128)(2,1)S(1)} %collective-permute-done.1.refs_3_.refs_7_.refs_6_.refs_10_), channel_id=1, source_target_pairs={{0,2},{2,0},{4,6},{6,4},{8,10},{10,8},{12,14},{14,12},{16,18},{18,... | collective-permute-start | bytes 1572872 | tf_op jit(solution)/shard_map/ppermute | solution.py:30
  34.2 44.3 %copy-start.13 = (bf16[1024,256]{1,0:T(8,128)(2,1)}, bf16[1024,256]{1,0:T(8,128)(2,1)S(1)}, u32[]{:S(2)}) copy-start(bf16[1024,256]{1,0:T(8,128)(2,1)S(1)} %fusion.39.refs_1_.refs_5_.refs_4_.refs_8_) | copy-start | bytes 1572868
  35.4 43.0 %collective-permute-start.6 = (bf16[512,1024]{1,0:T(8,128)(2,1)S(1)}, bf16[512,1024]{1,0:T(8,128)(2,1)S(1)}, u32[]{:S(2)}, u32[]{:S(2)}) collective-permute-start(bf16[512,1024]{1,0:T(8,128)(2,1)S(1)} %copy-done.94), channel_id=1, source_target_pairs={{0,1},{1,0},{2,3},{3,2},{4,5},{5,4},{6,7},{7,6},{8,9},{9,8},{10,11... | collective-permute-start | bytes 3145736 | tf_op jit(solution)/shard_map/ppermute | solution.py:30
  39.2 17.8 %collective-permute-start.8 = (bf16[1024,256]{1,0:T(8,128)(2,1)S(1)}, bf16[1024,256]{1,0:T(8,128)(2,1)S(1)}, u32[]{:S(2)}, u32[]{:S(2)}) collective-permute-start(bf16[1024,256]{1,0:T(8,128)(2,1)S(1)} %fusion.39.refs_1_.refs_5_.refs_4_.refs_8_), channel_id=1, source_target_pairs={{0,4},{2,6},{4,0},{6,2},{8,12},{10,14},{12,8},{14,10},{16,20},{18,... | collective-permute-start | bytes 1572872 | tf_op jit(solution)/shard_map/ppermute | solution.py:30
  40.7 23.1 %collective-permute-start.12 = (bf16[1024,256]{1,0:T(8,128)(2,1)S(1)}, bf16[1024,256]{1,0:T(8,128)(2,1)S(1)}, u32[]{:S(2)}, u32[]{:S(2)}) collective-permute-start(bf16[1024,256]{1,0:T(8,128)(2,1)S(1)} %fusion.38.refs_1_.refs_5_.refs_4_.refs_8_), channel_id=1, source_target_pairs={{0,4},{2,6},{4,0},{6,2},{8,12},{10,14},{12,8},{14,10},{16,20},{18,... | collective-permute-start | bytes 1572872 | tf_op jit(solution)/shard_map/ppermute | solution.py:30
  41.2 22.5 %collective-permute-start.5 = (bf16[1024,256]{1,0:T(8,128)(2,1)S(1)}, bf16[1024,256]{1,0:T(8,128)(2,1)S(1)}, u32[]{:S(2)}, u32[]{:S(2)}) collective-permute-start(bf16[1024,256]{1,0:T(8,128)(2,1)S(1)} %collective-permute-done.4.refs_3_.refs_7_.refs_6_.refs_10_), channel_id=1, source_target_pairs={{0,2},{2,0},{4,6},{6,4},{8,10},{10,8},{12,14},{14,12},{16,18},{18,... | collective-permute-start | bytes 1572872 | tf_op jit(solution)/shard_map/ppermute | solution.py:30
  56.6 35.8 %copy-start.3 = (f32[1024,128]{1,0:T(8,128)}, f32[1024,128]{1,0:T(8,128)S(1)}, u32[]{:S(2)}) copy-start(f32[1024,128]{1,0:T(8,128)S(1)} %get-tuple-element.93.refs_2_) | copy-start | bytes 1572868
  56.6 21.9 %collective-permute-start.7 = (bf16[1024,256]{1,0:T(8,128)(2,1)S(1)}, bf16[1024,256]{1,0:T(8,128)(2,1)S(1)}, u32[]{:S(2)}, u32[]{:S(2)}) collective-permute-start(bf16[1024,256]{1,0:T(8,128)(2,1)S(1)} %fusion.39.refs_1_.refs_5_.refs_4_.refs_8_), channel_id=1, source_target_pairs={{0,2},{2,0},{4,6},{6,4},{8,10},{10,8},{12,14},{14,12},{16,18},{18,... | collective-permute-start | bytes 1572872 | tf_op jit(solution)/shard_map/ppermute | solution.py:30
  57.0 38.2 %collective-permute-start.11 = (bf16[1024,256]{1,0:T(8,128)(2,1)S(1)}, bf16[1024,256]{1,0:T(8,128)(2,1)S(1)}, u32[]{:S(2)}, u32[]{:S(2)}) collective-permute-start(bf16[1024,256]{1,0:T(8,128)(2,1)S(1)} %fusion.38.refs_1_.refs_5_.refs_4_.refs_8_), channel_id=1, source_target_pairs={{0,2},{2,0},{4,6},{6,4},{8,10},{10,8},{12,14},{14,12},{16,18},{18,... | collective-permute-start | bytes 1572872 | tf_op jit(solution)/shard_map/ppermute | solution.py:30
  63.7 14.7 %collective-permute-start.9 = (bf16[1024,256]{1,0:T(8,128)(2,1)S(1)}, bf16[1024,256]{1,0:T(8,128)(2,1)S(1)}, u32[]{:S(2)}, u32[]{:S(2)}) collective-permute-start(bf16[1024,256]{1,0:T(8,128)(2,1)S(1)} %collective-permute-done.8.refs_3_.refs_7_.refs_6_.refs_10_), channel_id=1, source_target_pairs={{0,2},{2,0},{4,6},{6,4},{8,10},{10,8},{12,14},{14,12},{16,18},{18,... | collective-permute-start | bytes 1572872 | tf_op jit(solution)/shard_map/ppermute | solution.py:30
  63.8 31.4 %collective-permute-start.13 = (bf16[1024,256]{1,0:T(8,128)(2,1)S(1)}, bf16[1024,256]{1,0:T(8,128)(2,1)S(1)}, u32[]{:S(2)}, u32[]{:S(2)}) collective-permute-start(bf16[1024,256]{1,0:T(8,128)(2,1)S(1)} %collective-permute-done.12.refs_3_.refs_7_.refs_6_.refs_10_), channel_id=1, source_target_pairs={{0,2},{2,0},{4,6},{6,4},{8,10},{10,8},{12,14},{14,12},{16,18},{18,... | collective-permute-start | bytes 1572872 | tf_op jit(solution)/shard_map/ppermute | solution.py:30
  92.8 20.8 %collective-permute-start.16 = (bf16[1024,128]{1,0:T(8,128)(2,1)S(1)}, bf16[1024,128]{1,0:T(8,128)(2,1)S(1)}, u32[]{:S(2)}, u32[]{:S(2)}) collective-permute-start(bf16[1024,128]{1,0:T(8,128)(2,1)S(1)} %get-tuple-element.270), channel_id=1, source_target_pairs={{0,1},{1,0},{2,3},{3,2},{4,5},{5,4},{6,7},{7,6},{8,9},{9,8},{10,11... | collective-permute-start | bytes 786440 | tf_op jit(solution)/shard_map/ppermute | solution.py:30
  93.1 20.3 %collective-permute-start.15 = (bf16[1024,128]{1,0:T(8,128)(2,1)S(1)}, bf16[1024,128]{1,0:T(8,128)(2,1)S(1)}, u32[]{:S(2)}, u32[]{:S(2)}) collective-permute-start(bf16[1024,128]{1,0:T(8,128)(2,1)S(1)} %get-tuple-element.272), channel_id=1, source_target_pairs={{0,1},{1,0},{2,3},{3,2},{4,5},{5,4},{6,7},{7,6},{8,9},{9,8},{10,11... | collective-permute-start | bytes 786440 | tf_op jit(solution)/shard_map/ppermute | solution.py:30
  94.9 18.4 %collective-permute-start.14 = (bf16[1024,128]{1,0:T(8,128)(2,1)S(1)}, bf16[1024,128]{1,0:T(8,128)(2,1)S(1)}, u32[]{:S(2)}, u32[]{:S(2)}) collective-permute-start(bf16[1024,128]{1,0:T(8,128)(2,1)S(1)} %get-tuple-element.274), channel_id=1, source_target_pairs={{0,1},{1,0},{2,3},{3,2},{4,5},{5,4},{6,7},{7,6},{8,9},{9,8},{10,11... | collective-permute-start | bytes 786440 | tf_op jit(solution)/shard_map/ppermute | solution.py:30
  108.9 9.1 %collective-permute-start.17 = (bf16[1024,128]{1,0:T(8,128)(2,1)S(1)}, bf16[1024,128]{1,0:T(8,128)(2,1)S(1)}, u32[]{:S(2)}, u32[]{:S(2)}) collective-permute-start(bf16[1024,128]{1,0:T(8,128)(2,1)S(1)} %get-tuple-element.268), channel_id=1, source_target_pairs={{0,1},{1,0},{2,3},{3,2},{4,5},{5,4},{6,7},{7,6},{8,9},{9,8},{10,11... | collective-permute-start | bytes 786440 | tf_op jit(solution)/shard_map/ppermute | solution.py:30
  132.7 26.1 %collective-permute-start.18 = (bf16[512,1024]{1,0:T(8,128)(2,1)S(1)}, bf16[512,1024]{1,0:T(8,128)(2,1)S(1)}, u32[]{:S(2)}, u32[]{:S(2)}) collective-permute-start(bf16[512,1024]{1,0:T(8,128)(2,1)S(1)} %convolution_convert_fusion.6), channel_id=1, source_target_pairs={{0,1},{1,0},{2,3},{3,2},{4,5},{5,4},{6,7},{7,6},{8,9},{9,8},{10,11... | collective-permute-start | bytes 3145736 | tf_op jit(solution)/shard_map/ppermute | solution.py:30
  135.1 46.1 %copy-start.25 = (f32[512,1024]{1,0:T(8,128)}, f32[512,1024]{1,0:T(8,128)S(1)}, u32[]{:S(2)}) copy-start(f32[512,1024]{1,0:T(8,128)S(1)} %get-tuple-element.368) | copy-start | bytes 6291460
  141.6 39.6 %collective-permute-start.19 = (bf16[512,1024]{1,0:T(8,128)(2,1)S(1)}, bf16[512,1024]{1,0:T(8,128)(2,1)S(1)}, u32[]{:S(2)}, u32[]{:S(2)}) collective-permute-start(bf16[512,1024]{1,0:T(8,128)(2,1)S(1)} %convolution_convert_fusion.5), channel_id=1, source_target_pairs={{0,1},{1,0},{2,3},{3,2},{4,5},{5,4},{6,7},{7,6},{8,9},{9,8},{10,11... | collective-permute-start | bytes 3145736 | tf_op jit(solution)/shard_map/ppermute | solution.py:30
  174.8 56.1 %collective-permute-start.20 = (bf16[512,1024]{1,0:T(8,128)(2,1)}, bf16[512,1024]{1,0:T(8,128)(2,1)}, u32[]{:S(2)}, u32[]{:S(2)}) collective-permute-start(bf16[512,1024]{1,0:T(8,128)(2,1)} %convolution_convert_fusion.4), channel_id=1, source_target_pairs={{0,1},{1,0},{2,3},{3,2},{4,5},{5,4},{6,7},{7,6},{8,9},{9,8},{10,11... | collective-permute-start | bytes 3145736 | tf_op jit(solution)/shard_map/ppermute | solution.py:30
  202.5 21.6 %collective-permute-start.21 = (bf16[512,2048]{1,0:T(8,128)(2,1)}, bf16[512,2048]{1,0:T(8,128)(2,1)}, u32[]{:S(2)}, u32[]{:S(2)}) collective-permute-start(bf16[512,2048]{1,0:T(8,128)(2,1)} %bitcast.9), channel_id=1, source_target_pairs={{0,2},{2,0},{4,6},{6,4},{8,10},{10,8},{12,14},{14,12},{16,18},{18,... | collective-permute-start | bytes 6291464 | tf_op jit(solution)/shard_map/ppermute | solution.py:30
  205.1 25.9 %collective-permute-start.22 = (bf16[512,1024]{1,0:T(8,128)(2,1)}, bf16[512,1024]{1,0:T(8,128)(2,1)}, u32[]{:S(2)}, u32[]{:S(2)}) collective-permute-start(bf16[512,1024]{1,0:T(8,128)(2,1)} %convolution_convert_fusion.3), channel_id=1, source_target_pairs={{0,1},{1,0},{2,3},{3,2},{4,5},{5,4},{6,7},{7,6},{8,9},{9,8},{10,11... | collective-permute-start | bytes 3145736 | tf_op jit(solution)/shard_map/ppermute | solution.py:30
  222.4 27.4 %collective-permute-start.23 = (bf16[512,2048]{1,0:T(8,128)(2,1)}, bf16[512,2048]{1,0:T(8,128)(2,1)}, u32[]{:S(2)}, u32[]{:S(2)}) collective-permute-start(bf16[512,2048]{1,0:T(8,128)(2,1)} %bitcast.13), channel_id=1, source_target_pairs={{0,2},{2,0},{4,6},{6,4},{8,10},{10,8},{12,14},{14,12},{16,18},{18,... | collective-permute-start | bytes 6291464 | tf_op jit(solution)/shard_map/ppermute | solution.py:30
  332.3 37.4 %copy-start.62 = (f32[2,1,64,512]{3,2,1,0:T(8,128)}, f32[2,1,64,512]{3,2,1,0:T(8,128)S(1)}, u32[]{:S(2)}) copy-start(f32[2,1,64,512]{3,2,1,0:T(8,128)S(1)} %get-tuple-element.323) | copy-start | bytes 786436
  374.3 33.8 %copy-start.68 = (bf16[128,2048]{1,0:T(8,128)(2,1)S(1)}, bf16[128,2048]{1,0:T(8,128)(2,1)}, u32[]{:S(2)}) copy-start(bf16[128,2048]{1,0:T(8,128)(2,1)} %get-tuple-element.122) | copy-start | bytes 1572868
  (93 other events, 800.6 us)

commit v5 on v4

--- a/solution.py
+++ b/solution.py
@@ -14,7 +14,7 @@
 LANES = 128
 HALF = 64
 SOURCES = 4
-CHUNKS = 2
+CHUNKS = 3
 NN = (((1,), (0,)), ((), ()))
 NT = (((1,), (1,)), ((), ()))
 TN = (((0,), (0,)), ((), ()))
@@ -151,6 +151,10 @@
 
 def gelu_tanh(values):
     return jax.nn.gelu(values, approximate=True)
+
+
+def column_sums(values):
+    return dot(jnp.ones((16, values.shape[0]), BF16), values, NN)[0]
 
 
 def head_lanes(shape, head):
@@ -448,7 +452,7 @@
     )(queries, grads, context, lse, *blocks, *blocks, tokens, *values)
 
 
-def tail_kernel(plans, widths, *refs):
+def tail_kernel(plans, widths, merged, *refs):
     chains = len(plans)
     groups = len(widths)
     pieces = sum(len(part) for part in widths)
@@ -465,7 +469,11 @@
     own_weights, other_weights, base_refs = take(pieces), take(pieces - 1), take(CHUNKS)
     keep_refs, cargo_refs = take(chains), take(chains)
     total_ref = take(1)[0]
-    result_refs = take(chains)
+    merged_ref = take(1)[0]
+    result_refs = list(take(chains - len(merged)))
+    result_refs = [
+        None if chain in merged else result_refs.pop(0) for chain in range(chains)
+    ]
     rows_refs, weight_refs, last_rows, last_weights = take(2), take(2), take(2), take(2)
     base_ref = take(1)[0]
     hops = [[take(3) for _ in plan] for plan in plans]
@@ -514,9 +522,11 @@
                 load(parts.pop(0), target.at[:, base : base + piece])
                 base += piece
     load(joined_refs[last], last_rows[0])
+    top = 0
     for part in range(CHUNKS):
         height = base_refs[part].shape[0]
-        load(base_refs[part], base_ref.at[part * height : (part + 1) * height, :])
+        load(base_refs[part], base_ref.at[top : top + height, :])
+        top += height
 
     def advance(level):
         for chain, plan in enumerate(plans):
@@ -533,7 +543,14 @@
                 held = hops[chain][level][2][:, own].reshape(land.shape)
             whole = held + land[...].astype(F32)
             if level == len(plan) - 1:
-                result_refs[chain][...] = whole
+                if chain not in merged:
+                    result_refs[chain][...] = whole
+                    continue
+                for piece in range(3):
+                    at = (piece * groups + merged.index(chain)) * LANES
+                    merged_ref[:, at : at + LANES] = whole[
+                        :, piece * LANES : (piece + 1) * LANES
+                    ]
                 continue
             bit, high, low = plan[level + 1]
             _, out, split = hops[chain][level + 1]
@@ -575,7 +592,9 @@
     advance(depth - 1)
 
 
-def tail(joined, others, own_weights, other_weights, base, chains, collective_id):
+def tail(
+    joined, others, own_weights, other_weights, base, chains, merged, collective_id
+):
     groups = len(joined)
     rows, wide = joined[0].shape
     width = own_weights[0][0].shape[0]
@@ -601,18 +620,22 @@
                 pltpu.VMEM((high, 2, low, cols), F32),
             ]
         plans.append(plan)
-        results.append(jax.ShapeDtypeStruct((part, cols), F32))
+        if chain not in merged:
+            results.append(jax.ShapeDtypeStruct((part, cols), F32))
+    results.insert(0, jax.ShapeDtypeStruct((merged[0].part, groups * wide), F32))
     anywhere = pl.BlockSpec(memory_space=pl.ANY)
     inside = pl.BlockSpec(memory_space=pltpu.VMEM)
     values = [*joined, *others, *own_weights, *other_weights, *base]
     loads = 2 * (groups - 1) + 2 * len(own_weights) + CHUNKS
     hops = sum(len(plan) for plan in plans)
     return pl.pallas_call(
-        functools.partial(tail_kernel, plans, widths),
+        functools.partial(
+            tail_kernel, plans, widths, [chains.index(chain) for chain in merged]
+        ),
         in_specs=[anywhere] * len(values)
         + [inside] * len(chains)
         + [anywhere] * len(chains),
-        out_specs=[inside] * (1 + len(chains)),
+        out_specs=[inside] * (1 + len(results)),
         out_shape=[jax.ShapeDtypeStruct((rows, width), F32)] + results,
         scratch_shapes=[pltpu.VMEM((rows, (groups - 1) * wide), BF16)] * 2
         + [pltpu.VMEM((width, (groups - 1) * wide), BF16)] * 2
@@ -704,8 +727,8 @@
     context = jnp.concatenate(own_context, axis=1)
     context_whole = in_order(context, jnp.concatenate(other_context, axis=1), 1)
 
-    step = rows // CHUNKS
-    cuts = [slice(i * step, (i + 1) * step) for i in range(CHUNKS)]
+    edges = [0, rows // 4, 3 * rows // 4, rows]
+    cuts = [slice(*edges[i : i + 2]) for i in range(CHUNKS)]
     firsts, lows, actives, active_lows, feed_lows, feed_others = [], [], [], [], [], []
     done = context_whole
     for cut in cuts:
@@ -756,8 +779,8 @@
     up_rows = dot(first_low, hidden_low, TN).astype(BF16)
     up_scatter = Scatter(up_rows, BF16, True)
     up_flight = up_scatter.fly()
-    downbias_grad = jnp.sum(feed_grad.astype(F32), axis=0)
-    upbias_grad = jnp.sum(hidden_low.astype(F32), axis=0)
+    downbias_grad = column_sums(feed_grad)
+    upbias_grad = column_sums(hidden_low)
     secondgain_grad = sum(grads[1] for grads in second_grads)
     secondshift_grad = sum(grads[2] for grads in second_grads)
     done = down_scatter.gather(after(down_flight, up_rows))
@@ -779,7 +802,7 @@
     firstgain_grad = sum(firstgain_parts)
     firstshift_grad = sum(firstshift_parts)
     attention_grad = attention_back.astype(BF16)
-    outbias_grad = jnp.sum(attention_grad.astype(F32), axis=0)
+    outbias_grad = column_sums(attention_grad)
     context_grad = dot(attention_grad, out_weight, NT).astype(BF16)
     out_rows = dot(attention_grad, context, TN).astype(BF16)
     out_scatter = Scatter(out_rows, BF16)
@@ -856,17 +879,22 @@
     late_scatter = Scatter(late_rows.reshape(8 * size, -1), F32)
     active.append(late_scatter)
 
-    tokens_grad, *ends = tail(
-        joined, others, weights, other_weights, attention_backs, active, groups
+    tokens_grad, proj_grad, *ends = tail(
+        joined,
+        others,
+        weights,
+        other_weights,
+        attention_backs,
+        active,
+        proj_scatters,
+        groups,
     )
-    for scatter, value in zip(active, ends):
-        scatter.whole = value
+    for scatter in active:
+        if scatter not in proj_scatters:
+            scatter.whole = ends.pop(0)
     outweight_grad = out_scatter.result()
     upweight_grad = up_scatter.result()
     downweight_grad = jnp.concatenate([part.result() for part in down_parts], axis=1)
-    proj_grad = jnp.stack(
-        [scatter.result().reshape(-1, 3, LANES) for scatter in proj_scatters], axis=2
-    )
     vectors = unpack(late_scatter.result()[0], late) + unpack(
         early_scatter.result()[0], early
     )

time: 468 us -> 459 us (0.981)
  waiting for transfers between devices: 41.6 us -> 26.2 us
  matrix products: 61 us -> 69.9 us
  local copies, waits for them, and re-layouts: 56.5 us -> 50.5 us
    ppermute x24 -> x26, waiting for transfers between devices: 41.6 us -> 26.2 us  [flip(): return lax.ppermute(value, axis, pairs)]
    dot_general x19 -> x27, matrix products: 61 us -> 69.9 us  [dot(): return lax.dot_general(left, right, dims, preferred_element_type=F32)]
    reduce_sum x3 -> x0, other arithmetic: 5.14 us -> none  [the longest x1 2.83 us: body(): upbias_grad = jnp.sum(hidden_low.astype(F32), axis=0)]
    ppermute x24 -> x26, starting transfers between devices: 17.4 us -> 21.4 us  [flip(): return lax.ppermute(value, axis, pairs)]
    unnamed x215 -> x245, local copies, waits for them, and re-layouts: 24.7 us -> 24.1 us
  transfers between devices with their start and end apart: 24 -> 26, of which waited for: 8 -> 5; matrix products, arithmetic and copies ran while one was open for 23% -> 26% of each run, Pallas kernels for 12% -> 12%
where the time goes in v5:
time: 459 us; the launch traced here: 455 us
  Pallas kernels  216 us (47%)
  matrix products  69.9 us (15%)
  other arithmetic  68.9 us (15%)
  local copies, waits for them, and re-layouts  50.5 us (11%)
  waiting for transfers between devices  26.2 us (6%)
  starting transfers between devices  21.4 us (5%)
    pallas_call x4, Pallas kernels, attend_back(): pl.pallas_call(functools.partial(backward_kernel, scale, span // 2, links...  129 us
    dot_general x27, matrix products, dot(): return lax.dot_general(left, right, dims, preferred_element_type=F32)  69.9 us
    pallas_call x4, Pallas kernels, attend(): pl.pallas_call(functools.partial(forward_kernel, scale, span // 2), grid=...  54.9 us
    pallas_call x1, Pallas kernels, tail(): pl.pallas_call(functools.partial(tail_kernel, plans, widths, [chains.inde...  32.1 us
    ppermute x26, waiting for transfers between devices, flip(): return lax.ppermute(value, axis, pairs)  26.2 us
    unnamed x245, local copies, waits for them, and re-layouts  24.1 us
    ppermute x26, starting transfers between devices, flip(): return lax.ppermute(value, axis, pairs)  21.4 us
    add x14, other arithmetic, land(): self.split([a.astype(F32) + b.astype(F32) for a, b in zip(kept, sent)])  17 us
  transfers between devices with their start and end apart: 26, of which 5 were waited for; matrix products, arithmetic and copies ran while one was open for 26% of the time, Pallas kernels for 12%

profile of v5, /device:TPU:0, one launch (start us, length us, event | category | flops | bytes accessed | tf_op | source)
XLA Modules:
  0.0 455.0 jit_solution(13876878561172291970)
XLA Ops:
  0.7 3.0 slice_bitcast_fusion.2
  6.6 3.0 collective-permute-start.1
  9.7 2.4 fusion.52.refs_1_.refs_5_.refs_4_.refs_8_
  16.5 2.4 fusion.50.refs_1_.refs_5_.refs_4_.refs_8_
  19.0 4.5 copy.79
  25.6 3.2 add_convert_fusion.2.refs_0_
  29.7 5.0 %collective-permute-done.10 = bf16[1024,384]{1,0:T(8,128)(2,1)} collective-permute-done((bf16[1024,384]{1,0:T(8,128)(2,1)}, bf16[1024,384]{1,0:T(8,128)(2,1)}, u32[]{:S(2)}, u32[]{:S(2)}) %collective-permute-start.10) | collective-permute-done | bytes 786464 | tf_op jit(solution)/shard_map/ppermute | solution.py:30
  41.8 14.1 %attend.4 = (f32[1024,128]{1,0:T(8,128)S(1)}, f32[2,1024]{1,0:T(2,128)S(1)}) custom-call(bf16[1024,512]{1,0:T(8,128)(2,1)S(1)} %add_convert_fusion.2.refs_0_, bf16[1024,256]{1,0:T(8,128)(2,1)S(1)} %fusion.53.refs_1_.refs_5_.refs_4_.refs_8_, bf16[1024,256]{1,0:T(8,128)(2,1)} %collective-permute-done.refs_2_.refs_6_.refs_5_.refs_9_, ...), custom_call_target="tpu_custom_call" | custom-call | flops 8589934592 | bytes 3145728 | tf_op jit(solution)/shard_map/attend/pallas_call | solution.py:209
  56.5 6.2 %collective-permute-done.12.refs_3_.refs_7_.refs_6_.refs_10_ = bf16[1024,256]{1,0:T(8,128)(2,1)S(1)} collective-permute-done((bf16[1024,256]{1,0:T(8,128)(2,1)S(1)}, bf16[1024,256]{1,0:T(8,128)(2,1)S(1)}, u32[]{:S(2)}, u32[]{:S(2)}) %collective-permute-start.12) | collective-permute-done | bytes 524320 | tf_op jit(solution)/shard_map/ppermute | solution.py:30
  63.2 13.5 %attend.5 = (f32[1024,128]{1,0:T(8,128)S(1)}, f32[2,1024]{1,0:T(2,128)S(1)}) custom-call(bf16[1024,512]{1,0:T(8,128)(2,1)S(1)} %add_convert_fusion.2.refs_0_, bf16[1024,256]{1,0:T(8,128)(2,1)S(1)} %fusion.52.refs_1_.refs_5_.refs_4_.refs_8_, bf16[1024,256]{1,0:T(8,128)(2,1)S(1)} %collective-permute-done.3.refs_2_.refs_6_.refs_5_.refs_9_, ...), custom_call_target="tpu_custom_call" | custom-call | flops 8589934592 | bytes 3145728 | tf_op jit(solution)/shard_map/attend/pallas_call | solution.py:209
  77.4 13.5 %attend.6 = (f32[1024,128]{1,0:T(8,128)S(1)}, f32[2,1024]{1,0:T(2,128)S(1)}) custom-call(bf16[1024,512]{1,0:T(8,128)(2,1)S(1)} %add_convert_fusion.2.refs_0_, bf16[1024,256]{1,0:T(8,128)(2,1)S(1)} %fusion.51.refs_1_.refs_5_.refs_4_.refs_8_, bf16[1024,256]{1,0:T(8,128)(2,1)S(1)} %collective-permute-done.7.refs_2_.refs_6_.refs_5_.refs_9_, ...), custom_call_target="tpu_custom_call" | custom-call | flops 8589934592 | bytes 3145728 | tf_op jit(solution)/shard_map/attend/pallas_call | solution.py:209
  94.0 13.8 %attend.7 = (f32[1024,128]{1,0:T(8,128)S(1)}, f32[2,1024]{1,0:T(2,128)S(1)}) custom-call(bf16[1024,512]{1,0:T(8,128)(2,1)S(1)} %add_convert_fusion.2.refs_0_, bf16[1024,256]{1,0:T(8,128)(2,1)S(1)} %fusion.50.refs_1_.refs_5_.refs_4_.refs_8_, bf16[1024,256]{1,0:T(8,128)(2,1)S(1)} %collective-permute-done.11.refs_2_.refs_6_.refs_5_.refs_9_, ...), custom_call_target="tpu_custom_call" | custom-call | flops 8589934592 | bytes 3145728 | tf_op jit(solution)/shard_map/attend/pallas_call | solution.py:209
  111.7 4.6 %collective-permute-done.17 = bf16[1024,128]{1,0:T(8,128)(2,1)S(1)} collective-permute-done((bf16[1024,128]{1,0:T(8,128)(2,1)S(1)}, bf16[1024,128]{1,0:T(8,128)(2,1)S(1)}, u32[]{:S(2)}, u32[]{:S(2)}) %collective-permute-start.17) | collective-permute-done | bytes 262176 | tf_op jit(solution)/shard_map/ppermute | solution.py:30
  128.1 5.2 %multiply_convert_fusion = (bf16[512,2048]{1,0:T(8,128)(2,1)S(1)}, f32[512,2048]{1,0:T(8,128)}) fusion(f32[2048]{0:T(1024)S(1)} %add.816, bf16[512,1024]{1,0:T(8,128)(2,1)S(1)} %fusion.39, bf16[1024,2048]{1,0:T(8,128)(2,1)S(1)} %copy-done.108), kind=kOutput, calls=%fused_computation.17 | convolution fusion | flops 2157969408 | bytes 11542528 | tf_op jit(solution)/shard_map/dot_general | solution.py:25
  152.9 8.9 %collective-permute-done.19 = bf16[512,1024]{1,0:T(8,128)(2,1)S(1)} collective-permute-done((bf16[512,1024]{1,0:T(8,128)(2,1)S(1)}, bf16[512,1024]{1,0:T(8,128)(2,1)S(1)}, u32[]{:S(2)}, u32[]{:S(2)}) %collective-permute-start.19) | collective-permute-done | bytes 1048608 | tf_op jit(solution)/shard_map/ppermute | solution.py:30
  167.4 5.2 %fusion.6 = bf16[512,2048]{1,0:T(8,128)(2,1)S(1)} fusion(f32[512,2048]{1,0:T(8,128)S(1)} %copy-done.114, f32[2048]{0:T(1024)S(1)} %add.816, bf16[512,1024]{1,0:T(8,128)(2,1)S(1)} %add_convert_fusion.3, bf16[2048,1024]{1,0:T(8,128)(2,1)S(1)} %copy-done.107), kind=kOutput, calls=%fused_computation.8 | convolution fusion | flops 2169503744 | bytes 11542528 | tf_op jit(solution)/shard_map/dot_general | solution.py:25
  172.7 3.4 convolution_convert_fusion.3
  190.2 7.4 %fusion.13 = bf16[1024,2048]{1,0:T(8,128)(2,1)S(1)} fusion(bf16[1024,1024]{1,0:T(8,128)(2,1)} %pad_maximum_fusion.2, bf16[256,2048]{1,0:T(8,128)(2,1)} %copy-done.113, bf16[512,2048]{1,0:T(8,128)(2,1)} %copy-done.115, bf16[256,2048]{1,0:T(8,128)(2,1)} %copy-done.112), kind=kOutput, calls=%fused_computation.18 | convolution fusion | flops 4309647360 | bytes 10485760 | tf_op jit(solution)/shard_map/dot_general | solution.py:25
  200.0 2.8 convolution_reduce_fusion
  207.1 7.6 %convolution_convert_fusion = bf16[1024,2048]{1,0:T(8,128)(2,1)S(1)} fusion(bf16[1024,2048]{1,0:T(8,128)(2,1)} %pad_maximum_fusion, bf16[256,1024]{1,0:T(8,128)(2,1)} %copy-done.77, bf16[512,1024]{1,0:T(8,128)(2,1)} %copy-done.52, bf16[256,1024]{1,0:T(8,128)(2,1)} %copy-done.76), kind=kOutput, calls=%fused_computation.19 | convolution fusion | flops 4303355904 | bytes 10485760 | tf_op jit(solution)/shard_map/dot_general | solution.py:25
  214.7 2.4 constant_dynamic-slice_fusion.18
  220.0 4.6 %convert_add_fusion = f32[512,2048]{1,0:T(8,128)} fusion(bf16[512,2048]{1,0:T(8,128)(2,1)} %collective-permute-done.22, bf16[8,1,64,2048]{3,2,1,0:T(8,128)(2,1)S(1)} %copy-done.38), kind=kLoop, calls=%fused_computation.16 | loop fusion | flops 3145728 | bytes 8388608 | tf_op jit(solution)/shard_map/add | solution.py:103
  224.6 2.8 multiply_reduce_fusion
  227.4 2.5 multiply_reduce_fusion.5
  239.3 2.5 convolution_convert_fusion.1
  248.7 3.2 convert_add_fusion.1
  251.9 35.3 %attend_back.4 = (bf16[1024,384]{1,0:T(8,128)(2,1)}, f32[1,384]{1,0:T(1,128)}, bf16[512,384]{1,0:T(8,128)(2,1)}, bf16[512,384]{1,0:T(8,128)(2,1)}, bf16[256,2048...) custom-call(bf16[1024,512]{1,0:T(8,128)(2,1)} %copy-done.20, ...), custom_call_target="tpu_custom_call" | custom-call | flops 15032385536 | bytes 5767168 | tf_op jit(solution)/shard_map/attend_back/pallas_call | solution.py:403
  293.0 31.7 %attend_back.5 = (bf16[1024,384]{1,0:T(8,128)(2,1)}, f32[1,384]{1,0:T(1,128)}, bf16[512,384]{1,0:T(8,128)(2,1)}, bf16[512,384]{1,0:T(8,128)(2,1)}, bf16[128,2048...) custom-call(bf16[1024,512]{1,0:T(8,128)(2,1)} %copy-done.20, ...), custom_call_target="tpu_custom_call" | custom-call | flops 15032385536 | bytes 5767168 | tf_op jit(solution)/shard_map/attend_back/pallas_call | solution.py:403
  331.2 30.7 %attend_back.6 = (bf16[1024,384]{1,0:T(8,128)(2,1)}, f32[1,384]{1,0:T(1,128)}, bf16[512,384]{1,0:T(8,128)(2,1)}, bf16[512,384]{1,0:T(8,128)(2,1)}, bf16[64,2048]...) custom-call(bf16[1024,512]{1,0:T(8,128)(2,1)} %copy-done.20, ...), custom_call_target="tpu_custom_call" | custom-call | flops 15032385536 | bytes 5767168 | tf_op jit(solution)/shard_map/attend_back/pallas_call | solution.py:403
  368.1 30.9 %attend_back.7 = (bf16[1024,384]{1,0:T(8,128)(2,1)}, f32[1,384]{1,0:T(1,128)}, bf16[512,384]{1,0:T(8,128)(2,1)}, bf16[512,384]{1,0:T(8,128)(2,1)}, bf16[64,512]{...) custom-call(bf16[1024,512]{1,0:T(8,128)(2,1)} %copy-done.20, ...), custom_call_target="tpu_custom_call" | custom-call | flops 15032385536 | bytes 5767168 | tf_op jit(solution)/shard_map/attend_back/pallas_call | solution.py:403
  412.0 32.1 %tail.1 = (f32[1024,1024]{1,0:T(8,128)}, f32[64,1536]{1,0:T(8,128)}, f32[64,1024]{1,0:T(8,128)}, f32[8,64]{1,0:T(8,128)}) custom-call(bf16[1024,384]{1,0:T(8,128)(2,1)} %get-tuple-element.118.refs_19_.refs_0_, bf16[1024,384]{1,0:T(8,128)(2,1)} %get-tuple-element.124.refs_21_.refs_1_, bf16[1024,384]{1,0:T(8,128)(2,1)} %get-tuple-element.132.refs_20_.refs_2_, ...), custom_call_target="tpu_custom_call" | custom-call | flops 6442450944 | bytes 33554432 | tf_op jit(solution)/shard_map/tail/pallas_call | solution.py:631
  450.0 4.8 %copy.148 = f32[1024,1024]{1,0:T(8,128)} copy(f32[1024,1024]{1,0:T(8,128)} %get-tuple-element.394) | data formatting | bytes 8388608
  (456 shorter events, 139.1 us)
Async XLA Ops:
  6.6 22.3 %collective-permute-start.1 = (bf16[1024,256]{1,0:T(8,128)(2,1)S(1)}, bf16[1024,256]{1,0:T(8,128)(2,1)S(1)}, u32[]{:S(2)}, u32[]{:S(2)}) collective-permute-start(bf16[1024,256]{1,0:T(8,128)(2,1)S(1)} %fusion.53.refs_1_.refs_5_.refs_4_.refs_8_), channel_id=1, source_target_pairs={{0,4},{2,6},{4,0},{6,2},{8,12},{10,14},{12,8},{14,10},{16,20},{18,... | collective-permute-start | bytes 1572872 | tf_op jit(solution)/shard_map/ppermute | solution.py:30
  9.6 28.9 %collective-permute-start = (bf16[1024,256]{1,0:T(8,128)(2,1)S(1)}, bf16[1024,256]{1,0:T(8,128)(2,1)}, u32[]{:S(2)}, u32[]{:S(2)}) collective-permute-start(bf16[1024,256]{1,0:T(8,128)(2,1)S(1)} %fusion.53.refs_1_.refs_5_.refs_4_.refs_8_), channel_id=1, source_target_pairs={{0,2},{2,0},{4,6},{6,4},{8,10},{10,8},{12,14},{14,12},{16,18},{18,... | collective-permute-start | bytes 1572872 | tf_op jit(solution)/shard_map/ppermute | solution.py:30
  12.1 51.1 %copy-start.5 = (bf16[1024,256]{1,0:T(8,128)(2,1)}, bf16[1024,256]{1,0:T(8,128)(2,1)S(1)}, u32[]{:S(2)}) copy-start(bf16[1024,256]{1,0:T(8,128)(2,1)S(1)} %fusion.52.refs_1_.refs_5_.refs_4_.refs_8_) | copy-start | bytes 1572868
  12.1 27.9 %collective-permute-start.4 = (bf16[1024,256]{1,0:T(8,128)(2,1)S(1)}, bf16[1024,256]{1,0:T(8,128)(2,1)S(1)}, u32[]{:S(2)}, u32[]{:S(2)}) collective-permute-start(bf16[1024,256]{1,0:T(8,128)(2,1)S(1)} %fusion.52.refs_1_.refs_5_.refs_4_.refs_8_), channel_id=1, source_target_pairs={{0,4},{2,6},{4,0},{6,2},{8,12},{10,14},{12,8},{14,10},{16,20},{18,... | collective-permute-start | bytes 1572872 | tf_op jit(solution)/shard_map/ppermute | solution.py:30
  12.3 43.6 %collective-permute-start.3 = (bf16[1024,256]{1,0:T(8,128)(2,1)S(1)}, bf16[1024,256]{1,0:T(8,128)(2,1)S(1)}, u32[]{:S(2)}, u32[]{:S(2)}) collective-permute-start(bf16[1024,256]{1,0:T(8,128)(2,1)S(1)} %fusion.52.refs_1_.refs_5_.refs_4_.refs_8_), channel_id=1, source_target_pairs={{0,2},{2,0},{4,6},{6,4},{8,10},{10,8},{12,14},{14,12},{16,18},{18,... | collective-permute-start | bytes 1572872 | tf_op jit(solution)/shard_map/ppermute | solution.py:30
  14.8 20.0 %collective-permute-start.10 = (bf16[1024,384]{1,0:T(8,128)(2,1)}, bf16[1024,384]{1,0:T(8,128)(2,1)}, u32[]{:S(2)}, u32[]{:S(2)}) collective-permute-start(bf16[1024,384]{1,0:T(8,128)(2,1)} %pad_maximum_fusion.4), channel_id=1, source_target_pairs={{0,1},{1,0},{2,3},{3,2},{4,5},{5,4},{6,7},{7,6},{8,9},{9,8},{10,11... | collective-permute-start | bytes 2359304 | tf_op jit(solution)/shard_map/ppermute | solution.py:30
  19.0 75.0 %copy-start.4 = (bf16[1024,256]{1,0:T(8,128)(2,1)}, bf16[1024,256]{1,0:T(8,128)(2,1)S(1)}, u32[]{:S(2)}) copy-start(bf16[1024,256]{1,0:T(8,128)(2,1)S(1)} %fusion.50.refs_1_.refs_5_.refs_4_.refs_8_) | copy-start | bytes 1572868
  28.8 65.1 %copy-start.20 = (bf16[1024,512]{1,0:T(8,128)(2,1)}, bf16[1024,512]{1,0:T(8,128)(2,1)S(1)}, u32[]{:S(2)}) copy-start(bf16[1024,512]{1,0:T(8,128)(2,1)S(1)} %add_convert_fusion.2.refs_0_) | copy-start | bytes 3145732
  28.9 11.7 %collective-permute-start.2 = (bf16[1024,256]{1,0:T(8,128)(2,1)S(1)}, bf16[1024,256]{1,0:T(8,128)(2,1)S(1)}, u32[]{:S(2)}, u32[]{:S(2)}) collective-permute-start(bf16[1024,256]{1,0:T(8,128)(2,1)S(1)} %collective-permute-done.1.refs_3_.refs_7_.refs_6_.refs_10_), channel_id=1, source_target_pairs={{0,2},{2,0},{4,6},{6,4},{8,10},{10,8},{12,14},{14,12},{16,18},{18,... | collective-permute-start | bytes 1572872 | tf_op jit(solution)/shard_map/ppermute | solution.py:30
  29.7 47.6 %copy-start.13 = (bf16[1024,256]{1,0:T(8,128)(2,1)}, bf16[1024,256]{1,0:T(8,128)(2,1)S(1)}, u32[]{:S(2)}) copy-start(bf16[1024,256]{1,0:T(8,128)(2,1)S(1)} %fusion.51.refs_1_.refs_5_.refs_4_.refs_8_) | copy-start | bytes 1572868
  34.8 42.6 %collective-permute-start.6 = (bf16[512,1024]{1,0:T(8,128)(2,1)S(1)}, bf16[512,1024]{1,0:T(8,128)(2,1)S(1)}, u32[]{:S(2)}, u32[]{:S(2)}) collective-permute-start(bf16[512,1024]{1,0:T(8,128)(2,1)S(1)} %copy-done.109), channel_id=1, source_target_pairs={{0,1},{1,0},{2,3},{3,2},{4,5},{5,4},{6,7},{7,6},{8,9},{9,8},{10,11... | collective-permute-start | bytes 3145736 | tf_op jit(solution)/shard_map/ppermute | solution.py:30
  38.5 17.8 %collective-permute-start.8 = (bf16[1024,256]{1,0:T(8,128)(2,1)S(1)}, bf16[1024,256]{1,0:T(8,128)(2,1)S(1)}, u32[]{:S(2)}, u32[]{:S(2)}) collective-permute-start(bf16[1024,256]{1,0:T(8,128)(2,1)S(1)} %fusion.51.refs_1_.refs_5_.refs_4_.refs_8_), channel_id=1, source_target_pairs={{0,4},{2,6},{4,0},{6,2},{8,12},{10,14},{12,8},{14,10},{16,20},{18,... | collective-permute-start | bytes 1572872 | tf_op jit(solution)/shard_map/ppermute | solution.py:30
  40.0 22.7 %collective-permute-start.12 = (bf16[1024,256]{1,0:T(8,128)(2,1)S(1)}, bf16[1024,256]{1,0:T(8,128)(2,1)S(1)}, u32[]{:S(2)}, u32[]{:S(2)}) collective-permute-start(bf16[1024,256]{1,0:T(8,128)(2,1)S(1)} %fusion.50.refs_1_.refs_5_.refs_4_.refs_8_), channel_id=1, source_target_pairs={{0,4},{2,6},{4,0},{6,2},{8,12},{10,14},{12,8},{14,10},{16,20},{18,... | collective-permute-start | bytes 1572872 | tf_op jit(solution)/shard_map/ppermute | solution.py:30
  40.5 22.2 %collective-permute-start.5 = (bf16[1024,256]{1,0:T(8,128)(2,1)S(1)}, bf16[1024,256]{1,0:T(8,128)(2,1)S(1)}, u32[]{:S(2)}, u32[]{:S(2)}) collective-permute-start(bf16[1024,256]{1,0:T(8,128)(2,1)S(1)} %collective-permute-done.4.refs_3_.refs_7_.refs_6_.refs_10_), channel_id=1, source_target_pairs={{0,2},{2,0},{4,6},{6,4},{8,10},{10,8},{12,14},{14,12},{16,18},{18,... | collective-permute-start | bytes 1572872 | tf_op jit(solution)/shard_map/ppermute | solution.py:30
  55.9 21.4 %collective-permute-start.7 = (bf16[1024,256]{1,0:T(8,128)(2,1)S(1)}, bf16[1024,256]{1,0:T(8,128)(2,1)S(1)}, u32[]{:S(2)}, u32[]{:S(2)}) collective-permute-start(bf16[1024,256]{1,0:T(8,128)(2,1)S(1)} %fusion.51.refs_1_.refs_5_.refs_4_.refs_8_), channel_id=1, source_target_pairs={{0,2},{2,0},{4,6},{6,4},{8,10},{10,8},{12,14},{14,12},{16,18},{18,... | collective-permute-start | bytes 1572872 | tf_op jit(solution)/shard_map/ppermute | solution.py:30
  56.3 37.6 %collective-permute-start.11 = (bf16[1024,256]{1,0:T(8,128)(2,1)S(1)}, bf16[1024,256]{1,0:T(8,128)(2,1)S(1)}, u32[]{:S(2)}, u32[]{:S(2)}) collective-permute-start(bf16[1024,256]{1,0:T(8,128)(2,1)S(1)} %fusion.50.refs_1_.refs_5_.refs_4_.refs_8_), channel_id=1, source_target_pairs={{0,2},{2,0},{4,6},{6,4},{8,10},{10,8},{12,14},{14,12},{16,18},{18,... | collective-permute-start | bytes 1572872 | tf_op jit(solution)/shard_map/ppermute | solution.py:30
  62.7 14.6 %collective-permute-start.9 = (bf16[1024,256]{1,0:T(8,128)(2,1)S(1)}, bf16[1024,256]{1,0:T(8,128)(2,1)S(1)}, u32[]{:S(2)}, u32[]{:S(2)}) collective-permute-start(bf16[1024,256]{1,0:T(8,128)(2,1)S(1)} %collective-permute-done.8.refs_3_.refs_7_.refs_6_.refs_10_), channel_id=1, source_target_pairs={{0,2},{2,0},{4,6},{6,4},{8,10},{10,8},{12,14},{14,12},{16,18},{18,... | collective-permute-start | bytes 1572872 | tf_op jit(solution)/shard_map/ppermute | solution.py:30
  62.7 31.2 %collective-permute-start.13 = (bf16[1024,256]{1,0:T(8,128)(2,1)S(1)}, bf16[1024,256]{1,0:T(8,128)(2,1)S(1)}, u32[]{:S(2)}, u32[]{:S(2)}) collective-permute-start(bf16[1024,256]{1,0:T(8,128)(2,1)S(1)} %collective-permute-done.12.refs_3_.refs_7_.refs_6_.refs_10_), channel_id=1, source_target_pairs={{0,2},{2,0},{4,6},{6,4},{8,10},{10,8},{12,14},{14,12},{16,18},{18,... | collective-permute-start | bytes 1572872 | tf_op jit(solution)/shard_map/ppermute | solution.py:30
  91.1 18.7 %collective-permute-start.14 = (bf16[1024,128]{1,0:T(8,128)(2,1)S(1)}, bf16[1024,128]{1,0:T(8,128)(2,1)S(1)}, u32[]{:S(2)}, u32[]{:S(2)}) collective-permute-start(bf16[1024,128]{1,0:T(8,128)(2,1)S(1)} %get-tuple-element.272), channel_id=1, source_target_pairs={{0,1},{1,0},{2,3},{3,2},{4,5},{5,4},{6,7},{7,6},{8,9},{9,8},{10,11... | collective-permute-start | bytes 786440 | tf_op jit(solution)/shard_map/ppermute | solution.py:30
  91.6 18.3 %collective-permute-start.15 = (bf16[1024,128]{1,0:T(8,128)(2,1)S(1)}, bf16[1024,128]{1,0:T(8,128)(2,1)S(1)}, u32[]{:S(2)}, u32[]{:S(2)}) collective-permute-start(bf16[1024,128]{1,0:T(8,128)(2,1)S(1)} %get-tuple-element.270), channel_id=1, source_target_pairs={{0,1},{1,0},{2,3},{3,2},{4,5},{5,4},{6,7},{7,6},{8,9},{9,8},{10,11... | collective-permute-start | bytes 786440 | tf_op jit(solution)/shard_map/ppermute | solution.py:30
  93.6 17.9 %collective-permute-start.16 = (bf16[1024,128]{1,0:T(8,128)(2,1)S(1)}, bf16[1024,128]{1,0:T(8,128)(2,1)S(1)}, u32[]{:S(2)}, u32[]{:S(2)}) collective-permute-start(bf16[1024,128]{1,0:T(8,128)(2,1)S(1)} %get-tuple-element.268), channel_id=1, source_target_pairs={{0,1},{1,0},{2,3},{3,2},{4,5},{5,4},{6,7},{7,6},{8,9},{9,8},{10,11... | collective-permute-start | bytes 786440 | tf_op jit(solution)/shard_map/ppermute | solution.py:30
  108.0 8.3 %collective-permute-start.17 = (bf16[1024,128]{1,0:T(8,128)(2,1)S(1)}, bf16[1024,128]{1,0:T(8,128)(2,1)S(1)}, u32[]{:S(2)}, u32[]{:S(2)}) collective-permute-start(bf16[1024,128]{1,0:T(8,128)(2,1)S(1)} %get-tuple-element.266), channel_id=1, source_target_pairs={{0,1},{1,0},{2,3},{3,2},{4,5},{5,4},{6,7},{7,6},{8,9},{9,8},{10,11... | collective-permute-start | bytes 786440 | tf_op jit(solution)/shard_map/ppermute | solution.py:30
  124.4 19.2 %collective-permute-start.18 = (bf16[256,1024]{1,0:T(8,128)(2,1)S(1)}, bf16[256,1024]{1,0:T(8,128)(2,1)S(1)}, u32[]{:S(2)}, u32[]{:S(2)}) collective-permute-start(bf16[256,1024]{1,0:T(8,128)(2,1)S(1)} %convolution_convert_fusion.8), channel_id=1, source_target_pairs={{0,1},{1,0},{2,3},{3,2},{4,5},{5,4},{6,7},{7,6},{8,9},{9,8},{10,11... | collective-permute-start | bytes 1572872 | tf_op jit(solution)/shard_map/ppermute | solution.py:30
  135.7 26.1 %collective-permute-start.19 = (bf16[512,1024]{1,0:T(8,128)(2,1)S(1)}, bf16[512,1024]{1,0:T(8,128)(2,1)S(1)}, u32[]{:S(2)}, u32[]{:S(2)}) collective-permute-start(bf16[512,1024]{1,0:T(8,128)(2,1)S(1)} %convolution_convert_fusion.4), channel_id=1, source_target_pairs={{0,1},{1,0},{2,3},{3,2},{4,5},{5,4},{6,7},{7,6},{8,9},{9,8},{10,11... | collective-permute-start | bytes 3145736 | tf_op jit(solution)/shard_map/ppermute | solution.py:30
  138.0 38.1 %copy-start.25 = (f32[256,1024]{1,0:T(8,128)}, f32[256,1024]{1,0:T(8,128)S(1)}, u32[]{:S(2)}) copy-start(f32[256,1024]{1,0:T(8,128)S(1)} %get-tuple-element.371) | copy-start | bytes 3145732
  142.6 33.4 %collective-permute-start.20 = (bf16[256,1024]{1,0:T(8,128)(2,1)S(1)}, bf16[256,1024]{1,0:T(8,128)(2,1)S(1)}, u32[]{:S(2)}, u32[]{:S(2)}) collective-permute-start(bf16[256,1024]{1,0:T(8,128)(2,1)S(1)} %convolution_convert_fusion.7), channel_id=1, source_target_pairs={{0,1},{1,0},{2,3},{3,2},{4,5},{5,4},{6,7},{7,6},{8,9},{9,8},{10,11... | collective-permute-start | bytes 1572872 | tf_op jit(solution)/shard_map/ppermute | solution.py:30
  151.8 75.6 %collective-permute-start.21 = (bf16[256,1024]{1,0:T(8,128)(2,1)}, bf16[256,1024]{1,0:T(8,128)(2,1)}, u32[]{:S(2)}, u32[]{:S(2)}) collective-permute-start(bf16[256,1024]{1,0:T(8,128)(2,1)} %convolution_convert_fusion.6), channel_id=1, source_target_pairs={{0,1},{1,0},{2,3},{3,2},{4,5},{5,4},{6,7},{7,6},{8,9},{9,8},{10,11... | collective-permute-start | bytes 1572872 | tf_op jit(solution)/shard_map/ppermute | solution.py:30
  188.0 36.5 %collective-permute-start.23 = (bf16[512,1024]{1,0:T(8,128)(2,1)}, bf16[512,1024]{1,0:T(8,128)(2,1)}, u32[]{:S(2)}, u32[]{:S(2)}) collective-permute-start(bf16[512,1024]{1,0:T(8,128)(2,1)} %convolution_convert_fusion.3), channel_id=1, source_target_pairs={{0,1},{1,0},{2,3},{3,2},{4,5},{5,4},{6,7},{7,6},{8,9},{9,8},{10,11... | collective-permute-start | bytes 3145736 | tf_op jit(solution)/shard_map/ppermute | solution.py:30
  189.2 35.3 %collective-permute-start.24 = (bf16[256,1024]{1,0:T(8,128)(2,1)}, bf16[256,1024]{1,0:T(8,128)(2,1)}, u32[]{:S(2)}, u32[]{:S(2)}) collective-permute-start(bf16[256,1024]{1,0:T(8,128)(2,1)} %convolution_convert_fusion.5), channel_id=1, source_target_pairs={{0,1},{1,0},{2,3},{3,2},{4,5},{5,4},{6,7},{7,6},{8,9},{9,8},{10,11... | collective-permute-start | bytes 1572872 | tf_op jit(solution)/shard_map/ppermute | solution.py:30
  199.9 19.2 %collective-permute-start.22 = (bf16[512,2048]{1,0:T(8,128)(2,1)}, bf16[512,2048]{1,0:T(8,128)(2,1)}, u32[]{:S(2)}, u32[]{:S(2)}) collective-permute-start(bf16[512,2048]{1,0:T(8,128)(2,1)} %bitcast.9), channel_id=1, source_target_pairs={{0,2},{2,0},{4,6},{6,4},{8,10},{10,8},{12,14},{14,12},{16,18},{18,... | collective-permute-start | bytes 6291464 | tf_op jit(solution)/shard_map/ppermute | solution.py:30
  217.1 28.7 %collective-permute-start.25 = (bf16[512,2048]{1,0:T(8,128)(2,1)}, bf16[512,2048]{1,0:T(8,128)(2,1)}, u32[]{:S(2)}, u32[]{:S(2)}) collective-permute-start(bf16[512,2048]{1,0:T(8,128)(2,1)} %bitcast.13), channel_id=1, source_target_pairs={{0,2},{2,0},{4,6},{6,4},{8,10},{10,8},{12,14},{14,12},{16,18},{18,... | collective-permute-start | bytes 6291464 | tf_op jit(solution)/shard_map/ppermute | solution.py:30
  325.5 40.3 %copy-start.99 = (f32[2,1,1,512]{3,2,1,0:T(1,128)}, f32[2,1,1,512]{3,2,1,0:T(1,128)S(1)}, u32[]{:S(2)}) copy-start(f32[2,1,1,512]{3,2,1,0:T(1,128)S(1)} %get-tuple-element.344) | copy-start | bytes 12292
  (111 other events, 922.2 us)

commit v6 on v5

--- a/solution.py
+++ b/solution.py
@@ -711,7 +711,7 @@
 
     outs, own_context, other_context = [], [], []
     across = ("tensor", 0)
-    ahead = jnp.concatenate([weights[1][2], *weights[3][:2]], axis=1)
+    ahead = jnp.concatenate([*weights[1][1:], *weights[3][:2]], axis=1)
     ahead = flip(ahead, "tensor", 0)
     for group in range(groups):
         if group > 0:
@@ -836,9 +836,9 @@
     early_scatter = Scatter(jnp.concatenate([part for part, _ in early], axis=1), F32)
 
     tokens_turned = tokens.T
-    trips = [[(0, 0), (0, 1), (2, 0), (1, 1)], [(1, 0)], [(2, 1)], [(2, 2)]]
-    ahead = [ahead[:, i * LANES : (i + 1) * LANES] for i in range(3)]
-    other_weights = [[None] * 2, [None, None, ahead[0]], [None] * 3, ahead[1:]]
+    trips = [[(0, 0), (0, 1), (2, 0)], [(1, 0)], [(2, 1)], [(2, 2)]]
+    ahead = [ahead[:, i * LANES : (i + 1) * LANES] for i in range(4)]
+    other_weights = [[None] * 2, [None, *ahead[:2]], [None] * 3, ahead[2:]]
     joined, others, sums, proj_scatters = [], [], [], []
     active = [up_scatter, out_scatter, early_scatter, down_parts[0]]
     for group in range(groups):

time: 459 us -> 457 us (level)
    unnamed x245 -> x239, local copies, waits for them, and re-layouts: 24.1 us -> 24.2 us
  transfers between devices with their start and end apart: 26 -> 26, of which waited for: 5 -> 4; matrix products, arithmetic and copies ran while one was open for 26% -> 26% of each run, Pallas kernels for 12% -> 12%
where the time goes in v6:
time: 457 us; the launch traced here: 453 us
  Pallas kernels  212 us (46%)
  matrix products  69 us (15%)
  other arithmetic  69 us (15%)
  local copies, waits for them, and re-layouts  51 us (11%)
  waiting for transfers between devices  27.4 us (6%)
  starting transfers between devices  21.7 us (5%)
    pallas_call x4, Pallas kernels, attend_back(): pl.pallas_call(functools.partial(backward_kernel, scale, span // 2, links...  124 us
    dot_general x27, matrix products, dot(): return lax.dot_general(left, right, dims, preferred_element_type=F32)  69 us
    pallas_call x4, Pallas kernels, attend(): pl.pallas_call(functools.partial(forward_kernel, scale, span // 2), grid=...  56.2 us
    pallas_call x1, Pallas kernels, tail(): pl.pallas_call(functools.partial(tail_kernel, plans, widths, [chains.inde...  31.8 us
    ppermute x26, waiting for transfers between devices, flip(): return lax.ppermute(value, axis, pairs)  27.4 us
    unnamed x239, local copies, waits for them, and re-layouts  24.2 us
    ppermute x26, starting transfers between devices, flip(): return lax.ppermute(value, axis, pairs)  21.7 us
    add x14, other arithmetic, land(): self.split([a.astype(F32) + b.astype(F32) for a, b in zip(kept, sent)])  17 us
  transfers between devices with their start and end apart: 26, of which 4 were waited for; matrix products, arithmetic and copies ran while one was open for 26% of the time, Pallas kernels for 12%

profile of v6, /device:TPU:0, one launch (start us, length us, event | category | flops | bytes accessed | tf_op | source)
XLA Modules:
  0.0 452.9 jit_solution(6935912734371842420)
XLA Ops:
  0.7 3.0 slice_bitcast_fusion.2
  6.6 3.0 collective-permute-start.1
  23.6 4.3 copy.79
  29.9 3.2 add_convert_fusion.2.refs_0_
  35.8 14.3 %attend.4 = (f32[1024,128]{1,0:T(8,128)S(1)}, f32[2,1024]{1,0:T(2,128)S(1)}) custom-call(bf16[1024,512]{1,0:T(8,128)(2,1)S(1)} %add_convert_fusion.2.refs_0_, bf16[1024,256]{1,0:T(8,128)(2,1)S(1)} %copy-done.10, bf16[1024,256]{1,0:T(8,128)(2,1)} %collective-permute-done.refs_2_.refs_6_.refs_5_.refs_9_, ...), custom_call_target="tpu_custom_call" | custom-call | flops 8589934592 | bytes 3145728 | tf_op jit(solution)/shard_map/attend/pallas_call | solution.py:209
  52.8 14.6 %attend.5 = (f32[1024,128]{1,0:T(8,128)S(1)}, f32[2,1024]{1,0:T(2,128)S(1)}) custom-call(bf16[1024,512]{1,0:T(8,128)(2,1)S(1)} %add_convert_fusion.2.refs_0_, bf16[1024,256]{1,0:T(8,128)(2,1)S(1)} %fusion.52.refs_1_.refs_5_.refs_4_.refs_8_, bf16[1024,256]{1,0:T(8,128)(2,1)} %collective-permute-done.3.refs_2_.refs_6_.refs_5_.refs_9_, ...), custom_call_target="tpu_custom_call" | custom-call | flops 8589934592 | bytes 3145728 | tf_op jit(solution)/shard_map/attend/pallas_call | solution.py:209
  68.7 13.5 %attend.6 = (f32[1024,128]{1,0:T(8,128)S(1)}, f32[2,1024]{1,0:T(2,128)S(1)}) custom-call(bf16[1024,512]{1,0:T(8,128)(2,1)S(1)} %add_convert_fusion.2.refs_0_, bf16[1024,256]{1,0:T(8,128)(2,1)S(1)} %fusion.51.refs_1_.refs_5_.refs_4_.refs_8_, bf16[1024,256]{1,0:T(8,128)(2,1)S(1)} %collective-permute-done.7.refs_2_.refs_6_.refs_5_.refs_9_, ...), custom_call_target="tpu_custom_call" | custom-call | flops 8589934592 | bytes 3145728 | tf_op jit(solution)/shard_map/attend/pallas_call | solution.py:209
  82.3 11.0 %collective-permute-done.10 = bf16[1024,512]{1,0:T(8,128)(2,1)S(1)} collective-permute-done((bf16[1024,512]{1,0:T(8,128)(2,1)S(1)}, bf16[1024,512]{1,0:T(8,128)(2,1)S(1)}, u32[]{:S(2)}, u32[]{:S(2)}) %collective-permute-start.10) | collective-permute-done | bytes 1048608 | tf_op jit(solution)/shard_map/ppermute | solution.py:30
  96.4 13.7 %attend.7 = (f32[1024,128]{1,0:T(8,128)S(1)}, f32[2,1024]{1,0:T(2,128)S(1)}) custom-call(bf16[1024,512]{1,0:T(8,128)(2,1)S(1)} %add_convert_fusion.2.refs_0_, bf16[1024,256]{1,0:T(8,128)(2,1)S(1)} %fusion.50.refs_1_.refs_5_.refs_4_.refs_8_, bf16[1024,256]{1,0:T(8,128)(2,1)S(1)} %collective-permute-done.11.refs_2_.refs_6_.refs_5_.refs_9_, ...), custom_call_target="tpu_custom_call" | custom-call | flops 8589934592 | bytes 3145728 | tf_op jit(solution)/shard_map/attend/pallas_call | solution.py:209
  113.5 4.3 collective-permute-done.17
  130.5 3.3 multiply_convert_fusion
  153.5 10.7 %collective-permute-done.19 = bf16[512,1024]{1,0:T(8,128)(2,1)S(1)} collective-permute-done((bf16[512,1024]{1,0:T(8,128)(2,1)S(1)}, bf16[512,1024]{1,0:T(8,128)(2,1)S(1)}, u32[]{:S(2)}, u32[]{:S(2)}) %collective-permute-start.19) | collective-permute-done | bytes 1048608 | tf_op jit(solution)/shard_map/ppermute | solution.py:30
  169.9 5.3 %fusion.6 = bf16[512,2048]{1,0:T(8,128)(2,1)S(1)} fusion(f32[512,2048]{1,0:T(8,128)S(1)} %get-tuple-element.368, f32[2048]{0:T(1024)S(1)} %add.816, bf16[512,1024]{1,0:T(8,128)(2,1)S(1)} %add_convert_fusion.3, bf16[2048,1024]{1,0:T(8,128)(2,1)S(1)} %copy-done.105), kind=kOutput, calls=%fused_computation.8 | convolution fusion | flops 2169503744 | bytes 11542528 | tf_op jit(solution)/shard_map/dot_general | solution.py:25
  175.1 3.4 convolution_convert_fusion.3
  182.1 2.4 fusion.32
  184.5 2.4 pad_maximum_fusion
  192.6 7.4 %fusion.13 = bf16[1024,2048]{1,0:T(8,128)(2,1)S(1)} fusion(bf16[1024,1024]{1,0:T(8,128)(2,1)} %pad_maximum_fusion.2, bf16[256,2048]{1,0:T(8,128)(2,1)} %copy-done.111, bf16[512,2048]{1,0:T(8,128)(2,1)} %copy-done.112, bf16[256,2048]{1,0:T(8,128)(2,1)} %copy-done.110), kind=kOutput, calls=%fused_computation.18 | convolution fusion | flops 4309647360 | bytes 10485760 | tf_op jit(solution)/shard_map/dot_general | solution.py:25
  200.0 2.4 constant_dynamic-slice_fusion.20
  202.5 2.8 convolution_reduce_fusion
  209.5 7.6 %convolution_convert_fusion = bf16[1024,2048]{1,0:T(8,128)(2,1)S(1)} fusion(bf16[1024,2048]{1,0:T(8,128)(2,1)} %pad_maximum_fusion, bf16[256,1024]{1,0:T(8,128)(2,1)} %copy-done.76, bf16[512,1024]{1,0:T(8,128)(2,1)} %copy-done.49, bf16[256,1024]{1,0:T(8,128)(2,1)} %copy-done.75), kind=kOutput, calls=%fused_computation.19 | convolution fusion | flops 4303355904 | bytes 10485760 | tf_op jit(solution)/shard_map/dot_general | solution.py:25
  217.2 2.4 constant_dynamic-slice_fusion.18
  222.5 4.6 %convert_add_fusion = f32[512,2048]{1,0:T(8,128)} fusion(bf16[512,2048]{1,0:T(8,128)(2,1)} %collective-permute-done.22, bf16[8,1,64,2048]{3,2,1,0:T(8,128)(2,1)S(1)} %copy-done.35), kind=kLoop, calls=%fused_computation.16 | loop fusion | flops 3145728 | bytes 8388608 | tf_op jit(solution)/shard_map/add | solution.py:103
  227.1 2.8 multiply_reduce_fusion
  229.9 2.5 multiply_reduce_fusion.5
  241.8 2.5 convolution_convert_fusion.1
  251.2 3.2 convert_add_fusion.1
  254.5 31.1 %attend_back.4 = (bf16[1024,384]{1,0:T(8,128)(2,1)}, f32[1,384]{1,0:T(1,128)}, bf16[512,384]{1,0:T(8,128)(2,1)}, bf16[512,384]{1,0:T(8,128)(2,1)}, bf16[256,2048...) custom-call(bf16[1024,512]{1,0:T(8,128)(2,1)} %copy-done.17, ...), custom_call_target="tpu_custom_call" | custom-call | flops 15032385536 | bytes 5767168 | tf_op jit(solution)/shard_map/attend_back/pallas_call | solution.py:403
  291.3 31.7 %attend_back.5 = (bf16[1024,384]{1,0:T(8,128)(2,1)}, f32[1,384]{1,0:T(1,128)}, bf16[512,384]{1,0:T(8,128)(2,1)}, bf16[512,384]{1,0:T(8,128)(2,1)}, bf16[128,2048...) custom-call(bf16[1024,512]{1,0:T(8,128)(2,1)} %copy-done.17, ...), custom_call_target="tpu_custom_call" | custom-call | flops 15032385536 | bytes 5767168 | tf_op jit(solution)/shard_map/attend_back/pallas_call | solution.py:403
  329.4 30.7 %attend_back.6 = (bf16[1024,384]{1,0:T(8,128)(2,1)}, f32[1,384]{1,0:T(1,128)}, bf16[512,384]{1,0:T(8,128)(2,1)}, bf16[512,384]{1,0:T(8,128)(2,1)}, bf16[64,2048]...) custom-call(bf16[1024,512]{1,0:T(8,128)(2,1)} %copy-done.17, ...), custom_call_target="tpu_custom_call" | custom-call | flops 15032385536 | bytes 5767168 | tf_op jit(solution)/shard_map/attend_back/pallas_call | solution.py:403
  366.4 30.9 %attend_back.7 = (bf16[1024,384]{1,0:T(8,128)(2,1)}, f32[1,384]{1,0:T(1,128)}, bf16[512,384]{1,0:T(8,128)(2,1)}, bf16[512,384]{1,0:T(8,128)(2,1)}, bf16[64,512]{...) custom-call(bf16[1024,512]{1,0:T(8,128)(2,1)} %copy-done.17, ...), custom_call_target="tpu_custom_call" | custom-call | flops 15032385536 | bytes 5767168 | tf_op jit(solution)/shard_map/attend_back/pallas_call | solution.py:403
  410.3 31.8 %tail.1 = (f32[1024,1024]{1,0:T(8,128)}, f32[64,1536]{1,0:T(8,128)}, f32[64,1024]{1,0:T(8,128)}, f32[8,64]{1,0:T(8,128)}) custom-call(bf16[1024,384]{1,0:T(8,128)(2,1)} %get-tuple-element.117.refs_19_.refs_0_, bf16[1024,384]{1,0:T(8,128)(2,1)} %get-tuple-element.123.refs_21_.refs_1_, bf16[1024,384]{1,0:T(8,128)(2,1)} %get-tuple-element.131.refs_20_.refs_2_, ...), custom_call_target="tpu_custom_call" | custom-call | flops 6442450944 | bytes 33554432 | tf_op jit(solution)/shard_map/tail/pallas_call | solution.py:631
  447.9 4.8 %copy.148 = f32[1024,1024]{1,0:T(8,128)} copy(f32[1024,1024]{1,0:T(8,128)} %get-tuple-element.393) | data formatting | bytes 8388608
  (450 shorter events, 138.8 us)
Async XLA Ops:
  6.6 15.9 %collective-permute-start.1 = (bf16[1024,256]{1,0:T(8,128)(2,1)S(1)}, bf16[1024,256]{1,0:T(8,128)(2,1)}, u32[]{:S(2)}, u32[]{:S(2)}) collective-permute-start(bf16[1024,256]{1,0:T(8,128)(2,1)S(1)} %fusion.53.refs_1_.refs_5_.refs_4_.refs_8_), channel_id=1, source_target_pairs={{0,4},{2,6},{4,0},{6,2},{8,12},{10,14},{12,8},{14,10},{16,20},{18,... | collective-permute-start | bytes 1572872 | tf_op jit(solution)/shard_map/ppermute | solution.py:30
  9.6 23.5 %collective-permute-start = (bf16[1024,256]{1,0:T(8,128)(2,1)S(1)}, bf16[1024,256]{1,0:T(8,128)(2,1)}, u32[]{:S(2)}, u32[]{:S(2)}) collective-permute-start(bf16[1024,256]{1,0:T(8,128)(2,1)S(1)} %fusion.53.refs_1_.refs_5_.refs_4_.refs_8_), channel_id=1, source_target_pairs={{0,2},{2,0},{4,6},{6,4},{8,10},{10,8},{12,14},{14,12},{16,18},{18,... | collective-permute-start | bytes 1572872 | tf_op jit(solution)/shard_map/ppermute | solution.py:30
  12.1 40.7 %copy-start.7 = (bf16[1024,256]{1,0:T(8,128)(2,1)}, bf16[1024,256]{1,0:T(8,128)(2,1)S(1)}, u32[]{:S(2)}) copy-start(bf16[1024,256]{1,0:T(8,128)(2,1)S(1)} %fusion.52.refs_1_.refs_5_.refs_4_.refs_8_) | copy-start | bytes 1572868
  12.1 21.6 %collective-permute-start.4 = (bf16[1024,256]{1,0:T(8,128)(2,1)S(1)}, bf16[1024,256]{1,0:T(8,128)(2,1)S(1)}, u32[]{:S(2)}, u32[]{:S(2)}) collective-permute-start(bf16[1024,256]{1,0:T(8,128)(2,1)S(1)} %fusion.52.refs_1_.refs_5_.refs_4_.refs_8_), channel_id=1, source_target_pairs={{0,4},{2,6},{4,0},{6,2},{8,12},{10,14},{12,8},{14,10},{16,20},{18,... | collective-permute-start | bytes 1572872 | tf_op jit(solution)/shard_map/ppermute | solution.py:30
  12.3 38.5 %collective-permute-start.3 = (bf16[1024,256]{1,0:T(8,128)(2,1)S(1)}, bf16[1024,256]{1,0:T(8,128)(2,1)}, u32[]{:S(2)}, u32[]{:S(2)}) collective-permute-start(bf16[1024,256]{1,0:T(8,128)(2,1)S(1)} %fusion.52.refs_1_.refs_5_.refs_4_.refs_8_), channel_id=1, source_target_pairs={{0,2},{2,0},{4,6},{6,4},{8,10},{10,8},{12,14},{14,12},{16,18},{18,... | collective-permute-start | bytes 1572872 | tf_op jit(solution)/shard_map/ppermute | solution.py:30
  15.2 53.5 %copy-start.5 = (bf16[1024,256]{1,0:T(8,128)(2,1)}, bf16[1024,256]{1,0:T(8,128)(2,1)S(1)}, u32[]{:S(2)}) copy-start(bf16[1024,256]{1,0:T(8,128)(2,1)S(1)} %fusion.51.refs_1_.refs_5_.refs_4_.refs_8_) | copy-start | bytes 1572868
  15.2 37.1 %collective-permute-start.8 = (bf16[1024,256]{1,0:T(8,128)(2,1)S(1)}, bf16[1024,256]{1,0:T(8,128)(2,1)S(1)}, u32[]{:S(2)}, u32[]{:S(2)}) collective-permute-start(bf16[1024,256]{1,0:T(8,128)(2,1)S(1)} %fusion.51.refs_1_.refs_5_.refs_4_.refs_8_), channel_id=1, source_target_pairs={{0,4},{2,6},{4,0},{6,2},{8,12},{10,14},{12,8},{14,10},{16,20},{18,... | collective-permute-start | bytes 1572872 | tf_op jit(solution)/shard_map/ppermute | solution.py:30
  21.2 75.2 %copy-start.4 = (bf16[1024,256]{1,0:T(8,128)(2,1)}, bf16[1024,256]{1,0:T(8,128)(2,1)S(1)}, u32[]{:S(2)}) copy-start(bf16[1024,256]{1,0:T(8,128)(2,1)S(1)} %fusion.50.refs_1_.refs_5_.refs_4_.refs_8_) | copy-start | bytes 1572868
  22.5 13.3 %collective-permute-start.2 = (bf16[1024,256]{1,0:T(8,128)(2,1)}, bf16[1024,256]{1,0:T(8,128)(2,1)}, u32[]{:S(2)}, u32[]{:S(2)}) collective-permute-start(bf16[1024,256]{1,0:T(8,128)(2,1)} %collective-permute-done.1.refs_3_.refs_7_.refs_6_.refs_10_), channel_id=1, source_target_pairs={{0,2},{2,0},{4,6},{6,4},{8,10},{10,8},{12,14},{14,12},{16,18},{18,... | collective-permute-start | bytes 1572872 | tf_op jit(solution)/shard_map/ppermute | solution.py:30
  33.1 63.3 %copy-start.17 = (bf16[1024,512]{1,0:T(8,128)(2,1)}, bf16[1024,512]{1,0:T(8,128)(2,1)S(1)}, u32[]{:S(2)}) copy-start(bf16[1024,512]{1,0:T(8,128)(2,1)S(1)} %add_convert_fusion.2.refs_0_) | copy-start | bytes 3145732
  33.1 35.5 %collective-permute-start.7 = (bf16[1024,256]{1,0:T(8,128)(2,1)S(1)}, bf16[1024,256]{1,0:T(8,128)(2,1)S(1)}, u32[]{:S(2)}, u32[]{:S(2)}) collective-permute-start(bf16[1024,256]{1,0:T(8,128)(2,1)S(1)} %fusion.51.refs_1_.refs_5_.refs_4_.refs_8_), channel_id=1, source_target_pairs={{0,2},{2,0},{4,6},{6,4},{8,10},{10,8},{12,14},{14,12},{16,18},{18,... | collective-permute-start | bytes 1572872 | tf_op jit(solution)/shard_map/ppermute | solution.py:30
  33.7 34.9 %collective-permute-start.6 = (bf16[512,1024]{1,0:T(8,128)(2,1)S(1)}, bf16[512,1024]{1,0:T(8,128)(2,1)S(1)}, u32[]{:S(2)}, u32[]{:S(2)}) collective-permute-start(bf16[512,1024]{1,0:T(8,128)(2,1)S(1)} %copy-done.107), channel_id=1, source_target_pairs={{0,1},{1,0},{2,3},{3,2},{4,5},{5,4},{6,7},{7,6},{8,9},{9,8},{10,11... | collective-permute-start | bytes 3145736 | tf_op jit(solution)/shard_map/ppermute | solution.py:30
  35.8 16.7 %collective-permute-start.5 = (bf16[1024,256]{1,0:T(8,128)(2,1)S(1)}, bf16[1024,256]{1,0:T(8,128)(2,1)S(1)}, u32[]{:S(2)}, u32[]{:S(2)}) collective-permute-start(bf16[1024,256]{1,0:T(8,128)(2,1)S(1)} %collective-permute-done.4.refs_3_.refs_7_.refs_6_.refs_10_), channel_id=1, source_target_pairs={{0,2},{2,0},{4,6},{6,4},{8,10},{10,8},{12,14},{14,12},{16,18},{18,... | collective-permute-start | bytes 1572872 | tf_op jit(solution)/shard_map/ppermute | solution.py:30
  50.8 17.3 %collective-permute-start.12 = (bf16[1024,256]{1,0:T(8,128)(2,1)S(1)}, bf16[1024,256]{1,0:T(8,128)(2,1)S(1)}, u32[]{:S(2)}, u32[]{:S(2)}) collective-permute-start(bf16[1024,256]{1,0:T(8,128)(2,1)S(1)} %fusion.50.refs_1_.refs_5_.refs_4_.refs_8_), channel_id=1, source_target_pairs={{0,4},{2,6},{4,0},{6,2},{8,12},{10,14},{12,8},{14,10},{16,20},{18,... | collective-permute-start | bytes 1572872 | tf_op jit(solution)/shard_map/ppermute | solution.py:30
  52.3 44.1 %collective-permute-start.11 = (bf16[1024,256]{1,0:T(8,128)(2,1)S(1)}, bf16[1024,256]{1,0:T(8,128)(2,1)S(1)}, u32[]{:S(2)}, u32[]{:S(2)}) collective-permute-start(bf16[1024,256]{1,0:T(8,128)(2,1)S(1)} %fusion.50.refs_1_.refs_5_.refs_4_.refs_8_), channel_id=1, source_target_pairs={{0,2},{2,0},{4,6},{6,4},{8,10},{10,8},{12,14},{14,12},{16,18},{18,... | collective-permute-start | bytes 1572872 | tf_op jit(solution)/shard_map/ppermute | solution.py:30
  52.5 16.2 %collective-permute-start.9 = (bf16[1024,256]{1,0:T(8,128)(2,1)S(1)}, bf16[1024,256]{1,0:T(8,128)(2,1)S(1)}, u32[]{:S(2)}, u32[]{:S(2)}) collective-permute-start(bf16[1024,256]{1,0:T(8,128)(2,1)S(1)} %collective-permute-done.8.refs_3_.refs_7_.refs_6_.refs_10_), channel_id=1, source_target_pairs={{0,2},{2,0},{4,6},{6,4},{8,10},{10,8},{12,14},{14,12},{16,18},{18,... | collective-permute-start | bytes 1572872 | tf_op jit(solution)/shard_map/ppermute | solution.py:30
  68.0 25.3 %collective-permute-start.10 = (bf16[1024,512]{1,0:T(8,128)(2,1)S(1)}, bf16[1024,512]{1,0:T(8,128)(2,1)S(1)}, u32[]{:S(2)}, u32[]{:S(2)}) collective-permute-start(bf16[1024,512]{1,0:T(8,128)(2,1)S(1)} %copy-done.50), channel_id=1, source_target_pairs={{0,1},{1,0},{2,3},{3,2},{4,5},{5,4},{6,7},{7,6},{8,9},{9,8},{10,11... | collective-permute-start | bytes 3145736 | tf_op jit(solution)/shard_map/ppermute | solution.py:30
  68.6 27.7 %collective-permute-start.13 = (bf16[1024,256]{1,0:T(8,128)(2,1)S(1)}, bf16[1024,256]{1,0:T(8,128)(2,1)S(1)}, u32[]{:S(2)}, u32[]{:S(2)}) collective-permute-start(bf16[1024,256]{1,0:T(8,128)(2,1)S(1)} %collective-permute-done.12.refs_3_.refs_7_.refs_6_.refs_10_), channel_id=1, source_target_pairs={{0,2},{2,0},{4,6},{6,4},{8,10},{10,8},{12,14},{14,12},{16,18},{18,... | collective-permute-start | bytes 1572872 | tf_op jit(solution)/shard_map/ppermute | solution.py:30
  93.4 19.6 %collective-permute-start.14 = (bf16[1024,128]{1,0:T(8,128)(2,1)S(1)}, bf16[1024,128]{1,0:T(8,128)(2,1)S(1)}, u32[]{:S(2)}, u32[]{:S(2)}) collective-permute-start(bf16[1024,128]{1,0:T(8,128)(2,1)S(1)} %get-tuple-element.270), channel_id=1, source_target_pairs={{0,1},{1,0},{2,3},{3,2},{4,5},{5,4},{6,7},{7,6},{8,9},{9,8},{10,11... | collective-permute-start | bytes 786440 | tf_op jit(solution)/shard_map/ppermute | solution.py:30
  94.0 19.1 %collective-permute-start.15 = (bf16[1024,128]{1,0:T(8,128)(2,1)S(1)}, bf16[1024,128]{1,0:T(8,128)(2,1)S(1)}, u32[]{:S(2)}, u32[]{:S(2)}) collective-permute-start(bf16[1024,128]{1,0:T(8,128)(2,1)S(1)} %get-tuple-element.268), channel_id=1, source_target_pairs={{0,1},{1,0},{2,3},{3,2},{4,5},{5,4},{6,7},{7,6},{8,9},{9,8},{10,11... | collective-permute-start | bytes 786440 | tf_op jit(solution)/shard_map/ppermute | solution.py:30
  95.8 17.6 %collective-permute-start.16 = (bf16[1024,128]{1,0:T(8,128)(2,1)S(1)}, bf16[1024,128]{1,0:T(8,128)(2,1)S(1)}, u32[]{:S(2)}, u32[]{:S(2)}) collective-permute-start(bf16[1024,128]{1,0:T(8,128)(2,1)S(1)} %get-tuple-element.266), channel_id=1, source_target_pairs={{0,1},{1,0},{2,3},{3,2},{4,5},{5,4},{6,7},{7,6},{8,9},{9,8},{10,11... | collective-permute-start | bytes 786440 | tf_op jit(solution)/shard_map/ppermute | solution.py:30
  110.3 7.5 %collective-permute-start.17 = (bf16[1024,128]{1,0:T(8,128)(2,1)S(1)}, bf16[1024,128]{1,0:T(8,128)(2,1)S(1)}, u32[]{:S(2)}, u32[]{:S(2)}) collective-permute-start(bf16[1024,128]{1,0:T(8,128)(2,1)S(1)} %get-tuple-element.264), channel_id=1, source_target_pairs={{0,1},{1,0},{2,3},{3,2},{4,5},{5,4},{6,7},{7,6},{8,9},{9,8},{10,11... | collective-permute-start | bytes 786440 | tf_op jit(solution)/shard_map/ppermute | solution.py:30
  126.9 17.2 %collective-permute-start.18 = (bf16[256,1024]{1,0:T(8,128)(2,1)S(1)}, bf16[256,1024]{1,0:T(8,128)(2,1)S(1)}, u32[]{:S(2)}, u32[]{:S(2)}) collective-permute-start(bf16[256,1024]{1,0:T(8,128)(2,1)S(1)} %convolution_convert_fusion.8), channel_id=1, source_target_pairs={{0,1},{1,0},{2,3},{3,2},{4,5},{5,4},{6,7},{7,6},{8,9},{9,8},{10,11... | collective-permute-start | bytes 1572872 | tf_op jit(solution)/shard_map/ppermute | solution.py:30
  136.2 28.0 %collective-permute-start.19 = (bf16[512,1024]{1,0:T(8,128)(2,1)S(1)}, bf16[512,1024]{1,0:T(8,128)(2,1)S(1)}, u32[]{:S(2)}, u32[]{:S(2)}) collective-permute-start(bf16[512,1024]{1,0:T(8,128)(2,1)S(1)} %convolution_convert_fusion.4), channel_id=1, source_target_pairs={{0,1},{1,0},{2,3},{3,2},{4,5},{5,4},{6,7},{7,6},{8,9},{9,8},{10,11... | collective-permute-start | bytes 3145736 | tf_op jit(solution)/shard_map/ppermute | solution.py:30
  138.6 39.9 %copy-start.22 = (f32[256,1024]{1,0:T(8,128)}, f32[256,1024]{1,0:T(8,128)S(1)}, u32[]{:S(2)}) copy-start(f32[256,1024]{1,0:T(8,128)S(1)} %get-tuple-element.370) | copy-start | bytes 3145732
  143.3 35.3 %collective-permute-start.20 = (bf16[256,1024]{1,0:T(8,128)(2,1)S(1)}, bf16[256,1024]{1,0:T(8,128)(2,1)S(1)}, u32[]{:S(2)}, u32[]{:S(2)}) collective-permute-start(bf16[256,1024]{1,0:T(8,128)(2,1)S(1)} %convolution_convert_fusion.7), channel_id=1, source_target_pairs={{0,1},{1,0},{2,3},{3,2},{4,5},{5,4},{6,7},{7,6},{8,9},{9,8},{10,11... | collective-permute-start | bytes 1572872 | tf_op jit(solution)/shard_map/ppermute | solution.py:30
  152.3 77.6 %collective-permute-start.21 = (bf16[256,1024]{1,0:T(8,128)(2,1)}, bf16[256,1024]{1,0:T(8,128)(2,1)}, u32[]{:S(2)}, u32[]{:S(2)}) collective-permute-start(bf16[256,1024]{1,0:T(8,128)(2,1)} %convolution_convert_fusion.6), channel_id=1, source_target_pairs={{0,1},{1,0},{2,3},{3,2},{4,5},{5,4},{6,7},{7,6},{8,9},{9,8},{10,11... | collective-permute-start | bytes 1572872 | tf_op jit(solution)/shard_map/ppermute | solution.py:30
  190.5 36.5 %collective-permute-start.23 = (bf16[512,1024]{1,0:T(8,128)(2,1)}, bf16[512,1024]{1,0:T(8,128)(2,1)}, u32[]{:S(2)}, u32[]{:S(2)}) collective-permute-start(bf16[512,1024]{1,0:T(8,128)(2,1)} %convolution_convert_fusion.3), channel_id=1, source_target_pairs={{0,1},{1,0},{2,3},{3,2},{4,5},{5,4},{6,7},{7,6},{8,9},{9,8},{10,11... | collective-permute-start | bytes 3145736 | tf_op jit(solution)/shard_map/ppermute | solution.py:30
  190.6 36.5 %collective-permute-start.24 = (bf16[256,1024]{1,0:T(8,128)(2,1)}, bf16[256,1024]{1,0:T(8,128)(2,1)}, u32[]{:S(2)}, u32[]{:S(2)}) collective-permute-start(bf16[256,1024]{1,0:T(8,128)(2,1)} %convolution_convert_fusion.5), channel_id=1, source_target_pairs={{0,1},{1,0},{2,3},{3,2},{4,5},{5,4},{6,7},{7,6},{8,9},{9,8},{10,11... | collective-permute-start | bytes 1572872 | tf_op jit(solution)/shard_map/ppermute | solution.py:30
  202.4 19.3 %collective-permute-start.22 = (bf16[512,2048]{1,0:T(8,128)(2,1)}, bf16[512,2048]{1,0:T(8,128)(2,1)}, u32[]{:S(2)}, u32[]{:S(2)}) collective-permute-start(bf16[512,2048]{1,0:T(8,128)(2,1)} %bitcast.9), channel_id=1, source_target_pairs={{0,2},{2,0},{4,6},{6,4},{8,10},{10,8},{12,14},{14,12},{16,18},{18,... | collective-permute-start | bytes 6291464 | tf_op jit(solution)/shard_map/ppermute | solution.py:30
  219.6 28.7 %collective-permute-start.25 = (bf16[512,2048]{1,0:T(8,128)(2,1)}, bf16[512,2048]{1,0:T(8,128)(2,1)}, u32[]{:S(2)}, u32[]{:S(2)}) collective-permute-start(bf16[512,2048]{1,0:T(8,128)(2,1)} %bitcast.13), channel_id=1, source_target_pairs={{0,2},{2,0},{4,6},{6,4},{8,10},{10,8},{12,14},{14,12},{16,18},{18,... | collective-permute-start | bytes 6291464 | tf_op jit(solution)/shard_map/ppermute | solution.py:30
  323.8 40.3 %copy-start.97 = (f32[2,1,1,512]{3,2,1,0:T(1,128)}, f32[2,1,1,512]{3,2,1,0:T(1,128)S(1)}, u32[]{:S(2)}) copy-start(f32[2,1,1,512]{3,2,1,0:T(1,128)S(1)} %get-tuple-element.343) | copy-start | bytes 12292
  (108 other events, 879.9 us)
